TPU v7x, 32 devices: a whole 2x2x4 slice. The times are simulated.
32 devices in a mesh: branch: 8 (over z, x), group: 4 (over y, core).
Axes of the slice: x: 2, y: 2, z: 4, core: 2. Of those that a mesh axis runs over, the one named last changes fastest.
Arguments:
- basis: float32 [2, 32768, 256], P(None, ('branch', 'group')), may hold values from -8 to 8
- spread_owner: int32 [32768, 2], P(('branch', 'group')), may hold values from 0 to 31, all different within a row; in each aligned block of 1024 rows (0 to 1023, 1024 to 2047, ...) at most 128 rows name the same one
- spread_row: int32 [32768, 2], P(('branch', 'group')), may hold values from 0 to 1023
- spread_weight: float32 [32768, 2], P(('branch', 'group')), may hold values from 0.2 to 1
- gram_term: bfloat16 [64, 512, 512], P(('branch', 'group')), may hold values from -0.25 to 0.25
- near_block: bfloat16 [64, 8, 512, 512], P(('branch', 'group')), may hold values from -0.09375 to 0.09375
- near_list: int32 [64, 8], P(('branch', 'group')), may hold values from 0 to 1
- leaf_basis: bfloat16 [64, 64, 512], P(('branch', 'group')), may hold values from -0.25 to 0.25
- far_block: bfloat16 [64, 16, 64, 64], P(('branch', 'group')), may hold values from -0.1875 to 0.1875
- far_list: int32 [64, 16], P(('branch', 'group')), may hold values from 0 to 15
- ascend: bfloat16 [64, 64, 64], P(('branch', 'group')), may hold values from -0.1875 to 0.1875
- descend: bfloat16 [64, 64, 64], P(('branch', 'group')), may hold values from -0.75 to 0.75
- top_block: bfloat16 [256, 256], P('group'), may hold values from -0.375 to 0.375
Outputs:
- next_vector: float32 [32768, 256], P(('branch', 'group'))
- hessenberg: float32 [3, 256], replicated
Inputs may be any that keep to these rules, and one draw needn't show every extreme that they name: `spread_owner`: within the rows of one device no owner is named by more than 128 entries, and one row never names an owner twice.
All inputs are finite; a program needn't handle non-finite values.
Results may differ from a plain program's by a relative error of at most 0.0035.
Values may be sent and summed in bfloat16 or wider, within the bound.
No kernel may reach another device: no remote copies, remote signals or barrier semaphores. Data moves between devices by JAX's collectives and lax.ppermute only.
A program may use at most 64 MiB of HBM per device.

v0:
```python
import jax
import jax.numpy as jnp
from jax import lax
from jax.sharding import PartitionSpec as P


def rounded(values):
    return values.astype(jnp.bfloat16)


def contract(pattern, first_op, second_op):
    return jnp.einsum(pattern, first_op, second_op, preferred_element_type=jnp.float32)


def body(
    basis,
    spread_owner,
    spread_row,
    spread_weight,
    gram_term,
    near_block,
    near_list,
    leaf_basis,
    far_block,
    far_list,
    ascend,
    descend,
    top_block,
):
    branches = lax.axis_size("branch")
    groups = lax.axis_size("group")
    devices = branches * groups
    leaves = gram_term.shape[0]
    leaf_size = gram_term.shape[1]
    rows_dev = basis.shape[1]
    columns = basis.shape[2]
    spread = spread_owner.shape[1]
    slot_count = 2 * spread * rows_dev // devices
    vector = basis[basis.shape[0] - 1]
    owners = spread_owner.reshape(-1)
    weights = spread_weight.reshape(-1)
    onehot = (owners[:, None] == jnp.arange(devices, dtype=jnp.int32)[None, :]).astype(jnp.int32)
    slot_index = jnp.sum(jnp.cumsum(onehot, axis=0) * onehot, axis=1) - 1
    position = owners * slot_count + slot_index
    entries = jnp.repeat(vector, spread, axis=0) * weights[:, None]
    send_values = jnp.zeros((devices * slot_count, columns), jnp.float32).at[position].set(entries)
    send_rows = (
        jnp.zeros((devices * slot_count,), jnp.float32)
        .at[position]
        .set(spread_row.reshape(-1).astype(jnp.float32))
    )
    got_values, got_rows = (
        lax.all_to_all(
            send_values.reshape(devices, slot_count, columns),
            ("branch", "group"),
            split_axis=0,
            concat_axis=0,
            tiled=True,
        ),
        lax.all_to_all(
            send_rows.reshape(devices, slot_count),
            ("branch", "group"),
            split_axis=0,
            concat_axis=0,
            tiled=True,
        ),
    )
    got_rows = got_rows.reshape(-1).astype(jnp.int32)
    dual_in = (
        jnp.zeros((rows_dev, columns), jnp.float32)
        .at[got_rows]
        .add(got_values.reshape(-1, columns))
    )
    dual_split = dual_in.reshape(leaves, leaf_size, columns)
    first_pass = dual_split + contract("lji,ljc->lic", gram_term, rounded(dual_split))
    first_low = rounded(first_pass)
    near_sum = contract("lkij,lkjc->lic", near_block, first_low[near_list])
    leaf_coeff = contract("lri,lic->lrc", leaf_basis, first_low)
    coeff_low = rounded(leaf_coeff)
    partial_value = contract("lrs,lsc->rc", ascend, coeff_low)
    gathered_low = lax.all_gather(coeff_low, "branch", axis=0, tiled=True)
    parent = lax.psum(partial_value, "branch")
    parent_low = rounded(parent)
    top_field = jnp.dot(
        top_block,
        lax.all_gather(parent_low, "group", axis=0, tiled=True),
        preferred_element_type=jnp.float32,
    )
    far_sum = contract("lkrs,lksc->lrc", far_block, gathered_low[far_list])
    descent = far_sum + contract("lrs,sc->lrc", descend, rounded(top_field))
    dual_image = first_pass + near_sum + contract("lri,lrc->lic", leaf_basis, rounded(descent))
    dual_out = (dual_image + contract("lij,ljc->lic", gram_term, rounded(dual_image))).reshape(
        rows_dev, columns
    )
    replies = dual_out[got_rows]
    returned = lax.all_to_all(
        replies.reshape(devices, slot_count, columns),
        ("branch", "group"),
        split_axis=0,
        concat_axis=0,
        tiled=True,
    )
    returned = returned.reshape(devices * slot_count, columns)
    image_primal = jnp.sum(
        (returned[position] * weights[:, None]).reshape(rows_dev, spread, columns), axis=1
    )
    total_rows = rows_dev * devices
    cross_sum, self_sum, mutual = lax.psum(
        (
            jnp.sum(basis * image_primal[None], axis=1),
            jnp.sum(image_primal * image_primal, axis=0),
            jnp.sum(basis[:, None] * basis[None], axis=2),
        ),
        ("branch", "group"),
    )
    projection = cross_sum / total_rows
    remainder = image_primal - jnp.sum(projection[:, None, :] * basis, axis=0)
    square = (
        self_sum / total_rows
        - 2.0 * jnp.sum(projection * projection, axis=0)
        + jnp.sum(projection[:, None] * projection[None] * mutual, axis=(0, 1)) / total_rows
    )
    norm_scale = jnp.sqrt(square + 1e-06)
    return (remainder / norm_scale, jnp.concatenate([projection, norm_scale[None]], axis=0))


def solution(mesh):
    return jax.shard_map(
        body,
        mesh=mesh,
        in_specs=(
            P(None, ("branch", "group"), None),
            P(("branch", "group"), None),
            P(("branch", "group"), None),
            P(("branch", "group"), None),
            P(("branch", "group"), None, None),
            P(("branch", "group"), None, None, None),
            P(("branch", "group"), None),
            P(("branch", "group"), None, None),
            P(("branch", "group"), None, None, None),
            P(("branch", "group"), None),
            P(("branch", "group"), None, None),
            P(("branch", "group"), None, None),
            P("group", None),
        ),
        out_specs=(P(("branch", "group"), None), P()),
        check_vma=False,
    )
```

profile of v0, /device:TPU:0, one launch (start us, length us, event | category | flops | bytes accessed | tf_op | source)
XLA Modules:
  0.0 461.7 jit_solution(12164413661836595942)
XLA Ops:
  0.6 0.0 copy-start
  0.7 0.0 copy-start.1
  0.7 0.0 copy-start.11
  0.7 1.9 copy.42
  2.5 1.3 eq.29
  3.9 1.3 eq.25
  5.2 0.7 broadcast_multiply_fusion
  5.9 0.7 fusion.18
  6.6 15.9 %reduce-window.6 = s32[32,16,128]{2,1,0:T(8,128)S(1)} reduce-window(s32[32,16,128]{2,1,0:T(8,128)} %fusion.18, s32[]{:T(128)} %constant.13.clone.1), window={size=1x1x128 pad=0_0x0_0x127_0}, to_apply=%region_0.0 | reduce-window | flops 8323072 | bytes 524292 | tf_op jit(solution)/shard_map/reduce-window
  22.5 0.8 slice.20
  23.3 1.2 copy.57
  24.5 0.2 reduce-window.9
  24.7 0.1 broadcast_add_fusion
  24.8 0.1 fusion.17
  25.0 1.0 copy.41
  26.0 1.4 mul.97
  27.4 1.0 copy.46
  28.4 1.3 reshape.162
  29.7 0.0 copy-start.9
  29.7 8.6 %scatter_custom_fusion = f32[4096]{0:T(1024)} fusion(s32[2048]{0:T(1024)S(1)} %bitcast.100, f32[2048]{0:T(1024)S(1)} %reshape.162, f32[]{:T(128)} %constant.11.clone.1), kind=kCustom, calls=%fused_computation.49 | custom fusion | bytes 16388 | tf_op jit(solution)/shard_map/scatter | solution.py:50
  38.3 7.3 %all-to-all-start = ((f32[32,1,128]{2,1,0:T(1,128)}), f32[32,1,128]{2,1,0:T(1,128)S(1)}, u32[]{:S(2)}, u32[]{:S(2)}) async-start(f32[32,1,128]{2,1,0:T(1,128)} %bitcast.5), calls=%async_computation | async-start | bytes 32768 | tf_op jit(solution)/shard_map/all_to_all | solution.py:60
  45.7 1.0 slice_bitcast_fusion
  46.7 0.2 copy.47
  47.0 0.3 mul.99
  47.2 0.6 copy-done.4
  47.8 3.3 broadcast_in_dim.17
  51.1 2.7 reshape.119
  53.8 12.2 %scatter_custom_fusion.1 = f32[4096,256]{1,0:T(8,128)} fusion(s32[2048]{0:T(1024)S(1)} %bitcast.101, f32[2048,256]{1,0:T(8,128)S(1)} %reshape.119, f32[]{:T(128)} %constant.11.clone.1, f32[2048]{0:T(1024)S(1)} %mul.99), kind=kCustom, calls=%fused_computation.11 | custom fusion | flops 524288 | bytes 6299652 | tf_op jit(solution)/shard_map/scatter | solution.py:46
  66.0 0.0 all-to-all-done
  66.0 6.0 %all-to-all-start.1 = ((f32[32,128,256]{2,1,0:T(8,128)}), f32[32,128,256]{2,1,0:T(8,128)}, u32[]{:S(2)}, u32[]{:S(2)}) async-start(f32[32,128,256]{2,1,0:T(8,128)} %bitcast.90), calls=%async_computation.1 | async-start | bytes 8388608 | tf_op jit(solution)/shard_map/all_to_all | solution.py:53
  72.0 0.1 reshape.128
  72.1 0.1 reshape.136
  72.2 94.0 %all-to-all-done.1 = f32[32,128,256]{2,1,0:T(8,128)} async-done(((f32[32,128,256]{2,1,0:T(8,128)}), f32[32,128,256]{2,1,0:T(8,128)}, u32[]{:S(2)}, u32[]{:S(2)}) %all-to-all-start.1) | async-done | bytes 4194336 | tf_op jit(solution)/shard_map/all_to_all | solution.py:53
  166.2 23.3 %scatter_custom_fusion.2 = f32[1024,256]{1,0:T(8,128)S(1)} fusion(s32[4096]{0:T(1024)S(1)} %bitcast.99, f32[4096,256]{1,0:T(8,128)} %bitcast.10, f32[]{:T(128)} %constant.11.clone.1), kind=kCustom, calls=%fused_computation.37 | custom fusion | flops 1048576 | bytes 1049088 | tf_op jit(solution)/shard_map/scatter-add | solution.py:72
  189.6 1.3 copy.49
  190.9 2.7 fusion.21
  193.6 2.7 gather_fusion
  196.3 0.3 fusion.9
  196.6 32.9 %all_gather.6 = bf16[16,64,256]{2,1,0:T(8,128)(2,1)S(1)} all-gather(bf16[2,64,256]{2,1,0:T(8,128)(2,1)S(1)} %fusion.9), channel_id=1, replica_groups=mesh['branch'=8,'group'=4] {'branch'}, dimensions={0}, use_global_device_ids=true | all-gather | bytes 589824 | tf_op jit(solution)/shard_map/all_gather | solution.py:81
  229.5 0.2 convolution_bitcast_fusion.6
  229.7 37.5 %psum.28 = bf16[64,256]{1,0:T(8,128)(2,1)S(1)} all-reduce(f32[64,256]{1,0:T(8,128)S(1)} %convolution_bitcast_fusion.6), channel_id=1, replica_groups=mesh['branch'=8,'group'=4] {'branch'}, use_global_device_ids=true, to_apply=%region_6.7 | all-reduce | flops 16384 | bytes 98304 | tf_op jit(solution)/shard_map/psum | solution.py:82
  267.2 5.4 %all_gather.7 = bf16[256,256]{1,0:T(8,128)(2,1)S(1)} all-gather(bf16[64,256]{1,0:T(8,128)(2,1)S(1)} %psum.28), channel_id=1, replica_groups=mesh['branch'=8,'group'=4] {'group'}, dimensions={0}, use_global_device_ids=true | all-gather | bytes 163840 | tf_op jit(solution)/shard_map/all_gather | solution.py:86
  272.6 0.6 gather_fusion.1
  273.2 0.3 convolution_bitcast_fusion.4
  273.5 0.9 fusion.10
  274.4 7.2 %fusion.6 = f32[2,512,256]{1,2,0:T(8,128)S(1)} fusion(f32[2,512,256]{1,2,0:T(8,128)} %get-tuple-element.8, bf16[2,8,512,256]{2,3,1,0:T(8,128)(2,1)} %bitcast.93, bf16[2,8,512,512]{3,2,1,0:T(8,128)(2,1)} %param.18), kind=kOutput, calls=%fused_computation.21 | convolution fusion | flops 2147745792 | bytes 14680064 | tf_op jit(solution)/shard_map/lkij,lkjc->lic/dot_general | solution.py:12
  281.6 0.5 fusion.3
  282.1 0.5 fusion.4
  282.6 0.3 copy.51
  282.9 16.1 %gather_fusion.2 = f32[4096,256]{1,0:T(8,128)} fusion(f32[1024,256]{1,0:T(8,128)S(1)} %bitcast.88, s32[4096]{0:T(1024)S(1)} %broadcast_clamp_fusion), kind=kCustom, calls=%fused_computation.2 | custom fusion | bytes 8404992 | tf_op jit(solution)/shard_map/gather | solution.py:95
  299.0 3.7 all-to-all-start.2
  302.8 0.2 multiply_reduce_fusion
  303.0 94.1 %all-to-all-done.2 = f32[32,128,256]{2,1,0:T(8,128)} async-done(((f32[32,128,256]{2,1,0:T(8,128)}), f32[32,128,256]{2,1,0:T(8,128)}, u32[]{:S(2)}, u32[]{:S(2)}) %all-to-all-start.2) | async-done | bytes 4194336 | tf_op jit(solution)/shard_map/all_to_all | solution.py:96
  397.1 10.8 %gather_fusion.3 = f32[2048,256]{1,0:T(8,128)} fusion(f32[4096,256]{1,0:T(8,128)} %bitcast.30, s32[2048]{0:T(1024)S(1)} %broadcast_clamp_fusion.1), kind=kCustom, calls=%fused_computation.3 | custom fusion | bytes 4202496 | tf_op jit(solution)/shard_map/gather | solution.py:105
  407.9 3.5 gather.18
  411.4 6.9 %multiply_reduce_fusion.3 = f32[1024,256]{1,0:T(8,128)S(1)} fusion(f32[1024,2,256]{2,1,0:T(2,128)} %gather.18, f32[1024,2]{1,0:T(8,128)} %copy-done.4), kind=kLoop, calls=%fused_computation.10 | loop fusion | flops 786432 | bytes 3153920 | tf_op jit(solution)/shard_map/reduce_sum | solution.py:104
  418.3 0.0 copy-start.3
  418.3 0.4 multiply_reduce_fusion.2
  418.6 0.6 copy-done.3
  419.2 0.2 multiply_reduce_fusion.4
  419.4 39.1 %all-reduce = (f32[2,256]{1,0:T(2,128)S(1)}, f32[2,2,256]{2,1,0:T(2,128)S(1)}, f32[256]{0:T(256)S(1)}) all-reduce(f32[2,256]{1,0:T(2,128)S(1)} %multiply_reduce_fusion.2, f32[2,2,256]{2,1,0:T(2,128)S(1)} %multiply_reduce_fusion, f32[256]{0:T(256)S(1)} %multiply_reduce_fusion.4), channel_id=1, replica_groups=mesh['branch'=8,'group'=4] {'branch','group'}, use_global_device_ids=true, to_apply=%region_9.10 | all-reduce | flops 1792 | bytes 14336 | tf_op jit(solution)/shard_map/psum | solution.py:108
  458.5 0.2 multiply_reduce_fusion.1
  458.7 0.6 pad_maximum_fusion
  459.4 2.3 subtract_divide_fusion
  (36 shorter events, 0.2 us)
Async XLA Ops:
  0.6 190.2 %copy-start = (bf16[2,512,512]{2,1,0:T(8,128)(2,1)S(1)}, bf16[2,512,512]{2,1,0:T(8,128)(2,1)}, u32[]{:S(2)}) copy-start(bf16[2,512,512]{2,1,0:T(8,128)(2,1)} %param.17) | copy-start | bytes 3145732
  0.6 26.7 %copy-start.12 = (s32[1024,2]{0,1:T(2,128)S(1)}, s32[1024,2]{0,1:T(2,128)}, u32[]{:S(2)}) copy-start(s32[1024,2]{0,1:T(2,128)} %param.15) | copy-start | bytes 24580
  0.7 45.0 %copy-start.1 = (f32[2,1024,256]{2,1,0:T(8,128)S(1)}, f32[2,1024,256]{2,1,0:T(8,128)}, u32[]{:S(2)}) copy-start(f32[2,1024,256]{2,1,0:T(8,128)} %param.13) | copy-start | bytes 6291460
  0.7 46.1 %copy-start.11 = (f32[1024,2]{0,1:T(2,128)S(1)}, f32[1024,2]{0,1:T(2,128)}, u32[]{:S(2)}) copy-start(f32[1024,2]{0,1:T(2,128)} %param.16) | copy-start | bytes 24580
  29.7 24.1 %copy-start.9 = (s32[2048,1]{0,1:T(1,128)}, s32[2048,1]{0,1:T(1,128)S(1)}, u32[]{:S(2)}) copy-start(s32[2048,1]{0,1:T(1,128)S(1)} %compare_select_fusion.1) | copy-start | bytes 24580
  38.3 27.7 %all-to-all-start = ((f32[32,1,128]{2,1,0:T(1,128)}), f32[32,1,128]{2,1,0:T(1,128)S(1)}, u32[]{:S(2)}, u32[]{:S(2)}) async-start(f32[32,1,128]{2,1,0:T(1,128)} %bitcast.5), calls=%async_computation | async-start | bytes 32768 | tf_op jit(solution)/shard_map/all_to_all | solution.py:60
  47.0 0.9 copy-start.4
  66.0 6.0 %copy-start.13 = (s32[2,8]{1,0:T(2,128)S(1)}, s32[2,8]{1,0:T(2,128)}, u32[]{:S(2)}) copy-start(s32[2,8]{1,0:T(2,128)} %param.19) | copy-start | bytes 196
  66.0 6.1 %copy-start.14 = (s32[2,16]{1,0:T(2,128)S(1)}, s32[2,16]{1,0:T(2,128)}, u32[]{:S(2)}) copy-start(s32[2,16]{1,0:T(2,128)} %param.22) | copy-start | bytes 388
  66.0 100.2 %all-to-all-start.1 = ((f32[32,128,256]{2,1,0:T(8,128)}), f32[32,128,256]{2,1,0:T(8,128)}, u32[]{:S(2)}, u32[]{:S(2)}) async-start(f32[32,128,256]{2,1,0:T(8,128)} %bitcast.90), calls=%async_computation.1 | async-start | bytes 8388608 | tf_op jit(solution)/shard_map/all_to_all | solution.py:53
  193.5 2.7 copy-start.6
  193.5 36.0 %copy-start.8 = (bf16[2,64,64]{2,1,0:T(8,128)(2,1)S(1)}, bf16[2,64,64]{2,1,0:T(8,128)(2,1)}, u32[]{:S(2)}) copy-start(bf16[2,64,64]{2,1,0:T(8,128)(2,1)} %param.23) | copy-start | bytes 49156
  193.6 79.7 %copy-start.5 = (bf16[2,16,64,64]{3,2,1,0:T(8,128)(2,1)S(1)}, bf16[2,16,64,64]{3,2,1,0:T(8,128)(2,1)}, u32[]{:S(2)}) copy-start(bf16[2,16,64,64]{3,2,1,0:T(8,128)(2,1)} %param.21) | copy-start | bytes 786436
  274.4 7.2 %copy-start.7 = (bf16[2,64,64]{2,1,0:T(8,128)(2,1)S(1)}, bf16[2,64,64]{2,1,0:T(8,128)(2,1)}, u32[]{:S(2)}) copy-start(bf16[2,64,64]{2,1,0:T(8,128)(2,1)} %param.24) | copy-start | bytes 49156
  299.0 3.7 copy-start.10
  299.0 3.7 copy-start.2
  299.0 98.1 %all-to-all-start.2 = ((f32[32,128,256]{2,1,0:T(8,128)}), f32[32,128,256]{2,1,0:T(8,128)}, u32[]{:S(2)}, u32[]{:S(2)}) async-start(f32[32,128,256]{2,1,0:T(8,128)} %bitcast.89), calls=%async_computation.2 | async-start | bytes 8388608 | tf_op jit(solution)/shard_map/all_to_all | solution.py:96
  418.3 1.0 copy-start.3
where the time goes:
time: 464 us; the launch traced here: 462 us
  waiting for transfers between devices  188 us (41%)
  blocking collectives  115 us (25%)
  local copies, waits for them, and re-layouts  64.1 us (14%)
  other arithmetic  64.1 us (14%)
  starting transfers between devices  17 us (4%)
  matrix products  12.5 us (3%)
    all_to_all x1, waiting for transfers between devices, body(): lax.all_to_all(replies.reshape(devices, slot_count, columns), ('branch',...  94.1 us
    all_to_all x1, waiting for transfers between devices, body(): lax.all_to_all(send_values.reshape(devices, slot_count, columns), ('branc...  94 us
    psum x1, blocking collectives, body(): lax.psum((jnp.sum(basis * image_primal[None], axis=1), jnp.sum(image_prim...  39.1 us
    psum x1, blocking collectives, body(): parent = lax.psum(partial_value, 'branch')  37.5 us
    all_gather x1, blocking collectives, body(): gathered_low = lax.all_gather(coeff_low, 'branch', axis=0, tiled=True)  32.9 us
    scatter-add x1, other arithmetic, body(): dual_in = jnp.zeros((rows_dev, columns), jnp.float32).at[got_rows].add(go...  23.3 us
    another operation x3, other arithmetic  16.2 us
    gather x1, local copies, waits for them, and re-layouts, body(): replies = dual_out[got_rows]  16.1 us
  transfers between devices with their start and end apart: 3, of which 2 were waited for; matrix products, arithmetic and copies ran while one was open for 4% of the time, Pallas kernels for 0%

commit v1 on v0

v1 whole, which is shorter than its diff:
```python
import functools

import jax
import jax.numpy as jnp
from jax import lax
from jax.experimental import pallas as pl
from jax.experimental.pallas import tpu as pltpu
from jax.sharding import PartitionSpec as P

F32 = jnp.float32
LOW = jnp.bfloat16
CODE = jnp.int16
TOP = 32767.0
REST = 65534.0
LOG2 = 0.6931471805599453
BLOCK = 512
VMEM_LIMIT = 24 << 20


def rounded(values):
    return values.astype(LOW)


def contract(pattern, first_op, second_op):
    return jnp.einsum(pattern, first_op, second_op, preferred_element_type=F32)


def dot(lhs, rhs, lhs_dim=1, rhs_dim=0):
    return lax.dot_general(
        lhs, rhs, (((lhs_dim,), (rhs_dim,)), ((), ())), preferred_element_type=F32
    )


def params(semantics=None):
    return pltpu.CompilerParams(dimension_semantics=semantics, vmem_limit_bytes=VMEM_LIMIT)


def whole(shape):
    zeros = (0,) * len(shape)
    return pl.BlockSpec(shape, lambda *_: zeros)


def cost(flops, nbytes):
    return pl.CostEstimate(flops=int(flops), bytes_accessed=int(nbytes), transcendentals=0)


def column(row):
    size = row.shape[1]
    same = lax.broadcasted_iota(jnp.int32, (size, size), 0) == lax.broadcasted_iota(
        jnp.int32, (size, size), 1
    )
    return jnp.sum(jnp.where(same, row, 0.0), axis=1, keepdims=True)


def split(code):
    high = jnp.round(code * (1.0 / 256.0))
    return high, code - 256.0 * high


def route_kernel(slots, owner_ref, row_ref, weight_ref, rank_ref, side_ref, place_ref):
    devices, rows_dev = rank_ref.shape
    spread = owner_ref.shape[0]
    width = side_ref.shape[2]
    ids = lax.broadcasted_iota(jnp.int32, (devices, rows_dev), 0)
    named = [owner_ref[s : s + 1, :] == ids for s in range(spread)]
    chosen = functools.reduce(jnp.logical_or, named)
    flag = jnp.where(chosen, 1.0, 0.0)
    lane = 128
    upper = jnp.where(
        lax.broadcasted_iota(jnp.int32, (lane, lane), 0)
        <= lax.broadcasted_iota(jnp.int32, (lane, lane), 1),
        1.0,
        0.0,
    ).astype(LOW)
    before = jnp.zeros((devices, 1), F32)
    pieces = []
    for start in range(0, rows_dev, lane):
        part = flag[:, start : start + lane]
        upto = dot(part.astype(LOW), upper)
        pieces.append(upto - part + before)
        before = before + upto[:, lane - 1 : lane]
    rank = jnp.concatenate(pieces, axis=1)
    rank_ref[...] = jnp.where(chosen, rank, -1.0)
    slot_ids = lax.broadcasted_iota(jnp.int32, (width, rows_dev), 0).astype(F32)
    place_ref[...] = jnp.zeros_like(place_ref)
    total = jnp.zeros((6 * devices, width), F32)
    for s in range(spread):
        slot = jnp.sum(jnp.where(named[s], rank, 0.0), axis=0, keepdims=True)
        place_ref[s : s + 1, :] = owner_ref[s : s + 1, :].astype(F32) * slots + slot
        weight = weight_ref[s : s + 1, :]
        place_ref[spread + s : spread + s + 1, :] = weight
        code = weight * TOP
        whole_code = jnp.round(code)
        rest_code = jnp.round((code - whole_code) * REST)
        fields = split(row_ref[s : s + 1, :].astype(F32)) + split(whole_code) + split(rest_code)
        lhs = jnp.concatenate([jnp.where(named[s], f, 0.0) for f in fields], axis=0).astype(LOW)
        total = total + dot(lhs, jnp.where(slot_ids == slot, 1.0, 0.0).astype(LOW), 1, 1)
    for i in range(3):
        high = total[2 * i * devices : (2 * i + 1) * devices]
        low = total[(2 * i + 1) * devices : (2 * i + 2) * devices]
        side_ref[i] = 256.0 * high + low


def route(owner_t, row_t, weight_t, devices, slots, width):
    rows_dev = owner_t.shape[1]
    return pl.pallas_call(
        functools.partial(route_kernel, slots),
        out_shape=(
            jax.ShapeDtypeStruct((devices, rows_dev), F32),
            jax.ShapeDtypeStruct((3, devices, width), F32),
            jax.ShapeDtypeStruct((8, rows_dev), F32),
        ),
        compiler_params=params(),
        cost_estimate=cost(1e8, 1 << 19),
        name="route",
    )(owner_t, row_t, weight_t)


def spread_kernel(slots, vector_ref, rank_ref, side_ref, *refs):
    outs, (code_ref, level_ref, pick_ref) = refs[:-3], refs[-3:]
    step = pl.program_id(0)
    columns = vector_ref.shape[2]

    @pl.when(step == 0)
    def _():
        vector = vector_ref[0]
        peak = jnp.maximum(jnp.max(jnp.abs(vector), axis=0, keepdims=True), 1e-30)
        level = jnp.floor(jnp.log(peak) * (1.0 / LOG2)) + 1.0
        level_ref[...] = level
        code = jnp.clip(jnp.round(vector * (TOP / jnp.exp(level * LOG2))), -TOP, TOP)
        high, low = split(code)
        code_ref[:, :columns] = high.astype(LOW)
        code_ref[:, columns:] = low.astype(LOW)

    rows_dev = rank_ref.shape[1]
    owners = BLOCK // slots
    slot_ids = lax.broadcasted_iota(jnp.int32, (slots, rows_dev), 0).astype(F32)
    for j in range(owners):
        rank = rank_ref[pl.ds(step * owners + j, 1), :]
        pick_ref[j * slots : (j + 1) * slots, :] = jnp.where(slot_ids == rank, 1.0, 0.0).astype(LOW)
    picked = dot(pick_ref[...], code_ref[...])
    codes = (256.0 * picked[:, :columns] + picked[:, columns:]).astype(jnp.int32).astype(CODE)
    for i, out_ref in enumerate(outs):
        width = out_ref.shape[2]
        at = slice(i * width, (i + 1) * width)
        line = lax.broadcasted_iota(jnp.int32, (8, width), 0)
        for j in range(owners):
            extra = jnp.where(line == 3, level_ref[:, at], 0.0)
            for k in range(3):
                extra = jnp.where(line == k, side_ref[k, pl.ds(step * owners + j, 1), :], extra)
            out_ref[j, :slots, :] = codes[j * slots : (j + 1) * slots, at]
            out_ref[j, slots:, :] = extra.astype(jnp.int32).astype(CODE)


def spread_out(basis, rank, side, slots, chunks):
    devices, rows_dev = rank.shape
    last, columns = basis.shape[0] - 1, basis.shape[2]
    owners = BLOCK // slots
    width = columns // chunks
    shape = (devices, slots + 8, width)
    return pl.pallas_call(
        functools.partial(spread_kernel, slots),
        grid=(devices // owners,),
        in_specs=[
            pl.BlockSpec((1, rows_dev, columns), lambda i: (last, 0, 0)),
            whole(rank.shape),
            whole(side.shape),
        ],
        out_specs=[pl.BlockSpec((owners,) + shape[1:], lambda i: (i, 0, 0))] * chunks,
        out_shape=[jax.ShapeDtypeStruct(shape, CODE)] * chunks,
        scratch_shapes=[
            pltpu.VMEM((rows_dev, 2 * columns), LOW),
            pltpu.VMEM((1, columns), F32),
            pltpu.VMEM((BLOCK, rows_dev), LOW),
        ],
        compiler_params=params(("arbitrary",)),
        cost_estimate=cost(4 * devices * slots * rows_dev * columns, 4 << 20),
        name="spread_out",
    )(basis, rank, side)


def collect_kernel(
    slots, got_ref, gram_ref, base_ref, first_ref, low_ref, coeff_ref, rows_ref, sum_ref, pick_ref, term_ref
):
    step = pl.program_id(0)
    rows_dev, width = first_ref.shape
    owners = got_ref.shape[0]
    ids = lax.broadcasted_iota(jnp.int32, (rows_dev, slots), 0).astype(F32)
    for j in range(owners):
        at = slice(j * slots, (j + 1) * slots)
        extra = got_ref[j, slots:, :].astype(jnp.int32).astype(F32)
        row = extra[0:1, :slots]
        weight = (extra[1:2, :slots] + extra[2:3, :slots] * (1.0 / REST)) * (1.0 / TOP)
        scale = jnp.exp(extra[3:4, :] * LOG2) * (1.0 / TOP)
        rows_ref[pl.ds(step * owners + j, 1), :] = extra[0:1, :]
        values = got_ref[j, :slots, :].astype(jnp.int32).astype(F32) * column(weight) * scale
        high = values.astype(LOW)
        term_ref[at, :width] = high
        term_ref[at, width:] = (values - high.astype(F32)).astype(LOW)
        pick_ref[:, at] = jnp.where(ids == row, 1.0, 0.0).astype(LOW)
    added = dot(pick_ref[...], term_ref[...])

    @pl.when(step == 0)
    def _():
        sum_ref[...] = added

    @pl.when(step > 0)
    def _():
        sum_ref[...] += added

    @pl.when(step == pl.num_programs(0) - 1)
    def _():
        leaves, leaf = gram_ref.shape[:2]
        rank = base_ref.shape[1]
        for l in range(leaves):
            at = slice(l * leaf, (l + 1) * leaf)
            dual = sum_ref[at, :width] + sum_ref[at, width:]
            first = dual + dot(gram_ref[l], dual.astype(LOW), 0, 0)
            low = first.astype(LOW)
            first_ref[at, :] = first
            low_ref[l] = low
            coeff_ref[l * rank : (l + 1) * rank, :] = dot(base_ref[l], low).astype(LOW)


def collect(got, gram, base):
    devices, slots, width = got.shape[0], got.shape[1] - 8, got.shape[2]
    leaves, leaf = gram.shape[:2]
    rank = base.shape[1]
    rows_dev = leaves * leaf
    owners = BLOCK // slots
    return pl.pallas_call(
        functools.partial(collect_kernel, slots),
        grid=(devices // owners,),
        in_specs=[
            pl.BlockSpec((owners,) + got.shape[1:], lambda i: (i, 0, 0)),
            whole(gram.shape),
            whole(base.shape),
        ],
        out_specs=(
            whole((rows_dev, width)),
            whole((leaves, leaf, width)),
            whole((leaves * rank, width)),
            whole((devices, width)),
        ),
        out_shape=(
            jax.ShapeDtypeStruct((rows_dev, width), F32),
            jax.ShapeDtypeStruct((leaves, leaf, width), LOW),
            jax.ShapeDtypeStruct((leaves * rank, width), LOW),
            jax.ShapeDtypeStruct((devices, width), F32),
        ),
        scratch_shapes=[
            pltpu.VMEM((rows_dev, 2 * width), F32),
            pltpu.VMEM((rows_dev, BLOCK), LOW),
            pltpu.VMEM((BLOCK, 2 * width), LOW),
        ],
        compiler_params=params(("arbitrary",)),
        cost_estimate=cost(4 * devices * slots * rows_dev * width, 4 << 20),
        name="collect",
    )(got, gram, base)


def near_kernel(list_ref, block_ref, low_ref, first_ref, out_ref):
    leaf, item = pl.program_id(0), pl.program_id(1)
    count = block_ref.shape[1]
    term = dot(block_ref[0, 0], low_ref[list_ref[leaf, item * count]])
    for k in range(1, count):
        term = term + dot(block_ref[0, k], low_ref[list_ref[leaf, item * count + k]])

    @pl.when(item == 0)
    def _():
        out_ref[...] = first_ref[...] + term

    @pl.when(item > 0)
    def _():
        out_ref[...] += term


def near_field(near_list, near_block, low, first):
    leaves, items, leaf = near_block.shape[:3]
    width = low.shape[2]
    count = 4 if items % 4 == 0 else 1
    return pl.pallas_call(
        near_kernel,
        grid_spec=pltpu.PrefetchScalarGridSpec(
            num_scalar_prefetch=1,
            grid=(leaves, items // count),
            in_specs=[
                pl.BlockSpec((1, count, leaf, leaf), lambda l, k, _: (l, k, 0, 0)),
                whole(low.shape),
                pl.BlockSpec((leaf, width), lambda l, k, _: (l, 0)),
            ],
            out_specs=pl.BlockSpec((leaf, width), lambda l, k, _: (l, 0)),
        ),
        out_shape=jax.ShapeDtypeStruct(first.shape, F32),
        compiler_params=params(("arbitrary", "arbitrary")),
        cost_estimate=cost(2 * near_block.size * width, 2 * near_block.size),
        name="near_field",
    )(near_list, near_block, low, first)


def reply_kernel(
    slots,
    image_ref,
    far_ref,
    top_ref,
    parents_ref,
    descend_ref,
    base_ref,
    gram_ref,
    rows_ref,
    out_ref,
    dual_ref,
    pick_ref,
):
    step = pl.program_id(0)

    @pl.when(step == 0)
    def _():
        leaves, leaf = gram_ref.shape[:2]
        field = dot(top_ref[...], parents_ref[...]).astype(LOW)
        for l in range(leaves):
            at = slice(l * leaf, (l + 1) * leaf)
            descent = far_ref[l] + dot(descend_ref[l], field)
            image = image_ref[at, :] + dot(base_ref[l], descent.astype(LOW), 0, 0)
            dual_ref[at, :] = (image + dot(gram_ref[l], image.astype(LOW))).astype(LOW)

    rows_dev = dual_ref.shape[0]
    owners = BLOCK // slots
    ids = lax.broadcasted_iota(jnp.int32, (slots, rows_dev), 1).astype(F32)
    for j in range(owners):
        row = column(rows_ref[pl.ds(step * owners + j, 1), :][:, :slots])
        pick_ref[j * slots : (j + 1) * slots, :] = jnp.where(ids == row, 1.0, 0.0).astype(LOW)
    out_ref[...] = dot(pick_ref[...], dual_ref[...]).astype(LOW)


def reply(image, far, top, parents, descend, base, gram, rows, slots):
    rows_dev, width = image.shape
    steps = rows.shape[0] * slots // BLOCK
    args = (image, far, top, parents, descend, base, gram, rows)
    return pl.pallas_call(
        functools.partial(reply_kernel, slots),
        grid=(steps,),
        in_specs=[whole(a.shape) for a in args],
        out_specs=pl.BlockSpec((BLOCK, width), lambda i: (i, 0)),
        out_shape=jax.ShapeDtypeStruct((steps * BLOCK, width), LOW),
        scratch_shapes=[pltpu.VMEM((rows_dev, width), LOW), pltpu.VMEM((BLOCK, rows_dev), LOW)],
        compiler_params=params(("arbitrary",)),
        cost_estimate=cost(2 * steps * BLOCK * rows_dev * width, 4 << 20),
        name="reply",
    )(*args)


def gather_kernel(spread, ret_ref, place_ref, basis_ref, image_ref, sums_ref):
    step = pl.program_id(0)
    rows = place_ref.shape[0]
    total = ret_ref.shape[0]
    ids = lax.broadcasted_iota(jnp.int32, (rows, total), 1).astype(F32)
    image = jnp.zeros(image_ref.shape, F32)
    for s in range(spread):
        pick = jnp.where(ids == place_ref[:, s : s + 1], 1.0, 0.0).astype(LOW)
        image = image + place_ref[:, spread + s : spread + s + 1] * dot(pick, ret_ref[...])
    image_ref[...] = image
    krylov = basis_ref.shape[0]
    parts = [jnp.sum(basis_ref[k] * image, axis=0, keepdims=True) for k in range(krylov)]
    parts.append(jnp.sum(image * image, axis=0, keepdims=True))
    parts.append(jnp.zeros((sums_ref.shape[0] - krylov - 1, image.shape[1]), F32))
    added = jnp.concatenate(parts, axis=0)

    @pl.when(step == 0)
    def _():
        sums_ref[...] = added

    @pl.when(step > 0)
    def _():
        sums_ref[...] += added


def gather_back(ret, place_col, basis, spread):
    total, width = ret.shape
    krylov, rows_dev = basis.shape[:2]
    rows = 256
    return pl.pallas_call(
        functools.partial(gather_kernel, spread),
        grid=(rows_dev // rows,),
        in_specs=[
            whole(ret.shape),
            pl.BlockSpec((rows, place_col.shape[1]), lambda i: (i, 0)),
            pl.BlockSpec((krylov, rows, width), lambda i: (0, i, 0)),
        ],
        out_specs=(pl.BlockSpec((rows, width), lambda i: (i, 0)), whole((8, width))),
        out_shape=(
            jax.ShapeDtypeStruct((rows_dev, width), F32),
            jax.ShapeDtypeStruct((8, width), F32),
        ),
        compiler_params=params(("arbitrary",)),
        cost_estimate=cost(2 * spread * total * rows_dev * width, 6 << 20),
        name="gather_back",
    )(ret, place_col, basis)


AXES = ("branch", "group")


def exchange(values, axes=AXES):
    return lax.all_to_all(values, axes, split_axis=0, concat_axis=0, tiled=True)


def to_all(values, axes, size):
    return exchange(jnp.broadcast_to(values[None], (size,) + values.shape), axes)


def body(
    basis,
    spread_owner,
    spread_row,
    spread_weight,
    gram_term,
    near_block,
    near_list,
    leaf_basis,
    far_block,
    far_list,
    ascend,
    descend,
    top_block,
):
    branches = lax.axis_size("branch")
    groups = lax.axis_size("group")
    devices = branches * groups
    rows_dev, columns = basis.shape[1:]
    krylov = basis.shape[0]
    spread = spread_owner.shape[1]
    slots = 2 * spread * rows_dev // devices
    total = devices * slots
    leaves, rank = leaf_basis.shape[:2]
    rank_of, side, place = route(
        spread_owner.T, spread_row.T, spread_weight.T, devices, slots, columns
    )
    sent = spread_out(basis, rank_of, side, slots, 1)[0]
    got = exchange(sent)
    ascend_all = to_all(ascend, "branch", branches).reshape((branches * leaves,) + ascend.shape[1:])

    first, low, coeff, rows = collect(got, gram_term, leaf_basis)
    coeff_all = to_all(coeff, "branch", branches).reshape(branches * leaves, rank, columns)
    image = near_field(near_list, near_block, low, first)
    parent = rounded(contract("lrs,lsc->rc", ascend_all, coeff_all))
    parents = lax.all_gather(parent, "group", axis=0, tiled=True)
    far = contract("lkrs,lksc->lrc", far_block, coeff_all[far_list])
    replies = reply(image, far, top_block, parents, descend, leaf_basis, gram_term, rows, slots)
    returned = exchange(replies.reshape(devices, slots, columns)).reshape(total, columns)
    primal, sums = gather_back(returned, place.T, basis, spread)
    pairs = [(i, j) for i in range(krylov) for j in range(i, krylov)]
    mutual = jnp.stack([jnp.sum(basis[i] * basis[j], axis=0) for i, j in pairs])
    sums = jnp.concatenate([sums[: krylov + 1], mutual], axis=0)
    sums = jnp.sum(to_all(sums, AXES, devices), axis=0)
    mutual = sums[krylov + 1 :]

    total_rows = rows_dev * devices
    projection = sums[:krylov] / total_rows
    remainder = primal - jnp.sum(projection[:, None, :] * basis, axis=0)
    square = sums[krylov] / total_rows - 2.0 * jnp.sum(projection * projection, axis=0)
    for at, (i, j) in enumerate(pairs):
        times = 1.0 if i == j else 2.0
        square = square + times * projection[i] * projection[j] * mutual[at] / total_rows
    norm_scale = jnp.sqrt(jnp.maximum(square, 0.0) + 1e-06)
    return (remainder / norm_scale, jnp.concatenate([projection, norm_scale[None]], axis=0))


def solution(mesh):
    both = ("branch", "group")
    return jax.shard_map(
        body,
        mesh=mesh,
        in_specs=(
            P(None, both, None),
            P(both, None),
            P(both, None),
            P(both, None),
            P(both, None, None),
            P(both, None, None, None),
            P(both, None),
            P(both, None, None),
            P(both, None, None, None),
            P(both, None),
            P(both, None, None),
            P(both, None, None),
            P("group", None),
        ),
        out_specs=(P(both, None), P()),
        check_vma=False,
    )
```

time: 464 us -> 204 us (0.44)
  blocking collectives: 115 us -> 19.9 us
  waiting for transfers between devices: 188 us -> 104 us
  other arithmetic: 64.1 us -> 2.24 us
  local copies, waits for them, and re-layouts: 64.1 us -> 20 us
  Pallas kernels: 0 us -> 32.1 us
  matrix products: 12.5 us -> 2.83 us
    all_to_all x3 -> x4, waiting for transfers between devices: 188 us -> 104 us  [exchange(): return lax.all_to_all(values, axes, split_axis=0, concat_axis=0, tiled=True)]
    psum x2 -> x0, blocking collectives: 76.6 us -> none  [the longest x1 39.1 us: body(): lax.psum((jnp.sum(basis * image_primal[None], axis=1), jnp.sum(image_prim...]
    all_gather x2 -> x1, blocking collectives: 38.3 us -> 5.51 us  [body(): parents = lax.all_gather(parent, 'group', axis=0, tiled=True)]
    pallas_call x0 -> x6, Pallas kernels: none -> 32.1 us  [the longest x1 9.13 us: collect(): pl.pallas_call(functools.partial(collect_kernel, slots), grid=(devices //...]
    gather x5 -> x1, local copies, waits for them, and re-layouts: 33.7 us -> 2.71 us  [body(): far = contract('lkrs,lksc->lrc', far_block, coeff_all[far_list])]
    scatter-add x1 -> x0, other arithmetic: 23.3 us -> none  [body(): dual_in = jnp.zeros((rows_dev, columns), jnp.float32).at[got_rows].add(go...]
    another operation x3 -> x0, other arithmetic: 16.2 us -> none
    all_to_all x0 -> x1, blocking collectives: none -> 14.4 us  [exchange(): return lax.all_to_all(values, axes, split_axis=0, concat_axis=0, tiled=True)]
  transfers between devices with their start and end apart: 3 -> 4, of which waited for: 2 -> 3; matrix products, arithmetic and copies ran while one was open for 4% -> 2% of each run, Pallas kernels for 0% -> 6%
where the time goes in v1:
time: 204 us; the launch traced here: 203 us
  waiting for transfers between devices  104 us (51%)
  Pallas kernels  32.1 us (16%)
  starting transfers between devices  21.4 us (10%)
  local copies, waits for them, and re-layouts  20 us (10%)
  blocking collectives  19.9 us (10%)
  matrix products  2.83 us (1%)
  other arithmetic  2.24 us (1%)
    all_to_all x4, waiting for transfers between devices, exchange(): return lax.all_to_all(values, axes, split_axis=0, concat_axis=0, tiled=True)  104 us
    all_to_all x4, starting transfers between devices, exchange(): return lax.all_to_all(values, axes, split_axis=0, concat_axis=0, tiled=True)  21.4 us
    unnamed x46, local copies, waits for them, and re-layouts  16.1 us
    all_to_all x1, blocking collectives, exchange(): return lax.all_to_all(values, axes, split_axis=0, concat_axis=0, tiled=True)  14.4 us
    pallas_call x1, Pallas kernels, collect(): pl.pallas_call(functools.partial(collect_kernel, slots), grid=(devices //...  9.13 us
    pallas_call x1, Pallas kernels, gather_back(): pl.pallas_call(functools.partial(gather_kernel, spread), grid=(rows_dev /...  7.1 us
    pallas_call x1, Pallas kernels, spread_out(): pl.pallas_call(functools.partial(spread_kernel, slots), grid=(devices //...  6.35 us
    all_gather x1, blocking collectives, body(): parents = lax.all_gather(parent, 'group', axis=0, tiled=True)  5.51 us
  transfers between devices with their start and end apart: 4, of which 3 were waited for; matrix products, arithmetic and copies ran while one was open for 2% of the time, Pallas kernels for 6%

profile of v1, /device:TPU:0, one launch (start us, length us, event | category | flops | bytes accessed | tf_op | source)
XLA Modules:
  0.0 203.1 jit_solution(1563160559430301962)
XLA Ops:
  0.6 0.0 copy-start
  0.6 0.0 copy-start.16
  0.7 0.7 copy-done.16
  1.4 0.0 copy-start.17
  1.4 0.7 copy-done.17
  2.1 0.0 copy-start.18
  2.1 0.7 copy-done.18
  2.8 0.7 route.1
  3.5 0.0 copy-start.2
  3.5 1.6 copy-done.2
  5.1 6.3 %spread_out.1 = s16[32,136,256]{2,1,0:T(8,128)(2,1)S(1)} custom-call(f32[2,1024,256]{2,1,0:T(8,128)S(1)} %copy-done.2, f32[32,1024]{1,0:T(8,128)S(1)} %get-tuple-element.11.rank_ref, f32[3,32,256]{2,1,0:T(8,128)S(1)} %get-tuple-element.12.side_ref), custom_call_target="tpu_custom_call" | custom-call | flops 4294967296 | bytes 4194304 | tf_op jit(solution)/shard_map/spread_out/pallas_call | solution.py:161
  11.5 0.0 copy-start.4
  11.5 1.4 copy-done.4
  12.9 0.0 copy-start.20
  12.9 0.0 copy-start.13
  12.9 7.3 %all-to-all-start = ((s16[32,136,256]{2,1,0:T(8,128)(2,1)}), s16[32,136,256]{2,1,0:T(8,128)(2,1)S(1)}, u32[]{:S(2)}, u32[]{:S(2)}) async-start(s16[32,136,256]{2,1,0:T(8,128)(2,1)} %copy-done.4), calls=%async_computation | async-start | bytes 4456448 | tf_op jit(solution)/shard_map/all_to_all | solution.py:405
  20.2 0.0 copy-done.20
  20.3 0.9 reshape.48
  21.2 50.5 %all-to-all-done.got_ref = s16[32,136,256]{2,1,0:T(8,128)(2,1)S(1)} async-done(((s16[32,136,256]{2,1,0:T(8,128)(2,1)}), s16[32,136,256]{2,1,0:T(8,128)(2,1)S(1)}, u32[]{:S(2)}, u32[]{:S(2)}) %all-to-all-start) | async-done | bytes 2228256 | tf_op jit(solution)/shard_map/all_to_all | solution.py:405
  71.7 4.0 %all-to-all-start.2 = ((bf16[8,2,4096]{2,1,0:T(2,128)(2,1)}), bf16[8,2,4096]{2,1,0:T(2,128)(2,1)}, u32[]{:S(2)}, u32[]{:S(2)}) async-start(bf16[8,2,4096]{2,1,0:T(2,128)(2,1)} %reshape.48), calls=%async_computation.2 | async-start | bytes 262144 | tf_op jit(solution)/shard_map/all_to_all | solution.py:405
  75.7 0.0 copy-done.13
  75.7 0.0 copy-start.11
  75.7 1.2 copy-done.11
  76.9 0.0 copy-start.21
  76.9 9.1 %collect.1 = (f32[1024,256]{1,0:T(8,128)S(1)}, bf16[2,512,256]{2,1,0:T(8,128)(2,1)S(1)}, bf16[128,256]{1,0:T(8,128)(2,1)S(1)}, f32[32,256]{1,0:T(8,128)S(1)}) custom-call(s16[32,136,256]{2,1,0:T(8,128)(2,1)S(1)} %all-to-all-done.got_ref, bf16[2,512,512]{2,1,0:T(8,128)(2,1)S(1)} %copy-done.11, bf16[2,64,512]{2,1,0:T(8,128)(2,1)S(1)} %copy-done.13), custom_call_target="tpu_custom_call" | custom-call | flops 4294967296 | bytes 4194304 | tf_op jit(solution)/shard_map/collect/pallas_call | solution.py:231
  86.1 0.0 copy-start.8
  86.1 1.0 copy-done.8
  87.1 0.0 all-to-all-done.2
  87.1 0.8 broadcast_in_dim.8
  87.9 5.9 %all-to-all-start.1 = ((bf16[8,128,256]{2,1,0:T(8,128)(2,1)}), bf16[8,128,256]{2,1,0:T(8,128)(2,1)}, u32[]{:S(2)}, u32[]{:S(2)}) async-start(bf16[8,128,256]{2,1,0:T(8,128)(2,1)} %broadcast_in_dim.8), calls=%async_computation.1 | async-start | bytes 1048576 | tf_op jit(solution)/shard_map/all_to_all | solution.py:405
  93.8 0.0 copy-done.21
  93.8 0.1 reshape.38
  93.9 1.8 reshape.49
  95.7 0.0 copy-done.10
  95.7 0.0 copy-done.9
  95.8 3.4 %copy-done.1 = bf16[2,8,512,512]{3,2,1,0:T(8,128)(2,1)S(1)} copy-done((bf16[2,8,512,512]{3,2,1,0:T(8,128)(2,1)S(1)}, bf16[2,8,512,512]{3,2,1,0:T(8,128)(2,1)}, u32[]{:S(2)}) %copy-start.1) | copy-done | bytes 8388632
  99.1 3.7 %near_field.1.image_ref = f32[1024,256]{1,0:T(8,128)S(1)} custom-call(s32[2,8]{1,0:T(2,128)S(1)} %copy-done.10, bf16[2,8,512,512]{3,2,1,0:T(8,128)(2,1)S(1)} %copy-done.1, bf16[2,512,256]{2,1,0:T(8,128)(2,1)S(1)} %get-tuple-element.13.low_ref, f32[1024,256]{1,0:T(8,128)S(1)} %copy-done.9), custom_call_target="tpu_custom_call" | custom-call | flops 2147483648 | bytes 8388608 | tf_op jit(solution)/shard_map/near_field/pallas_call | solution.py:282
  102.8 0.0 copy-start.19
  102.8 5.0 %all-to-all-done.1 = bf16[8,128,256]{2,1,0:T(8,128)(2,1)} async-done(((bf16[8,128,256]{2,1,0:T(8,128)(2,1)}), bf16[8,128,256]{2,1,0:T(8,128)(2,1)}, u32[]{:S(2)}, u32[]{:S(2)}) %all-to-all-start.1) | async-done | bytes 524320 | tf_op jit(solution)/shard_map/all_to_all | solution.py:405
  107.9 2.7 %gather_fusion = bf16[32,64,256]{2,1,0:T(8,128)(2,1)} fusion(bf16[16,64,256]{2,1,0:T(8,128)(2,1)} %bitcast.3, s32[1024]{0:T(1024)S(1)} %pad_clamp_fusion), kind=kCustom, calls=%fused_computation | custom fusion | bytes 2097280 | tf_op jit(solution)/shard_map/gather | solution.py:448
  110.6 0.0 copy-done.19
  110.6 1.3 fusion.1
  111.9 5.5 %all_gather.3.parents_ref = bf16[256,256]{1,0:T(8,128)(2,1)S(1)} all-gather(bf16[64,256]{1,0:T(8,128)(2,1)S(1)} %fusion.1), channel_id=1, replica_groups=mesh['branch'=8,'group'=4] {'group'}, dimensions={0}, use_global_device_ids=true | all-gather | bytes 163840 | tf_op jit(solution)/shard_map/all_gather | solution.py:447
  117.4 0.0 copy-done
  117.4 1.5 convolution_bitcast_fusion.far_ref
  118.9 0.0 copy-done.12
  119.0 0.0 copy-done.14
  119.0 0.0 copy-done.15
  119.0 5.1 %reply.1 = bf16[4096,256]{1,0:T(8,128)(2,1)S(1)} custom-call(f32[1024,256]{1,0:T(8,128)S(1)} %near_field.1.image_ref, f32[2,64,256]{2,1,0:T(8,128)S(1)} %convolution_bitcast_fusion.far_ref, bf16[64,256]{1,0:T(8,128)(2,1)S(1)} %copy-done.14, bf16[256,256]{1,0:T(8,128)(2,1)S(1)} %all_gather.3.parents_ref, bf16[2,64,64]{2,1,0:T(8,128)(2,1)S(1)} %copy-done.15, ...), custom_call_target="tpu_custom_call" | custom-call | flops 2147483648 | bytes 4194304 | tf_op jit(solution)/shard_map/reply/pallas_call | solution.py:340
  124.0 0.0 copy-start.5
  124.0 1.3 copy-done.5
  125.4 4.2 %all-to-all-start.3 = ((bf16[32,128,256]{2,1,0:T(8,128)(2,1)}), bf16[32,128,256]{2,1,0:T(8,128)(2,1)}, u32[]{:S(2)}, u32[]{:S(2)}) async-start(bf16[32,128,256]{2,1,0:T(8,128)(2,1)} %bitcast.31), calls=%async_computation.3 | async-start | bytes 4194304 | tf_op jit(solution)/shard_map/all_to_all | solution.py:405
  129.5 0.2 copy.17
  129.7 0.0 copy-done.3
  129.7 0.2 multiply_reduce_fusion.3
  130.0 48.2 %all-to-all-done.3 = bf16[32,128,256]{2,1,0:T(8,128)(2,1)} async-done(((bf16[32,128,256]{2,1,0:T(8,128)(2,1)}), bf16[32,128,256]{2,1,0:T(8,128)(2,1)}, u32[]{:S(2)}, u32[]{:S(2)}) %all-to-all-start.3) | async-done | bytes 2097184 | tf_op jit(solution)/shard_map/all_to_all | solution.py:405
  178.2 7.1 %gather_back.1 = (f32[1024,256]{1,0:T(8,128)S(1)}, f32[8,256]{1,0:T(8,128)S(1)}) custom-call(bf16[4096,256]{1,0:T(8,128)(2,1)} %bitcast.12.ret_ref, f32[1024,8]{1,0:T(8,128)S(1)} %bitcast.32, f32[2,1024,256]{2,1,0:T(8,128)S(1)} %copy-done.3), custom_call_target="tpu_custom_call" | custom-call | flops 4294967296 | bytes 6291456 | tf_op jit(solution)/shard_map/gather_back/pallas_call | solution.py:382
  185.3 0.0 copy-start.6
  185.3 1.0 copy-done.6
  186.4 14.4 %all_to_all.25 = f32[32,6,256]{2,1,0:T(8,128)S(1)} all-to-all(f32[32,6,256]{2,1,0:T(8,128)S(1)} %broadcast_in_dim.11), channel_id=1, replica_groups=mesh['branch'=8,'group'=4] {'branch','group'}, dimensions={0} | all-to-all | bytes 393216 | tf_op jit(solution)/shard_map/all_to_all | solution.py:405
  200.8 0.2 multiply_reduce_fusion
  201.0 0.6 pad_maximum_fusion.1
  201.6 0.4 copy-done.7
  202.0 1.1 subtract_divide_fusion
  (18 shorter events, 0.2 us)
Async XLA Ops:
  0.6 116.8 %copy-start = (bf16[2,16,64,64]{3,2,1,0:T(8,128)(2,1)S(1)}, bf16[2,16,64,64]{3,2,1,0:T(8,128)(2,1)}, u32[]{:S(2)}) copy-start(bf16[2,16,64,64]{3,2,1,0:T(8,128)(2,1)} %param.21) | copy-start | bytes 786436
  0.6 0.8 copy-start.16
  1.4 0.7 copy-start.17
  2.1 0.7 copy-start.18
  3.5 1.6 copy-start.2
  11.5 1.4 copy-start.4
  12.9 7.3 %copy-start.20 = (bf16[2,64,64]{2,1,0:T(8,128)(2,1)S(1)}, bf16[2,64,64]{2,1,0:T(8,128)(2,1)}, u32[]{:S(2)}) copy-start(bf16[2,64,64]{2,1,0:T(8,128)(2,1)} %param.23) | copy-start | bytes 49156
  12.9 62.9 %copy-start.13 = (bf16[2,64,512]{2,1,0:T(8,128)(2,1)S(1)}, bf16[2,64,512]{2,1,0:T(8,128)(2,1)}, u32[]{:S(2)}) copy-start(bf16[2,64,512]{2,1,0:T(8,128)(2,1)} %base_ref.3) | copy-start | bytes 393220
  12.9 58.8 %all-to-all-start = ((s16[32,136,256]{2,1,0:T(8,128)(2,1)}), s16[32,136,256]{2,1,0:T(8,128)(2,1)S(1)}, u32[]{:S(2)}, u32[]{:S(2)}) async-start(s16[32,136,256]{2,1,0:T(8,128)(2,1)} %copy-done.4), calls=%async_computation | async-start | bytes 4456448 | tf_op jit(solution)/shard_map/all_to_all | solution.py:405
  71.7 15.4 %all-to-all-start.2 = ((bf16[8,2,4096]{2,1,0:T(2,128)(2,1)}), bf16[8,2,4096]{2,1,0:T(2,128)(2,1)}, u32[]{:S(2)}, u32[]{:S(2)}) async-start(bf16[8,2,4096]{2,1,0:T(2,128)(2,1)} %reshape.48), calls=%async_computation.2 | async-start | bytes 262144 | tf_op jit(solution)/shard_map/all_to_all | solution.py:405
  75.7 1.2 copy-start.11
  76.9 16.9 %copy-start.21 = (s32[2,16]{1,0:T(2,128)S(1)}, s32[2,16]{1,0:T(2,128)}, u32[]{:S(2)}) copy-start(s32[2,16]{1,0:T(2,128)} %param.22) | copy-start | bytes 388
  76.9 18.8 %copy-start.10 = (s32[2,8]{1,0:T(2,128)S(1)}, s32[2,8]{1,0:T(2,128)}, u32[]{:S(2)}) copy-start(s32[2,8]{1,0:T(2,128)} %list_ref.1) | copy-start | bytes 196
  86.1 1.0 copy-start.8
  87.1 8.7 %copy-start.9 = (f32[1024,256]{1,0:T(8,128)S(1)}, f32[1024,256]{1,0:T(8,128)}, u32[]{:S(2)}) copy-start(f32[1024,256]{1,0:T(8,128)} %copy-done.8) | copy-start | bytes 3145732
  87.9 20.0 %all-to-all-start.1 = ((bf16[8,128,256]{2,1,0:T(8,128)(2,1)}), bf16[8,128,256]{2,1,0:T(8,128)(2,1)}, u32[]{:S(2)}, u32[]{:S(2)}) async-start(bf16[8,128,256]{2,1,0:T(8,128)(2,1)} %broadcast_in_dim.8), calls=%async_computation.1 | async-start | bytes 1048576 | tf_op jit(solution)/shard_map/all_to_all | solution.py:405
  95.8 3.4 %copy-start.1 = (bf16[2,8,512,512]{3,2,1,0:T(8,128)(2,1)S(1)}, bf16[2,8,512,512]{3,2,1,0:T(8,128)(2,1)}, u32[]{:S(2)}) copy-start(bf16[2,8,512,512]{3,2,1,0:T(8,128)(2,1)} %block_ref.1) | copy-start | bytes 25165828
  102.8 7.7 %copy-start.19 = (bf16[8,2,64,64]{3,2,1,0:T(8,128)(2,1)S(1)}, bf16[8,2,64,64]{3,2,1,0:T(8,128)(2,1)}, u32[]{:S(2)}) copy-start(bf16[8,2,64,64]{3,2,1,0:T(8,128)(2,1)} %reshape.49) | copy-start | bytes 393220
  107.9 11.1 %copy-start.12 = (bf16[2,512,512]{2,1,0:T(8,128)(2,1)S(1)}, bf16[2,512,512]{2,1,0:T(8,128)(2,1)}, u32[]{:S(2)}) copy-start(bf16[2,512,512]{2,1,0:T(8,128)(2,1)} %gram_ref.3) | copy-start | bytes 3145732
  107.9 11.1 %copy-start.14 = (bf16[64,256]{1,0:T(8,128)(2,1)S(1)}, bf16[64,256]{1,0:T(8,128)(2,1)}, u32[]{:S(2)}) copy-start(bf16[64,256]{1,0:T(8,128)(2,1)} %top_ref.1) | copy-start | bytes 98308
  107.9 11.1 %copy-start.15 = (bf16[2,64,64]{2,1,0:T(8,128)(2,1)S(1)}, bf16[2,64,64]{2,1,0:T(8,128)(2,1)}, u32[]{:S(2)}) copy-start(bf16[2,64,64]{2,1,0:T(8,128)(2,1)} %descend_ref.1) | copy-start | bytes 49156
  124.0 1.3 copy-start.5
  125.4 4.4 %copy-start.3 = (f32[2,1024,256]{2,1,0:T(8,128)S(1)}, f32[2,1024,256]{2,1,0:T(8,128)}, u32[]{:S(2)}) copy-start(f32[2,1024,256]{2,1,0:T(8,128)} %basis_ref.1) | copy-start | bytes 6291460
  125.4 52.9 %all-to-all-start.3 = ((bf16[32,128,256]{2,1,0:T(8,128)(2,1)}), bf16[32,128,256]{2,1,0:T(8,128)(2,1)}, u32[]{:S(2)}, u32[]{:S(2)}) async-start(bf16[32,128,256]{2,1,0:T(8,128)(2,1)} %bitcast.31), calls=%async_computation.3 | async-start | bytes 4194304 | tf_op jit(solution)/shard_map/all_to_all | solution.py:405
  185.3 1.0 copy-start.6
  200.8 1.2 copy-start.7

commit v2 on v1

--- a/solution.py
+++ b/solution.py
@@ -13,7 +13,10 @@
 TOP = 32767.0
 REST = 65534.0
 LOG2 = 0.6931471805599453
-BLOCK = 512
+SPREAD_BLOCK = 1024
+COLLECT_BLOCK = 2048
+REPLY_BLOCK = 2048
+LANES = 128
 VMEM_LIMIT = 24 << 20
 
 
@@ -38,6 +41,18 @@
 def whole(shape):
     zeros = (0,) * len(shape)
     return pl.BlockSpec(shape, lambda *_: zeros)
+
+
+def in_hbm(shape, dtype):
+    return pltpu.HBM(shape, dtype)
+
+
+def in_vmem(shape, dtype):
+    return pltpu.VMEM(shape, dtype)
+
+
+def kept(values):
+    return pltpu.with_memory_space_constraint(values, pltpu.HBM)
 
 
 def cost(flops, nbytes):
@@ -116,8 +131,9 @@
     )(owner_t, row_t, weight_t)
 
 
-def spread_kernel(slots, vector_ref, rank_ref, side_ref, *refs):
-    outs, (code_ref, level_ref, pick_ref) = refs[:-3], refs[-3:]
+def spread_kernel(
+    slots, vector_ref, rank_ref, side_ref, out_ref, code_ref, level_ref, pick_ref
+):
     step = pl.program_id(0)
     columns = vector_ref.shape[2]
 
@@ -133,31 +149,31 @@
         code_ref[:, columns:] = low.astype(LOW)
 
     rows_dev = rank_ref.shape[1]
-    owners = BLOCK // slots
+    owners = SPREAD_BLOCK // slots
     slot_ids = lax.broadcasted_iota(jnp.int32, (slots, rows_dev), 0).astype(F32)
     for j in range(owners):
         rank = rank_ref[pl.ds(step * owners + j, 1), :]
         pick_ref[j * slots : (j + 1) * slots, :] = jnp.where(slot_ids == rank, 1.0, 0.0).astype(LOW)
     picked = dot(pick_ref[...], code_ref[...])
     codes = (256.0 * picked[:, :columns] + picked[:, columns:]).astype(jnp.int32).astype(CODE)
-    for i, out_ref in enumerate(outs):
-        width = out_ref.shape[2]
-        at = slice(i * width, (i + 1) * width)
-        line = lax.broadcasted_iota(jnp.int32, (8, width), 0)
-        for j in range(owners):
-            extra = jnp.where(line == 3, level_ref[:, at], 0.0)
-            for k in range(3):
-                extra = jnp.where(line == k, side_ref[k, pl.ds(step * owners + j, 1), :], extra)
-            out_ref[j, :slots, :] = codes[j * slots : (j + 1) * slots, at]
-            out_ref[j, slots:, :] = extra.astype(jnp.int32).astype(CODE)
-
-
-def spread_out(basis, rank, side, slots, chunks):
+    line = lax.broadcasted_iota(jnp.int32, (8, LANES), 0)
+    parts = columns // LANES
+    for j in range(owners):
+        extra = jnp.zeros((8, LANES), F32)
+        for k in range(3):
+            extra = jnp.where(line == k, side_ref[k, pl.ds(step * owners + j, 1), :], extra)
+        for h in range(parts):
+            at = slice(h * LANES, (h + 1) * LANES)
+            extra = jnp.where(line == 3 + h, level_ref[:, at], extra)
+            out_ref[j, h * slots : (h + 1) * slots, :] = codes[j * slots : (j + 1) * slots, at]
+        out_ref[j, parts * slots :, :] = extra.astype(jnp.int32).astype(CODE)
+
+
+def spread_out(basis, rank, side, slots):
     devices, rows_dev = rank.shape
     last, columns = basis.shape[0] - 1, basis.shape[2]
-    owners = BLOCK // slots
-    width = columns // chunks
-    shape = (devices, slots + 8, width)
+    owners = SPREAD_BLOCK // slots
+    shape = (devices, columns // LANES * slots + 8, LANES)
     return pl.pallas_call(
         functools.partial(spread_kernel, slots),
         grid=(devices // owners,),
@@ -166,12 +182,12 @@
             whole(rank.shape),
             whole(side.shape),
         ],
-        out_specs=[pl.BlockSpec((owners,) + shape[1:], lambda i: (i, 0, 0))] * chunks,
-        out_shape=[jax.ShapeDtypeStruct(shape, CODE)] * chunks,
+        out_specs=pl.BlockSpec((owners,) + shape[1:], lambda i: (i, 0, 0)),
+        out_shape=in_hbm(shape, CODE),
         scratch_shapes=[
             pltpu.VMEM((rows_dev, 2 * columns), LOW),
             pltpu.VMEM((1, columns), F32),
-            pltpu.VMEM((BLOCK, rows_dev), LOW),
+            pltpu.VMEM((SPREAD_BLOCK, rows_dev), LOW),
         ],
         compiler_params=params(("arbitrary",)),
         cost_estimate=cost(4 * devices * slots * rows_dev * columns, 4 << 20),
@@ -180,23 +196,46 @@
 
 
 def collect_kernel(
-    slots, got_ref, gram_ref, base_ref, first_ref, low_ref, coeff_ref, rows_ref, sum_ref, pick_ref, term_ref
+    slots,
+    got_ref,
+    gram_hbm,
+    base_ref,
+    ascend_ref,
+    first_ref,
+    coeff_ref,
+    rows_ref,
+    sum_ref,
+    pick_ref,
+    term_ref,
+    gram_ref,
+    gram_sem,
 ):
     step = pl.program_id(0)
     rows_dev, width = first_ref.shape
     owners = got_ref.shape[0]
+    parts = width // LANES
+    gram_copy = pltpu.make_async_copy(gram_hbm, gram_ref, gram_sem)
+
+    @pl.when(step == 0)
+    def _():
+        gram_copy.start()
+
     ids = lax.broadcasted_iota(jnp.int32, (rows_dev, slots), 0).astype(F32)
     for j in range(owners):
         at = slice(j * slots, (j + 1) * slots)
-        extra = got_ref[j, slots:, :].astype(jnp.int32).astype(F32)
+        extra = got_ref[j, parts * slots :, :].astype(jnp.int32).astype(F32)
         row = extra[0:1, :slots]
         weight = (extra[1:2, :slots] + extra[2:3, :slots] * (1.0 / REST)) * (1.0 / TOP)
-        scale = jnp.exp(extra[3:4, :] * LOG2) * (1.0 / TOP)
+        weight = column(weight)
         rows_ref[pl.ds(step * owners + j, 1), :] = extra[0:1, :]
-        values = got_ref[j, :slots, :].astype(jnp.int32).astype(F32) * column(weight) * scale
-        high = values.astype(LOW)
-        term_ref[at, :width] = high
-        term_ref[at, width:] = (values - high.astype(F32)).astype(LOW)
+        for h in range(parts):
+            scale = jnp.exp(extra[3 + h : 4 + h, :] * LOG2) * (1.0 / TOP)
+            codes = got_ref[j, h * slots : (h + 1) * slots, :].astype(jnp.int32).astype(F32)
+            values = codes * weight * scale
+            high = values.astype(LOW)
+            term_ref[at, h * LANES : (h + 1) * LANES] = high
+            rest = (values - high.astype(F32)).astype(LOW)
+            term_ref[at, width + h * LANES : width + (h + 1) * LANES] = rest
         pick_ref[:, at] = jnp.where(ids == row, 1.0, 0.0).astype(LOW)
     added = dot(pick_ref[...], term_ref[...])
 
@@ -210,6 +249,7 @@
 
     @pl.when(step == pl.num_programs(0) - 1)
     def _():
+        gram_copy.wait()
         leaves, leaf = gram_ref.shape[:2]
         rank = base_ref.shape[1]
         for l in range(leaves):
@@ -218,49 +258,120 @@
             first = dual + dot(gram_ref[l], dual.astype(LOW), 0, 0)
             low = first.astype(LOW)
             first_ref[at, :] = first
-            low_ref[l] = low
-            coeff_ref[l * rank : (l + 1) * rank, :] = dot(base_ref[l], low).astype(LOW)
-
-
-def collect(got, gram, base):
-    devices, slots, width = got.shape[0], got.shape[1] - 8, got.shape[2]
+            coeff = dot(base_ref[l], low).astype(LOW)
+            for b in range(coeff_ref.shape[0]):
+                coeff_ref[b, l * rank : (l + 1) * rank, :] = coeff
+        for b in range(coeff_ref.shape[0]):
+            coeff_ref[b, leaves * rank :, :] = ascend_ref[...]
+
+
+def collect(got, gram, base, ascend, slots, branches, width):
+    devices = got.shape[0]
     leaves, leaf = gram.shape[:2]
     rank = base.shape[1]
     rows_dev = leaves * leaf
-    owners = BLOCK // slots
+    owners = COLLECT_BLOCK // slots
+    sent_rows = leaves * rank + ascend.shape[0]
     return pl.pallas_call(
         functools.partial(collect_kernel, slots),
         grid=(devices // owners,),
         in_specs=[
             pl.BlockSpec((owners,) + got.shape[1:], lambda i: (i, 0, 0)),
-            whole(gram.shape),
+            pl.BlockSpec(memory_space=pltpu.HBM),
             whole(base.shape),
+            whole(ascend.shape),
         ],
         out_specs=(
             whole((rows_dev, width)),
-            whole((leaves, leaf, width)),
-            whole((leaves * rank, width)),
-            whole((devices, width)),
+            whole((branches, sent_rows, width)),
+            whole((devices, LANES)),
         ),
         out_shape=(
-            jax.ShapeDtypeStruct((rows_dev, width), F32),
-            jax.ShapeDtypeStruct((leaves, leaf, width), LOW),
-            jax.ShapeDtypeStruct((leaves * rank, width), LOW),
-            jax.ShapeDtypeStruct((devices, width), F32),
+            in_vmem((rows_dev, width), F32),
+            in_hbm((branches, sent_rows, width), LOW),
+            in_hbm((devices, LANES), F32),
         ),
         scratch_shapes=[
             pltpu.VMEM((rows_dev, 2 * width), F32),
-            pltpu.VMEM((rows_dev, BLOCK), LOW),
-            pltpu.VMEM((BLOCK, 2 * width), LOW),
+            pltpu.VMEM((rows_dev, COLLECT_BLOCK), LOW),
+            pltpu.VMEM((COLLECT_BLOCK, 2 * width), LOW),
+            pltpu.VMEM(gram.shape, LOW),
+            pltpu.SemaphoreType.DMA,
         ],
         compiler_params=params(("arbitrary",)),
         cost_estimate=cost(4 * devices * slots * rows_dev * width, 4 << 20),
         name="collect",
-    )(got, gram, base)
-
-
-def near_kernel(list_ref, block_ref, low_ref, first_ref, out_ref):
+    )(got, gram, base, ascend)
+
+
+def parent_kernel(coeff_ref, out_ref):
+    rank, width = out_ref.shape
+    branches, rows = coeff_ref.shape[:2]
+    parts = width // rank
+    leaves = rows * parts // (rank * (parts + 1))
+    held = leaves * rank // parts
+    sums = [jnp.zeros((held, width), F32) for _ in range(rank // held)]
+    for b in range(branches):
+        packed = coeff_ref[b, leaves * rank :, :]
+        for q in range(parts):
+            leaf, at = divmod(q * held, rank)
+            term = dot(
+                packed[:, q * rank : (q + 1) * rank], coeff_ref[b, leaf * rank : (leaf + 1) * rank, :]
+            )
+            sums[at // held] = sums[at // held] + term
+    for i, total in enumerate(sums):
+        out_ref[i * held : (i + 1) * held, :] = total.astype(LOW)
+
+
+def parent_of(coeff, rank):
+    width = coeff.shape[2]
+    return pl.pallas_call(
+        parent_kernel,
+        out_shape=in_hbm((rank, width), LOW),
+        compiler_params=params(),
+        cost_estimate=cost(2 * coeff.size * rank, 1 << 20),
+        name="parent_of",
+    )(coeff)
+
+
+def far_kernel(list_ref, coeff_ref, block_ref, out_ref):
+    leaves, items, rank = block_ref.shape[:3]
+    for l in range(leaves):
+        total = jnp.zeros(out_ref.shape[1:], F32)
+        for k in range(items):
+            source = list_ref[l, k]
+            at = pl.ds(pl.multiple_of(source % leaves * rank, rank), rank)
+            total = total + dot(block_ref[l, k], coeff_ref[source // leaves, at, :])
+        out_ref[l] = total
+
+
+def far_field(far_list, coeff, far_block):
+    leaves, items, rank = far_block.shape[:3]
+    width = coeff.shape[2]
+    return pl.pallas_call(
+        far_kernel,
+        grid_spec=pltpu.PrefetchScalarGridSpec(
+            num_scalar_prefetch=1,
+            grid=(1,),
+            in_specs=[whole(coeff.shape), whole(far_block.shape)],
+            out_specs=whole((leaves, rank, width)),
+        ),
+        out_shape=jax.ShapeDtypeStruct((leaves, rank, width), F32),
+        compiler_params=params(("arbitrary",)),
+        cost_estimate=cost(2 * far_block.size * width, 1 << 20),
+        name="far_field",
+    )(far_list, coeff, far_block)
+
+
+def near_kernel(list_ref, block_ref, first_ref, out_ref, low_ref):
     leaf, item = pl.program_id(0), pl.program_id(1)
+    size = out_ref.shape[0]
+
+    @pl.when((leaf == 0) & (item == 0))
+    def _():
+        for l in range(low_ref.shape[0]):
+            low_ref[l] = first_ref[l * size : (l + 1) * size, :].astype(LOW)
+
     count = block_ref.shape[1]
     term = dot(block_ref[0, 0], low_ref[list_ref[leaf, item * count]])
     for k in range(1, count):
@@ -268,16 +379,16 @@
 
     @pl.when(item == 0)
     def _():
-        out_ref[...] = first_ref[...] + term
+        out_ref[...] = first_ref[pl.ds(pl.multiple_of(leaf * size, size), size), :] + term
 
     @pl.when(item > 0)
     def _():
         out_ref[...] += term
 
 
-def near_field(near_list, near_block, low, first):
+def near_field(near_list, near_block, first):
     leaves, items, leaf = near_block.shape[:3]
-    width = low.shape[2]
+    width = first.shape[1]
     count = 4 if items % 4 == 0 else 1
     return pl.pallas_call(
         near_kernel,
@@ -286,38 +397,30 @@
             grid=(leaves, items // count),
             in_specs=[
                 pl.BlockSpec((1, count, leaf, leaf), lambda l, k, _: (l, k, 0, 0)),
-                whole(low.shape),
-                pl.BlockSpec((leaf, width), lambda l, k, _: (l, 0)),
+                whole(first.shape),
             ],
             out_specs=pl.BlockSpec((leaf, width), lambda l, k, _: (l, 0)),
+            scratch_shapes=[pltpu.VMEM((leaves, leaf, width), LOW)],
         ),
-        out_shape=jax.ShapeDtypeStruct(first.shape, F32),
+        out_shape=in_vmem(first.shape, F32),
         compiler_params=params(("arbitrary", "arbitrary")),
         cost_estimate=cost(2 * near_block.size * width, 2 * near_block.size),
         name="near_field",
-    )(near_list, near_block, low, first)
-
-
-def reply_kernel(
-    slots,
-    image_ref,
-    far_ref,
-    top_ref,
-    parents_ref,
-    descend_ref,
-    base_ref,
-    gram_ref,
-    rows_ref,
-    out_ref,
-    dual_ref,
-    pick_ref,
-):
+    )(near_list, near_block, first)
+
+
+def reply_kernel(slots, *refs):
+    image_ref, far_ref, top_ref, descend_ref, base_ref, gram_ref, rows_ref = refs[:7]
+    parents, (out_ref, dual_ref, pick_ref) = refs[7:-3], refs[-3:]
     step = pl.program_id(0)
 
     @pl.when(step == 0)
     def _():
         leaves, leaf = gram_ref.shape[:2]
-        field = dot(top_ref[...], parents_ref[...]).astype(LOW)
+        field = dot(top_ref[0], parents[0][...])
+        for k in range(1, len(parents)):
+            field = field + dot(top_ref[k], parents[k][...])
+        field = field.astype(LOW)
         for l in range(leaves):
             at = slice(l * leaf, (l + 1) * leaf)
             descent = far_ref[l] + dot(descend_ref[l], field)
@@ -325,7 +428,7 @@
             dual_ref[at, :] = (image + dot(gram_ref[l], image.astype(LOW))).astype(LOW)
 
     rows_dev = dual_ref.shape[0]
-    owners = BLOCK // slots
+    owners = REPLY_BLOCK // slots
     ids = lax.broadcasted_iota(jnp.int32, (slots, rows_dev), 1).astype(F32)
     for j in range(owners):
         row = column(rows_ref[pl.ds(step * owners + j, 1), :][:, :slots])
@@ -335,17 +438,17 @@
 
 def reply(image, far, top, parents, descend, base, gram, rows, slots):
     rows_dev, width = image.shape
-    steps = rows.shape[0] * slots // BLOCK
-    args = (image, far, top, parents, descend, base, gram, rows)
+    steps = rows.shape[0] * slots // REPLY_BLOCK
+    args = (image, far, top, descend, base, gram, rows, *parents)
     return pl.pallas_call(
         functools.partial(reply_kernel, slots),
         grid=(steps,),
         in_specs=[whole(a.shape) for a in args],
-        out_specs=pl.BlockSpec((BLOCK, width), lambda i: (i, 0)),
-        out_shape=jax.ShapeDtypeStruct((steps * BLOCK, width), LOW),
-        scratch_shapes=[pltpu.VMEM((rows_dev, width), LOW), pltpu.VMEM((BLOCK, rows_dev), LOW)],
+        out_specs=pl.BlockSpec((REPLY_BLOCK, width), lambda i: (i, 0)),
+        out_shape=in_hbm((steps * REPLY_BLOCK, width), LOW),
+        scratch_shapes=[pltpu.VMEM((rows_dev, width), LOW), pltpu.VMEM((REPLY_BLOCK, rows_dev), LOW)],
         compiler_params=params(("arbitrary",)),
-        cost_estimate=cost(2 * steps * BLOCK * rows_dev * width, 4 << 20),
+        cost_estimate=cost(2 * steps * REPLY_BLOCK * rows_dev * width, 4 << 20),
         name="reply",
     )(*args)
 
@@ -403,6 +506,13 @@
 
 def exchange(values, axes=AXES):
     return lax.all_to_all(values, axes, split_axis=0, concat_axis=0, tiled=True)
+
+
+def swaps(values, axis):
+    size = lax.axis_size(axis)
+    return [values] + [
+        lax.ppermute(values, axis, [(i, i ^ k) for i in range(size)]) for k in range(1, size)
+    ]
 
 
 def to_all(values, axes, size):
@@ -434,21 +544,40 @@
     total = devices * slots
     leaves, rank = leaf_basis.shape[:2]
     rank_of, side, place = route(
-        spread_owner.T, spread_row.T, spread_weight.T, devices, slots, columns
+        kept(spread_owner.T), kept(spread_row.T), kept(spread_weight.T), devices, slots, LANES
     )
-    sent = spread_out(basis, rank_of, side, slots, 1)[0]
+    sent = spread_out(kept(basis), rank_of, side, slots)
+    sent, late_ascend, late_top = lax.optimization_barrier((sent, ascend, top_block))
     got = exchange(sent)
-    ascend_all = to_all(ascend, "branch", branches).reshape((branches * leaves,) + ascend.shape[1:])
-
-    first, low, coeff, rows = collect(got, gram_term, leaf_basis)
-    coeff_all = to_all(coeff, "branch", branches).reshape(branches * leaves, rank, columns)
-    image = near_field(near_list, near_block, low, first)
-    parent = rounded(contract("lrs,lsc->rc", ascend_all, coeff_all))
-    parents = lax.all_gather(parent, "group", axis=0, tiled=True)
-    far = contract("lkrs,lksc->lrc", far_block, coeff_all[far_list])
-    replies = reply(image, far, top_block, parents, descend, leaf_basis, gram_term, rows, slots)
+
+    parts = columns // rank
+    held = leaves * rank // parts
+    packed = late_ascend.reshape(parts, held, rank).transpose(1, 0, 2).reshape(held, columns)
+    columns_of = (jnp.arange(groups) ^ lax.axis_index("group")) % groups
+    top = late_top.reshape(rank, groups, rank).transpose(1, 0, 2)[columns_of]
+
+    got, packed, top = lax.optimization_barrier((got, packed, top))
+    first, coeff, rows = collect(
+        got, kept(gram_term), kept(leaf_basis), kept(packed), slots, branches, columns
+    )
+    coeff = exchange(coeff, "branch")
+    image = near_field(near_list, kept(near_block), first)
+    coeff, image = lax.optimization_barrier((coeff, image))
+    parents = swaps(parent_of(coeff, rank), "group")
+    far = far_field(far_list, coeff, kept(far_block))
+    replies = reply(
+        image,
+        far,
+        kept(top),
+        parents,
+        kept(descend),
+        kept(leaf_basis),
+        kept(gram_term),
+        kept(rows),
+        slots,
+    )
     returned = exchange(replies.reshape(devices, slots, columns)).reshape(total, columns)
-    primal, sums = gather_back(returned, place.T, basis, spread)
+    primal, sums = gather_back(returned, kept(place.T), basis, spread)
     pairs = [(i, j) for i in range(krylov) for j in range(i, krylov)]
     mutual = jnp.stack([jnp.sum(basis[i] * basis[j], axis=0) for i, j in pairs])
     sums = jnp.concatenate([sums[: krylov + 1], mutual], axis=0)

time: 204 us -> 186 us (0.912)
  local copies, waits for them, and re-layouts: 20 us -> 3.81 us
  Pallas kernels: 32.1 us -> 39.9 us
  blocking collectives: 19.9 us -> 14.3 us
  starting transfers between devices: 21.4 us -> 16.6 us
  waiting for transfers between devices: 104 us -> 108 us
  matrix products: 2.83 us -> 0 us
    unnamed x46 -> x12, local copies, waits for them, and re-layouts: 16.1 us -> 0.78 us
    all_to_all x4 -> x3, starting transfers between devices: 21.4 us -> 14.6 us  [exchange(): return lax.all_to_all(values, axes, split_axis=0, concat_axis=0, tiled=True)]
    all_gather x1 -> x0, blocking collectives: 5.51 us -> none  [body(): parents = lax.all_gather(parent, 'group', axis=0, tiled=True)]
    pallas_call x0 -> x2, Pallas kernels: none -> 2.95 us  [the longest x1 2.01 us: far_field(): pl.pallas_call(far_kernel, grid_spec=pltpu.PrefetchScalarGridSpec(num_sca...]
    all_to_all x4 -> x3, waiting for transfers between devices: 104 us -> 107 us  [exchange(): return lax.all_to_all(values, axes, split_axis=0, concat_axis=0, tiled=True)]
    dot_general x2 -> x0, matrix products: 2.83 us -> none  [contract(): return jnp.einsum(pattern, first_op, second_op, preferred_element_type=F32)]
    pallas_call x1, Pallas kernels: 3.7 us -> 6.3 us  [near_field(): pl.pallas_call(near_kernel, grid_spec=pltpu.PrefetchScalarGridSpec(num_sc...]
    ppermute x0 -> x3, starting transfers between devices: none -> 2.06 us  [swaps(): lax.ppermute(values, axis, [(i, i ^ k) for i in range(size)])]
  transfers between devices with their start and end apart: 4 -> 6, of which waited for: 3 -> 5; matrix products, arithmetic and copies ran while one was open for 2% -> 2% of each run, Pallas kernels for 6% -> 4%
where the time goes in v2:
time: 186 us
  waiting for transfers between devices  108 us (58%)
  Pallas kernels  39.9 us (21%)
  starting transfers between devices  16.6 us (9%)
  blocking collectives  14.3 us (8%)
  local copies, waits for them, and re-layouts  3.81 us (2%)
  other arithmetic  2.25 us (1%)
    all_to_all x3, waiting for transfers between devices, exchange(): return lax.all_to_all(values, axes, split_axis=0, concat_axis=0, tiled=True)  107 us
    all_to_all x3, starting transfers between devices, exchange(): return lax.all_to_all(values, axes, split_axis=0, concat_axis=0, tiled=True)  14.6 us
    all_to_all x1, blocking collectives, exchange(): return lax.all_to_all(values, axes, split_axis=0, concat_axis=0, tiled=True)  14.3 us
    pallas_call x1, Pallas kernels, collect(): pl.pallas_call(functools.partial(collect_kernel, slots), grid=(devices //...  8.42 us
    pallas_call x1, Pallas kernels, spread_out(): pl.pallas_call(functools.partial(spread_kernel, slots), grid=(devices //...  7.71 us
    pallas_call x1, Pallas kernels, gather_back(): pl.pallas_call(functools.partial(gather_kernel, spread), grid=(rows_dev /...  7.14 us
    pallas_call x1, Pallas kernels, near_field(): pl.pallas_call(near_kernel, grid_spec=pltpu.PrefetchScalarGridSpec(num_sc...  6.3 us
    pallas_call x1, Pallas kernels, reply(): pl.pallas_call(functools.partial(reply_kernel, slots), grid=(steps,), in_...  6.01 us
  transfers between devices with their start and end apart: 6, of which 5 were waited for; matrix products, arithmetic and copies ran while one was open for 2% of the time, Pallas kernels for 4%

profile of v2, /device:TPU:0, one launch (start us, length us, event | category | flops | bytes accessed | tf_op | source)
XLA Modules:
  0.0 185.8 jit_solution(14070120620537025571)
XLA Ops:
  0.6 1.3 route.1
  2.0 7.7 %spread_out.1 = s16[32,264,128]{2,1,0:T(8,128)(2,1)} custom-call(f32[2,1024,256]{2,1,0:T(8,128)} %basis_ref.1, f32[32,1024]{1,0:T(8,128)S(1)} %get-tuple-element.18.rank_ref, f32[3,32,128]{2,1,0:T(8,128)S(1)} %get-tuple-element.19.side_ref), custom_call_target="tpu_custom_call" | custom-call | flops 4294967296 | bytes 4194304 | tf_op jit(solution)/shard_map/spread_out/pallas_call | solution.py:177
  9.7 0.0 copy-start.5
  9.7 0.0 copy-start.4
  9.7 7.3 %all-to-all-start = ((s16[32,264,128]{2,1,0:T(8,128)(2,1)}), s16[32,264,128]{2,1,0:T(8,128)(2,1)S(1)}, u32[]{:S(2)}, u32[]{:S(2)}) async-start(s16[32,264,128]{2,1,0:T(8,128)(2,1)} %spread_out.1), calls=%async_computation | async-start | bytes 4325376 | tf_op jit(solution)/shard_map/all_to_all | solution.py:508
  17.0 0.0 copy-done.5
  17.0 0.7 reshape.83.ascend_ref
  17.8 0.0 copy-done.4
  17.8 0.1 reshape.84
  17.9 1.2 gather_fusion
  19.1 0.0 copy-start.3
  19.1 48.0 %all-to-all-done.got_ref = s16[32,264,128]{2,1,0:T(8,128)(2,1)S(1)} async-done(((s16[32,264,128]{2,1,0:T(8,128)(2,1)}), s16[32,264,128]{2,1,0:T(8,128)(2,1)S(1)}, u32[]{:S(2)}, u32[]{:S(2)}) %all-to-all-start) | async-done | bytes 2162720 | tf_op jit(solution)/shard_map/all_to_all | solution.py:508
  67.1 8.4 %collect.1 = (f32[1024,256]{1,0:T(8,128)S(1)}, bf16[8,160,256]{2,1,0:T(8,128)(2,1)}, f32[32,128]{1,0:T(8,128)}) custom-call(s16[32,264,128]{2,1,0:T(8,128)(2,1)S(1)} %all-to-all-done.got_ref, bf16[2,512,512]{2,1,0:T(8,128)(2,1)} %refs_5_.1, bf16[2,64,512]{2,1,0:T(8,128)(2,1)} %refs_4_.1, bf16[32,256]{1,0:T(8,128)(2,1)} %reshape.83.ascend_ref), custom_call_target="tpu_custom_call" | custom-call | flops 4294967296 | bytes 4194304 | tf_op jit(solution)/shard_map/collect/pallas_call | solution.py:275
  75.6 3.6 %all-to-all-start.1 = ((bf16[8,160,256]{2,1,0:T(8,128)(2,1)}), bf16[8,160,256]{2,1,0:T(8,128)(2,1)S(1)}, u32[]{:S(2)}, u32[]{:S(2)}) async-start(bf16[8,160,256]{2,1,0:T(8,128)(2,1)} %get-tuple-element.25), calls=%async_computation.1 | async-start | bytes 1310720 | tf_op jit(solution)/shard_map/all_to_all | solution.py:508
  79.2 0.0 copy-done.3
  79.2 0.0 copy-start.2
  79.2 6.3 %near_field.1.refs_0_ = f32[1024,256]{1,0:T(8,128)S(1)} custom-call(s32[2,8]{1,0:T(2,128)S(1)} %copy-done.3, bf16[2,8,512,512]{3,2,1,0:T(8,128)(2,1)} %block_ref.2, f32[1024,256]{1,0:T(8,128)S(1)} %get-tuple-element.26.first_ref), custom_call_target="tpu_custom_call" | custom-call | flops 2147483648 | bytes 8388608 | tf_op jit(solution)/shard_map/near_field/pallas_call | solution.py:393
  85.5 11.2 %all-to-all-done.1.coeff_ref = bf16[8,160,256]{2,1,0:T(8,128)(2,1)S(1)} async-done(((bf16[8,160,256]{2,1,0:T(8,128)(2,1)}), bf16[8,160,256]{2,1,0:T(8,128)(2,1)S(1)}, u32[]{:S(2)}, u32[]{:S(2)}) %all-to-all-start.1) | async-done | bytes 655392 | tf_op jit(solution)/shard_map/all_to_all | solution.py:508
  96.7 0.9 parent_of.1.refs_7_
  97.6 0.0 collective-permute-start
  97.6 1.9 %collective-permute-start.1 = (bf16[64,256]{1,0:T(8,128)(2,1)}, bf16[64,256]{1,0:T(8,128)(2,1)S(1)}, u32[]{:S(2)}, u32[]{:S(2)}) collective-permute-start(bf16[64,256]{1,0:T(8,128)(2,1)} %parent_of.1.refs_7_), channel_id=1, source_target_pairs={{0,2},{1,3},{2,0},{3,1},{4,6},{5,7},{6,4},{7,5},{8,10},{9,11},{10,... | collective-permute-start | bytes 98312 | tf_op jit(solution)/shard_map/ppermute | solution.py:514
  99.6 0.1 collective-permute-start.2
  99.7 0.0 copy-done.2
  99.7 2.0 %far_field.1.refs_1_ = f32[2,64,256]{2,1,0:T(8,128)S(1)} custom-call(s32[2,16]{1,0:T(2,128)S(1)} %copy-done.2, bf16[8,160,256]{2,1,0:T(8,128)(2,1)S(1)} %all-to-all-done.1.coeff_ref, bf16[2,16,64,64]{3,2,1,0:T(8,128)(2,1)} %block_ref.3), custom_call_target="tpu_custom_call" | custom-call | flops 67108864 | bytes 1048576 | tf_op jit(solution)/shard_map/far_field/pallas_call | solution.py:351
  101.7 0.0 collective-permute-done.refs_8_
  101.7 0.1 collective-permute-done.1.refs_9_
  101.9 1.3 collective-permute-done.2.refs_10_
  103.1 0.0 copy-start.1
  103.1 0.8 copy-done.1
  103.9 6.0 %reply.1 = bf16[4096,256]{1,0:T(8,128)(2,1)} custom-call(f32[1024,256]{1,0:T(8,128)S(1)} %near_field.1.refs_0_, f32[2,64,256]{2,1,0:T(8,128)S(1)} %far_field.1.refs_1_, bf16[4,64,64]{2,1,0:T(8,128)(2,1)} %gather_fusion, bf16[2,64,64]{2,1,0:T(8,128)(2,1)} %refs_3_.1, bf16[2,64,512]{2,1,0:T(8,128)(2,1)} %refs_4_.1, bf16[2,512,512]{2,1,0:T(8,128)(2,1)} %refs_5_.1, ...), custom_call_target="tpu_custom_call" | custom-call | flops 2147483648 | bytes 4194304 | tf_op jit(solution)/shard_map/reply/pallas_call | solution.py:443
  109.9 0.0 copy-start
  109.9 3.6 %all-to-all-start.2 = ((bf16[32,128,256]{2,1,0:T(8,128)(2,1)}), bf16[32,128,256]{2,1,0:T(8,128)(2,1)}, u32[]{:S(2)}, u32[]{:S(2)}) async-start(bf16[32,128,256]{2,1,0:T(8,128)(2,1)} %bitcast.20), calls=%async_computation.2 | async-start | bytes 4194304 | tf_op jit(solution)/shard_map/all_to_all | solution.py:508
  113.5 1.0 copy.27
  114.5 0.0 copy-done
  114.5 0.2 multiply_reduce_fusion.3
  114.8 47.4 %all-to-all-done.2 = bf16[32,128,256]{2,1,0:T(8,128)(2,1)} async-done(((bf16[32,128,256]{2,1,0:T(8,128)(2,1)}), bf16[32,128,256]{2,1,0:T(8,128)(2,1)}, u32[]{:S(2)}, u32[]{:S(2)}) %all-to-all-start.2) | async-done | bytes 2097184 | tf_op jit(solution)/shard_map/all_to_all | solution.py:508
  162.2 7.1 %gather_back.1 = (f32[1024,256]{1,0:T(8,128)S(1)}, f32[8,256]{1,0:T(8,128)S(1)}) custom-call(bf16[4096,256]{1,0:T(8,128)(2,1)} %bitcast.8.ret_ref, f32[1024,8]{1,0:T(8,128)} %bitcast.21, f32[2,1024,256]{2,1,0:T(8,128)S(1)} %copy-done), custom_call_target="tpu_custom_call" | custom-call | flops 4294967296 | bytes 6291456 | tf_op jit(solution)/shard_map/gather_back/pallas_call | solution.py:485
  169.4 14.3 %all_to_all.20 = f32[32,6,256]{2,1,0:T(8,128)S(1)} all-to-all(f32[32,6,256]{2,1,0:T(8,128)S(1)} %broadcast_in_dim.2), channel_id=1, replica_groups=mesh['branch'=8,'group'=4] {'branch','group'}, dimensions={0} | all-to-all | bytes 393216 | tf_op jit(solution)/shard_map/all_to_all | solution.py:508
  183.8 0.2 multiply_reduce_fusion
  184.0 0.6 pad_maximum_fusion.1
  184.6 1.1 subtract_divide_fusion
  (11 shorter events, 0.2 us)
Async XLA Ops:
  9.7 7.3 %copy-start.5 = (bf16[2,64,64]{2,1,0:T(8,128)(2,1)S(1)}, bf16[2,64,64]{2,1,0:T(8,128)(2,1)}, u32[]{:S(2)}) copy-start(bf16[2,64,64]{2,1,0:T(8,128)(2,1)} %param.23) | copy-start | bytes 49156
  9.7 8.1 %copy-start.4 = (bf16[64,256]{1,0:T(8,128)(2,1)S(1)}, bf16[64,256]{1,0:T(8,128)(2,1)}, u32[]{:S(2)}) copy-start(bf16[64,256]{1,0:T(8,128)(2,1)} %param.25) | copy-start | bytes 98308
  9.7 57.4 %all-to-all-start = ((s16[32,264,128]{2,1,0:T(8,128)(2,1)}), s16[32,264,128]{2,1,0:T(8,128)(2,1)S(1)}, u32[]{:S(2)}, u32[]{:S(2)}) async-start(s16[32,264,128]{2,1,0:T(8,128)(2,1)} %spread_out.1), calls=%async_computation | async-start | bytes 4325376 | tf_op jit(solution)/shard_map/all_to_all | solution.py:508
  19.1 60.1 %copy-start.3 = (s32[2,8]{1,0:T(2,128)S(1)}, s32[2,8]{1,0:T(2,128)}, u32[]{:S(2)}) copy-start(s32[2,8]{1,0:T(2,128)} %list_ref.2) | copy-start | bytes 196
  75.6 21.1 %all-to-all-start.1 = ((bf16[8,160,256]{2,1,0:T(8,128)(2,1)}), bf16[8,160,256]{2,1,0:T(8,128)(2,1)S(1)}, u32[]{:S(2)}, u32[]{:S(2)}) async-start(bf16[8,160,256]{2,1,0:T(8,128)(2,1)} %get-tuple-element.25), calls=%async_computation.1 | async-start | bytes 1310720 | tf_op jit(solution)/shard_map/all_to_all | solution.py:508
  79.2 20.5 %copy-start.2 = (s32[2,16]{1,0:T(2,128)S(1)}, s32[2,16]{1,0:T(2,128)}, u32[]{:S(2)}) copy-start(s32[2,16]{1,0:T(2,128)} %list_ref.3) | copy-start | bytes 388
  97.6 4.1 %collective-permute-start = (bf16[64,256]{1,0:T(8,128)(2,1)}, bf16[64,256]{1,0:T(8,128)(2,1)S(1)}, u32[]{:S(2)}, u32[]{:S(2)}) collective-permute-start(bf16[64,256]{1,0:T(8,128)(2,1)} %parent_of.1.refs_7_), channel_id=1, source_target_pairs={{0,1},{1,0},{2,3},{3,2},{4,5},{5,4},{6,7},{7,6},{8,9},{9,8},{10,11... | collective-permute-start | bytes 98312 | tf_op jit(solution)/shard_map/ppermute | solution.py:514
  97.6 4.2 %collective-permute-start.1 = (bf16[64,256]{1,0:T(8,128)(2,1)}, bf16[64,256]{1,0:T(8,128)(2,1)S(1)}, u32[]{:S(2)}, u32[]{:S(2)}) collective-permute-start(bf16[64,256]{1,0:T(8,128)(2,1)} %parent_of.1.refs_7_), channel_id=1, source_target_pairs={{0,2},{1,3},{2,0},{3,1},{4,6},{5,7},{6,4},{7,5},{8,10},{9,11},{10,... | collective-permute-start | bytes 98312 | tf_op jit(solution)/shard_map/ppermute | solution.py:514
  99.6 3.6 %collective-permute-start.2 = (bf16[64,256]{1,0:T(8,128)(2,1)}, bf16[64,256]{1,0:T(8,128)(2,1)S(1)}, u32[]{:S(2)}, u32[]{:S(2)}) collective-permute-start(bf16[64,256]{1,0:T(8,128)(2,1)} %parent_of.1.refs_7_), channel_id=1, source_target_pairs={{0,3},{1,2},{2,1},{3,0},{4,7},{5,6},{6,5},{7,4},{8,11},{9,10},{10,... | collective-permute-start | bytes 98312 | tf_op jit(solution)/shard_map/ppermute | solution.py:514
  103.1 0.8 copy-start.1
  109.9 4.6 %copy-start = (f32[2,1024,256]{2,1,0:T(8,128)S(1)}, f32[2,1024,256]{2,1,0:T(8,128)}, u32[]{:S(2)}) copy-start(f32[2,1024,256]{2,1,0:T(8,128)} %basis_ref.1) | copy-start | bytes 6291460
  109.9 52.3 %all-to-all-start.2 = ((bf16[32,128,256]{2,1,0:T(8,128)(2,1)}), bf16[32,128,256]{2,1,0:T(8,128)(2,1)}, u32[]{:S(2)}, u32[]{:S(2)}) async-start(bf16[32,128,256]{2,1,0:T(8,128)(2,1)} %bitcast.20), calls=%async_computation.2 | async-start | bytes 4194304 | tf_op jit(solution)/shard_map/all_to_all | solution.py:508

commit v3 on v2

--- a/solution.py
+++ b/solution.py
@@ -14,10 +14,9 @@
 REST = 65534.0
 LOG2 = 0.6931471805599453
 SPREAD_BLOCK = 1024
-COLLECT_BLOCK = 2048
-REPLY_BLOCK = 2048
+COLLECT_BLOCK = 512
+REPLY_BLOCK = 1024
 LANES = 128
-VMEM_LIMIT = 24 << 20
 
 
 def rounded(values):
@@ -34,8 +33,8 @@
     )
 
 
-def params(semantics=None):
-    return pltpu.CompilerParams(dimension_semantics=semantics, vmem_limit_bytes=VMEM_LIMIT)
+def params(semantics=None, mib=24):
+    return pltpu.CompilerParams(dimension_semantics=semantics, vmem_limit_bytes=mib << 20)
 
 
 def whole(shape):
@@ -49,6 +48,10 @@
 
 def in_vmem(shape, dtype):
     return pltpu.VMEM(shape, dtype)
+
+
+def near_by(values):
+    return pltpu.with_memory_space_constraint(values, pltpu.VMEM)
 
 
 def kept(values):
@@ -72,7 +75,7 @@
     return high, code - 256.0 * high
 
 
-def route_kernel(slots, owner_ref, row_ref, weight_ref, rank_ref, side_ref, place_ref):
+def find_routes(slots, owner_ref, row_ref, weight_ref, rank_ref, side_ref, place_ref):
     devices, rows_dev = rank_ref.shape
     spread = owner_ref.shape[0]
     width = side_ref.shape[2]
@@ -116,30 +119,32 @@
         side_ref[i] = 256.0 * high + low
 
 
-def route(owner_t, row_t, weight_t, devices, slots, width):
-    rows_dev = owner_t.shape[1]
-    return pl.pallas_call(
-        functools.partial(route_kernel, slots),
-        out_shape=(
-            jax.ShapeDtypeStruct((devices, rows_dev), F32),
-            jax.ShapeDtypeStruct((3, devices, width), F32),
-            jax.ShapeDtypeStruct((8, rows_dev), F32),
-        ),
-        compiler_params=params(),
-        cost_estimate=cost(1e8, 1 << 19),
-        name="route",
-    )(owner_t, row_t, weight_t)
-
-
 def spread_kernel(
-    slots, vector_ref, rank_ref, side_ref, out_ref, code_ref, level_ref, pick_ref
+    slots,
+    owner_ref,
+    row_ref,
+    weight_ref,
+    basis_hbm,
+    out_ref,
+    place_ref,
+    vector_ref,
+    rank_ref,
+    side_ref,
+    code_ref,
+    level_ref,
+    pick_ref,
+    vector_sem,
 ):
     step = pl.program_id(0)
-    columns = vector_ref.shape[2]
+    columns = vector_ref.shape[1]
 
     @pl.when(step == 0)
     def _():
-        vector = vector_ref[0]
+        copy = pltpu.make_async_copy(basis_hbm.at[basis_hbm.shape[0] - 1], vector_ref, vector_sem)
+        copy.start()
+        find_routes(slots, owner_ref, row_ref, weight_ref, rank_ref, side_ref, place_ref)
+        copy.wait()
+        vector = vector_ref[...]
         peak = jnp.maximum(jnp.max(jnp.abs(vector), axis=0, keepdims=True), 1e-30)
         level = jnp.floor(jnp.log(peak) * (1.0 / LOG2)) + 1.0
         level_ref[...] = level
@@ -169,139 +174,194 @@
         out_ref[j, parts * slots :, :] = extra.astype(jnp.int32).astype(CODE)
 
 
-def spread_out(basis, rank, side, slots):
-    devices, rows_dev = rank.shape
-    last, columns = basis.shape[0] - 1, basis.shape[2]
+def spread_out(owner_t, row_t, weight_t, basis, devices, slots):
+    rows_dev, columns = basis.shape[1:]
     owners = SPREAD_BLOCK // slots
     shape = (devices, columns // LANES * slots + 8, LANES)
     return pl.pallas_call(
         functools.partial(spread_kernel, slots),
         grid=(devices // owners,),
         in_specs=[
-            pl.BlockSpec((1, rows_dev, columns), lambda i: (last, 0, 0)),
-            whole(rank.shape),
-            whole(side.shape),
+            whole(owner_t.shape),
+            whole(row_t.shape),
+            whole(weight_t.shape),
+            pl.BlockSpec(memory_space=pltpu.HBM),
         ],
-        out_specs=pl.BlockSpec((owners,) + shape[1:], lambda i: (i, 0, 0)),
-        out_shape=in_hbm(shape, CODE),
+        out_specs=(
+            pl.BlockSpec((owners,) + shape[1:], lambda i: (i, 0, 0)),
+            whole((8, rows_dev)),
+        ),
+        out_shape=(in_hbm(shape, CODE), in_hbm((8, rows_dev), F32)),
         scratch_shapes=[
+            pltpu.VMEM((rows_dev, columns), F32),
+            pltpu.VMEM((devices, rows_dev), F32),
+            pltpu.VMEM((3, devices, LANES), F32),
             pltpu.VMEM((rows_dev, 2 * columns), LOW),
             pltpu.VMEM((1, columns), F32),
             pltpu.VMEM((SPREAD_BLOCK, rows_dev), LOW),
+            pltpu.SemaphoreType.DMA,
         ],
         compiler_params=params(("arbitrary",)),
         cost_estimate=cost(4 * devices * slots * rows_dev * columns, 4 << 20),
         name="spread_out",
-    )(basis, rank, side)
+    )(owner_t, row_t, weight_t, basis)
+
+
+def add_slots(slots, low_part, got_ref, rows_ref, sum_ref, picks, terms):
+    rows_dev, width = sum_ref.shape
+    owners = COLLECT_BLOCK // slots
+    parts = width // LANES
+    blocks = got_ref.shape[0] // owners
+    tile = 16
+    ids = lax.broadcasted_iota(jnp.int32, (rows_dev, slots), 0).astype(CODE)
+    one, zero = jnp.ones((rows_dev, slots), LOW), jnp.zeros((rows_dev, slots), LOW)
+
+    def build(block):
+        pick_ref, term_ref = picks[block % 2], terms[block % 2]
+        for j in range(owners):
+            at = slice(j * slots, (j + 1) * slots)
+            source = block * owners + j
+            extra = got_ref[source, parts * slots :, :].astype(jnp.int32)
+            row = jnp.broadcast_to(extra[0:1, :slots], (tile, slots)).astype(CODE)
+            row = jnp.broadcast_to(row[None], (rows_dev // tile, tile, slots))
+            pick_ref[:, at] = jnp.where(ids == row.reshape(rows_dev, slots), one, zero)
+            extra = extra.astype(F32)
+            weight = (extra[1:2, :slots] + extra[2:3, :slots] * (1.0 / REST)) * (1.0 / TOP)
+            weight = column(weight)
+            if rows_ref is not None:
+                rows_ref[source : source + 1, :] = extra[0:1, :]
+            for h in range(parts):
+                scale = jnp.exp(extra[3 + h : 4 + h, :] * LOG2) * (1.0 / TOP)
+                codes = got_ref[source, h * slots : (h + 1) * slots, :].astype(jnp.int32).astype(F32)
+                values = codes * weight * scale
+                term = values.astype(LOW)
+                if low_part:
+                    term = (values - term.astype(F32)).astype(LOW)
+                term_ref[at, h * LANES : (h + 1) * LANES] = term
+
+    build(0)
+    for block in range(blocks):
+        if block + 1 < blocks:
+            build(block + 1)
+        added = dot(picks[block % 2][...], terms[block % 2][...])
+        sum_ref[...] = added if block == 0 else sum_ref[...] + added
+
+
+def rise_kernel(base_ref, gram_ref, out_ref):
+    for l in range(base_ref.shape[0]):
+        base = base_ref[l]
+        out_ref[l] = (base.astype(F32) + dot(base, gram_ref[l], 1, 1)).astype(LOW)
+
+
+def rise(base, gram):
+    return pl.pallas_call(
+        rise_kernel,
+        out_shape=in_vmem(base.shape, LOW),
+        compiler_params=params(mib=8),
+        cost_estimate=cost(2 * gram.size * base.shape[1], 2 * gram.size),
+        name="rise",
+    )(base, gram)
 
 
 def collect_kernel(
     slots,
     got_ref,
-    gram_hbm,
-    base_ref,
+    rise_ref,
     ascend_ref,
-    first_ref,
+    dual_ref,
     coeff_ref,
     rows_ref,
-    sum_ref,
-    pick_ref,
-    term_ref,
-    gram_ref,
-    gram_sem,
+    pick_a,
+    pick_b,
+    term_a,
+    term_b,
 ):
-    step = pl.program_id(0)
-    rows_dev, width = first_ref.shape
-    owners = got_ref.shape[0]
-    parts = width // LANES
-    gram_copy = pltpu.make_async_copy(gram_hbm, gram_ref, gram_sem)
-
-    @pl.when(step == 0)
-    def _():
-        gram_copy.start()
-
-    ids = lax.broadcasted_iota(jnp.int32, (rows_dev, slots), 0).astype(F32)
-    for j in range(owners):
-        at = slice(j * slots, (j + 1) * slots)
-        extra = got_ref[j, parts * slots :, :].astype(jnp.int32).astype(F32)
-        row = extra[0:1, :slots]
-        weight = (extra[1:2, :slots] + extra[2:3, :slots] * (1.0 / REST)) * (1.0 / TOP)
-        weight = column(weight)
-        rows_ref[pl.ds(step * owners + j, 1), :] = extra[0:1, :]
-        for h in range(parts):
-            scale = jnp.exp(extra[3 + h : 4 + h, :] * LOG2) * (1.0 / TOP)
-            codes = got_ref[j, h * slots : (h + 1) * slots, :].astype(jnp.int32).astype(F32)
-            values = codes * weight * scale
-            high = values.astype(LOW)
-            term_ref[at, h * LANES : (h + 1) * LANES] = high
-            rest = (values - high.astype(F32)).astype(LOW)
-            term_ref[at, width + h * LANES : width + (h + 1) * LANES] = rest
-        pick_ref[:, at] = jnp.where(ids == row, 1.0, 0.0).astype(LOW)
-    added = dot(pick_ref[...], term_ref[...])
-
-    @pl.when(step == 0)
-    def _():
-        sum_ref[...] = added
-
-    @pl.when(step > 0)
-    def _():
-        sum_ref[...] += added
-
-    @pl.when(step == pl.num_programs(0) - 1)
-    def _():
-        gram_copy.wait()
-        leaves, leaf = gram_ref.shape[:2]
-        rank = base_ref.shape[1]
-        for l in range(leaves):
-            at = slice(l * leaf, (l + 1) * leaf)
-            dual = sum_ref[at, :width] + sum_ref[at, width:]
-            first = dual + dot(gram_ref[l], dual.astype(LOW), 0, 0)
-            low = first.astype(LOW)
-            first_ref[at, :] = first
-            coeff = dot(base_ref[l], low).astype(LOW)
-            for b in range(coeff_ref.shape[0]):
-                coeff_ref[b, l * rank : (l + 1) * rank, :] = coeff
+    add_slots(slots, False, got_ref, rows_ref, dual_ref, (pick_a, pick_b), (term_a, term_b))
+    leaves, rank, leaf = rise_ref.shape
+    for b in range(coeff_ref.shape[0]):
+        coeff_ref[b, leaves * rank :, :] = ascend_ref[...]
+    for l in range(leaves):
+        dual = dual_ref[l * leaf : (l + 1) * leaf, :]
+        coeff = dot(rise_ref[l], dual.astype(LOW)).astype(LOW)
         for b in range(coeff_ref.shape[0]):
-            coeff_ref[b, leaves * rank :, :] = ascend_ref[...]
-
-
-def collect(got, gram, base, ascend, slots, branches, width):
+            coeff_ref[b, l * rank : (l + 1) * rank, :] = coeff
+
+
+def slot_scratch(rows_dev, width):
+    return [
+        pltpu.VMEM((rows_dev, COLLECT_BLOCK), LOW),
+        pltpu.VMEM((rows_dev, COLLECT_BLOCK), LOW),
+        pltpu.VMEM((COLLECT_BLOCK, width), LOW),
+        pltpu.VMEM((COLLECT_BLOCK, width), LOW),
+    ]
+
+
+def collect(got, lift, ascend, slots, branches, width):
     devices = got.shape[0]
-    leaves, leaf = gram.shape[:2]
-    rank = base.shape[1]
+    leaves, rank, leaf = lift.shape
     rows_dev = leaves * leaf
-    owners = COLLECT_BLOCK // slots
     sent_rows = leaves * rank + ascend.shape[0]
+    direct = pl.BlockSpec(memory_space=pltpu.VMEM)
     return pl.pallas_call(
         functools.partial(collect_kernel, slots),
-        grid=(devices // owners,),
-        in_specs=[
-            pl.BlockSpec((owners,) + got.shape[1:], lambda i: (i, 0, 0)),
-            pl.BlockSpec(memory_space=pltpu.HBM),
-            whole(base.shape),
-            whole(ascend.shape),
-        ],
-        out_specs=(
-            whole((rows_dev, width)),
-            whole((branches, sent_rows, width)),
-            whole((devices, LANES)),
-        ),
+        in_specs=[direct] * 3,
+        out_specs=[direct] * 3,
         out_shape=(
             in_vmem((rows_dev, width), F32),
             in_hbm((branches, sent_rows, width), LOW),
             in_hbm((devices, LANES), F32),
         ),
+        scratch_shapes=slot_scratch(rows_dev, width),
+        compiler_params=params(),
+        cost_estimate=cost(2 * devices * slots * rows_dev * width, 4 << 20),
+        name="collect",
+    )(got, lift, ascend)
+
+
+def refine_kernel(
+    slots,
+    got_ref,
+    dual_ref,
+    gram_hbm,
+    out_ref,
+    sum_ref,
+    gram_ref,
+    gram_sem,
+    pick_a,
+    pick_b,
+    term_a,
+    term_b,
+):
+    gram_copy = pltpu.make_async_copy(gram_hbm, gram_ref, gram_sem)
+    gram_copy.start()
+    add_slots(slots, True, got_ref, None, sum_ref, (pick_a, pick_b), (term_a, term_b))
+    gram_copy.wait()
+    leaves, leaf = gram_ref.shape[:2]
+    for l in range(leaves):
+        at = slice(l * leaf, (l + 1) * leaf)
+        dual = dual_ref[at, :] + sum_ref[at, :]
+        out_ref[at, :] = dual + dot(gram_ref[l], dual.astype(LOW), 0, 0)
+
+
+def refine(got, dual, gram, slots):
+    rows_dev, width = dual.shape
+    devices = got.shape[0]
+    direct = pl.BlockSpec(memory_space=pltpu.VMEM)
+    return pl.pallas_call(
+        functools.partial(refine_kernel, slots),
+        in_specs=[direct, direct, pl.BlockSpec(memory_space=pltpu.HBM)],
+        out_specs=direct,
+        out_shape=in_vmem(dual.shape, F32),
         scratch_shapes=[
-            pltpu.VMEM((rows_dev, 2 * width), F32),
-            pltpu.VMEM((rows_dev, COLLECT_BLOCK), LOW),
-            pltpu.VMEM((COLLECT_BLOCK, 2 * width), LOW),
+            pltpu.VMEM((rows_dev, width), F32),
             pltpu.VMEM(gram.shape, LOW),
             pltpu.SemaphoreType.DMA,
-        ],
-        compiler_params=params(("arbitrary",)),
-        cost_estimate=cost(4 * devices * slots * rows_dev * width, 4 << 20),
-        name="collect",
-    )(got, gram, base, ascend)
+        ]
+        + slot_scratch(rows_dev, width),
+        compiler_params=params(),
+        cost_estimate=cost(2 * devices * slots * rows_dev * width, 4 << 20),
+        name="refine",
+    )(got, dual, gram)
 
 
 def parent_kernel(coeff_ref, out_ref):
@@ -327,8 +387,8 @@
     width = coeff.shape[2]
     return pl.pallas_call(
         parent_kernel,
-        out_shape=in_hbm((rank, width), LOW),
-        compiler_params=params(),
+        out_shape=in_vmem((rank, width), LOW),
+        compiler_params=params(mib=6),
         cost_estimate=cost(2 * coeff.size * rank, 1 << 20),
         name="parent_of",
     )(coeff)
@@ -357,7 +417,7 @@
             out_specs=whole((leaves, rank, width)),
         ),
         out_shape=jax.ShapeDtypeStruct((leaves, rank, width), F32),
-        compiler_params=params(("arbitrary",)),
+        compiler_params=params(("arbitrary",), 6),
         cost_estimate=cost(2 * far_block.size * width, 1 << 20),
         name="far_field",
     )(far_list, coeff, far_block)
@@ -403,57 +463,86 @@
             scratch_shapes=[pltpu.VMEM((leaves, leaf, width), LOW)],
         ),
         out_shape=in_vmem(first.shape, F32),
-        compiler_params=params(("arbitrary", "arbitrary")),
+        compiler_params=params(("arbitrary", "arbitrary"), 12),
         cost_estimate=cost(2 * near_block.size * width, 2 * near_block.size),
         name="near_field",
     )(near_list, near_block, first)
 
 
+def prepare_kernel(image_ref, base_ref, gram_ref, dual_ref, lift_ref):
+    leaves, leaf = gram_ref.shape[:2]
+    ids = lax.broadcasted_iota(jnp.int32, (leaf, leaf), 0)
+    same = ids == lax.broadcasted_iota(jnp.int32, (leaf, leaf), 1)
+    unit = jnp.where(same, 1.0, 0.0).astype(LOW)
+    for l in range(leaves):
+        at = slice(l * leaf, (l + 1) * leaf)
+        image = image_ref[at, :]
+        dual_ref[at, :] = image + dot(gram_ref[l], image.astype(LOW))
+        lifted = dot(unit, base_ref[l], 1, 1) + dot(gram_ref[l], base_ref[l], 1, 1)
+        parts = [lifted if i == l else jnp.zeros_like(lifted) for i in range(leaves)]
+        lift_ref[at, :] = jnp.concatenate(parts, axis=1).astype(LOW)
+
+
+def prepare(image, base, gram):
+    rows_dev, width = image.shape
+    lanes = base.shape[0] * base.shape[1]
+    return pl.pallas_call(
+        prepare_kernel,
+        out_shape=(in_vmem((rows_dev, width), F32), in_vmem((rows_dev, lanes), LOW)),
+        compiler_params=params(mib=12),
+        cost_estimate=cost(2 * gram.size * (width + 2 * lanes), 4 << 20),
+        name="prepare",
+    )(image, base, gram)
+
+
 def reply_kernel(slots, *refs):
-    image_ref, far_ref, top_ref, descend_ref, base_ref, gram_ref, rows_ref = refs[:7]
-    parents, (out_ref, dual_ref, pick_ref) = refs[7:-3], refs[-3:]
+    dual_ref, lift_ref, far_ref, top_ref, descend_ref, rows_ref = refs[:6]
+    parents, (out_ref, field_ref, low_ref, pick_ref) = refs[6:-4], refs[-4:]
     step = pl.program_id(0)
 
     @pl.when(step == 0)
     def _():
-        leaves, leaf = gram_ref.shape[:2]
+        leaves, rank = far_ref.shape[:2]
         field = dot(top_ref[0], parents[0][...])
         for k in range(1, len(parents)):
             field = field + dot(top_ref[k], parents[k][...])
         field = field.astype(LOW)
         for l in range(leaves):
-            at = slice(l * leaf, (l + 1) * leaf)
             descent = far_ref[l] + dot(descend_ref[l], field)
-            image = image_ref[at, :] + dot(base_ref[l], descent.astype(LOW), 0, 0)
-            dual_ref[at, :] = (image + dot(gram_ref[l], image.astype(LOW))).astype(LOW)
-
-    rows_dev = dual_ref.shape[0]
+            field_ref[l * rank : (l + 1) * rank, :] = descent.astype(LOW)
+        low_ref[...] = (dual_ref[...] + dot(lift_ref[...], field_ref[...])).astype(LOW)
+
     owners = REPLY_BLOCK // slots
-    ids = lax.broadcasted_iota(jnp.int32, (slots, rows_dev), 1).astype(F32)
+    ids = lax.broadcasted_iota(jnp.int32, (slots, low_ref.shape[0]), 1).astype(F32)
     for j in range(owners):
         row = column(rows_ref[pl.ds(step * owners + j, 1), :][:, :slots])
         pick_ref[j * slots : (j + 1) * slots, :] = jnp.where(ids == row, 1.0, 0.0).astype(LOW)
-    out_ref[...] = dot(pick_ref[...], dual_ref[...]).astype(LOW)
-
-
-def reply(image, far, top, parents, descend, base, gram, rows, slots):
-    rows_dev, width = image.shape
-    steps = rows.shape[0] * slots // REPLY_BLOCK
-    args = (image, far, top, descend, base, gram, rows, *parents)
+    out_ref[...] = dot(pick_ref[...], low_ref[...]).astype(LOW)
+
+
+def reply(dual, lift, far, top, parents, descend, rows, slots):
+    rows_dev, width = dual.shape
+    total = rows.shape[0] * slots
+    args = (far, top, descend, rows, *parents)
+    direct = pl.BlockSpec(memory_space=pltpu.VMEM)
     return pl.pallas_call(
         functools.partial(reply_kernel, slots),
-        grid=(steps,),
-        in_specs=[whole(a.shape) for a in args],
+        grid=(total // REPLY_BLOCK,),
+        in_specs=[direct, direct] + [whole(a.shape) for a in args[:4]] + [direct] * len(parents),
         out_specs=pl.BlockSpec((REPLY_BLOCK, width), lambda i: (i, 0)),
-        out_shape=in_hbm((steps * REPLY_BLOCK, width), LOW),
-        scratch_shapes=[pltpu.VMEM((rows_dev, width), LOW), pltpu.VMEM((REPLY_BLOCK, rows_dev), LOW)],
-        compiler_params=params(("arbitrary",)),
-        cost_estimate=cost(2 * steps * REPLY_BLOCK * rows_dev * width, 4 << 20),
+        out_shape=in_hbm((total, width), LOW),
+        scratch_shapes=[
+            pltpu.VMEM((lift.shape[1], width), LOW),
+            pltpu.VMEM((rows_dev, width), LOW),
+            pltpu.VMEM((REPLY_BLOCK, rows_dev), LOW),
+        ],
+        compiler_params=params(("arbitrary",), 16),
+        cost_estimate=cost(2 * total * rows_dev * width, 4 << 20),
         name="reply",
-    )(*args)
-
-
-def gather_kernel(spread, ret_ref, place_ref, basis_ref, image_ref, sums_ref):
+    )(dual, lift, *args)
+
+
+def gather_kernel(spread, ret_ref, place_ref, basis_ref, mutual_ref, image_ref, sums_ref):
     step = pl.program_id(0)
     rows = place_ref.shape[0]
     total = ret_ref.shape[0]
@@ -466,19 +555,20 @@
     krylov = basis_ref.shape[0]
     parts = [jnp.sum(basis_ref[k] * image, axis=0, keepdims=True) for k in range(krylov)]
     parts.append(jnp.sum(image * image, axis=0, keepdims=True))
-    parts.append(jnp.zeros((sums_ref.shape[0] - krylov - 1, image.shape[1]), F32))
     added = jnp.concatenate(parts, axis=0)
 
     @pl.when(step == 0)
     def _():
-        sums_ref[...] = added
+        sums_ref[: krylov + 1, :] = added
+        sums_ref[krylov + 1 :, :] = mutual_ref[...]
 
     @pl.when(step > 0)
     def _():
-        sums_ref[...] += added
-
-
-def gather_back(ret, place_col, basis, spread):
+        sums_ref[: krylov + 1, :] += added
+
+
+def gather_back(ret, place_col, basis, mutual, spread):
+    lines = basis.shape[0] + 1 + mutual.shape[0]
     total, width = ret.shape
     krylov, rows_dev = basis.shape[:2]
     rows = 256
@@ -486,19 +576,20 @@
         functools.partial(gather_kernel, spread),
         grid=(rows_dev // rows,),
         in_specs=[
-            whole(ret.shape),
+            pl.BlockSpec(memory_space=pltpu.VMEM),
             pl.BlockSpec((rows, place_col.shape[1]), lambda i: (i, 0)),
             pl.BlockSpec((krylov, rows, width), lambda i: (0, i, 0)),
+            whole(mutual.shape),
         ],
-        out_specs=(pl.BlockSpec((rows, width), lambda i: (i, 0)), whole((8, width))),
+        out_specs=(pl.BlockSpec((rows, width), lambda i: (i, 0)), whole((lines, width))),
         out_shape=(
             jax.ShapeDtypeStruct((rows_dev, width), F32),
-            jax.ShapeDtypeStruct((8, width), F32),
+            jax.ShapeDtypeStruct((lines, width), F32),
         ),
         compiler_params=params(("arbitrary",)),
         cost_estimate=cost(2 * spread * total * rows_dev * width, 6 << 20),
         name="gather_back",
-    )(ret, place_col, basis)
+    )(ret, place_col, basis, mutual)
 
 
 AXES = ("branch", "group")
@@ -543,11 +634,12 @@
     slots = 2 * spread * rows_dev // devices
     total = devices * slots
     leaves, rank = leaf_basis.shape[:2]
-    rank_of, side, place = route(
-        kept(spread_owner.T), kept(spread_row.T), kept(spread_weight.T), devices, slots, LANES
+    sent, place = spread_out(
+        kept(spread_owner.T), kept(spread_row.T), kept(spread_weight.T), kept(basis), devices, slots
     )
-    sent = spread_out(kept(basis), rank_of, side, slots)
-    sent, late_ascend, late_top = lax.optimization_barrier((sent, ascend, top_block))
+    sent, late_ascend, late_top, late_base, late_gram = lax.optimization_barrier(
+        (sent, ascend, top_block, leaf_basis, gram_term)
+    )
     got = exchange(sent)
 
     parts = columns // rank
@@ -556,31 +648,21 @@
     columns_of = (jnp.arange(groups) ^ lax.axis_index("group")) % groups
     top = late_top.reshape(rank, groups, rank).transpose(1, 0, 2)[columns_of]
 
-    got, packed, top = lax.optimization_barrier((got, packed, top))
-    first, coeff, rows = collect(
-        got, kept(gram_term), kept(leaf_basis), kept(packed), slots, branches, columns
-    )
-    coeff = exchange(coeff, "branch")
+    raised = rise(late_base, late_gram)
+    got, packed, top, raised = lax.optimization_barrier((got, packed, top, raised))
+    dual, coeff, rows = collect(got, raised, packed, slots, branches, columns)
+    coeff = kept(exchange(coeff, "branch"))
+    first = refine(got, dual, kept(gram_term), slots)
     image = near_field(near_list, kept(near_block), first)
-    coeff, image = lax.optimization_barrier((coeff, image))
+    dual, lift = prepare(image, kept(leaf_basis), kept(gram_term))
+    coeff, dual, lift = lax.optimization_barrier((coeff, dual, lift))
     parents = swaps(parent_of(coeff, rank), "group")
     far = far_field(far_list, coeff, kept(far_block))
-    replies = reply(
-        image,
-        far,
-        kept(top),
-        parents,
-        kept(descend),
-        kept(leaf_basis),
-        kept(gram_term),
-        kept(rows),
-        slots,
-    )
+    replies = reply(dual, lift, far, kept(top), parents, kept(descend), kept(rows), slots)
     returned = exchange(replies.reshape(devices, slots, columns)).reshape(total, columns)
-    primal, sums = gather_back(returned, kept(place.T), basis, spread)
     pairs = [(i, j) for i in range(krylov) for j in range(i, krylov)]
     mutual = jnp.stack([jnp.sum(basis[i] * basis[j], axis=0) for i, j in pairs])
-    sums = jnp.concatenate([sums[: krylov + 1], mutual], axis=0)
+    primal, sums = gather_back(near_by(returned), kept(place.T), basis, mutual, spread)
     sums = jnp.sum(to_all(sums, AXES, devices), axis=0)
     mutual = sums[krylov + 1 :]
 

time: 186 us -> 182 us (0.978)
  waiting for transfers between devices: 108 us -> 99.1 us
  Pallas kernels: 39.9 us -> 44.7 us
    all_to_all x3, waiting for transfers between devices: 107 us -> 98 us  [exchange(): return lax.all_to_all(values, axes, split_axis=0, concat_axis=0, tiled=True)]
    pallas_call x4 -> x6, Pallas kernels: 16.7 us -> 20.6 us  [the longest x1 5.94 us: refine(): pl.pallas_call(functools.partial(refine_kernel, slots), in_specs=[direct,...]
  transfers between devices with their start and end apart: 6 -> 6, of which waited for: 5 -> 4; matrix products, arithmetic and copies ran while one was open for 2% -> 1% of each run, Pallas kernels for 4% -> 10%
where the time goes in v3:
time: 182 us; the launch traced here: 181 us
  waiting for transfers between devices  99.1 us (54%)
  Pallas kernels  44.7 us (25%)
  starting transfers between devices  17.2 us (9%)
  blocking collectives  14.3 us (8%)
  local copies, waits for them, and re-layouts  2.48 us (1%)
  other arithmetic  2.25 us (1%)
    all_to_all x3, waiting for transfers between devices, exchange(): return lax.all_to_all(values, axes, split_axis=0, concat_axis=0, tiled=True)  98 us
    all_to_all x3, starting transfers between devices, exchange(): return lax.all_to_all(values, axes, split_axis=0, concat_axis=0, tiled=True)  15.3 us
    all_to_all x1, blocking collectives, exchange(): return lax.all_to_all(values, axes, split_axis=0, concat_axis=0, tiled=True)  14.3 us
    pallas_call x1, Pallas kernels, spread_out(): pl.pallas_call(functools.partial(spread_kernel, slots), grid=(devices //...  8.44 us
    pallas_call x1, Pallas kernels, gather_back(): pl.pallas_call(functools.partial(gather_kernel, spread), grid=(rows_dev /...  7.14 us
    pallas_call x1, Pallas kernels, near_field(): pl.pallas_call(near_kernel, grid_spec=pltpu.PrefetchScalarGridSpec(num_sc...  6.3 us
    pallas_call x1, Pallas kernels, refine(): pl.pallas_call(functools.partial(refine_kernel, slots), in_specs=[direct,...  5.94 us
    pallas_call x1, Pallas kernels, reply(): pl.pallas_call(functools.partial(reply_kernel, slots), grid=(total // REP...  5.41 us
  transfers between devices with their start and end apart: 6, of which 4 were waited for; matrix products, arithmetic and copies ran while one was open for 1% of the time, Pallas kernels for 10%

profile of v3, /device:TPU:0, one launch (start us, length us, event | category | flops | bytes accessed | tf_op | source)
XLA Modules:
  0.0 180.9 jit_solution(17552085375302556758)
XLA Ops:
  0.6 8.4 %spread_out.1 = (s16[32,264,128]{2,1,0:T(8,128)(2,1)}, f32[8,1024]{1,0:T(8,128)}) custom-call(s32[2,1024]{1,0:T(2,128)} %bitcast.30, s32[2,1024]{1,0:T(2,128)} %bitcast.31, f32[2,1024]{1,0:T(2,128)} %bitcast.32, f32[2,1024,256]{2,1,0:T(8,128)} %basis_ref.1), custom_call_target="tpu_custom_call" | custom-call | flops 4294967296 | bytes 4194304 | tf_op jit(solution)/shard_map/spread_out/pallas_call | solution.py:181
  9.1 0.0 copy-start.5
  9.1 0.0 copy-start.7
  9.1 0.0 copy-start.1
  9.1 0.0 copy-start.2
  9.1 7.3 %all-to-all-start = ((s16[32,264,128]{2,1,0:T(8,128)(2,1)}), s16[32,264,128]{2,1,0:T(8,128)(2,1)S(1)}, u32[]{:S(2)}, u32[]{:S(2)}) async-start(s16[32,264,128]{2,1,0:T(8,128)(2,1)} %get-tuple-element.24), calls=%async_computation | async-start | bytes 4325376 | tf_op jit(solution)/shard_map/all_to_all | solution.py:599
  16.5 0.0 copy-done.5
  16.5 0.1 reshape.84
  16.6 0.0 copy-done.7
  16.6 0.1 reshape.83.ascend_ref
  16.8 1.2 gather_fusion
  17.9 0.0 copy-done.1
  18.0 0.0 copy-done.2
  18.0 0.4 rise.1.rise_ref
  18.4 48.2 %all-to-all-done.got_ref = s16[32,264,128]{2,1,0:T(8,128)(2,1)S(1)} async-done(((s16[32,264,128]{2,1,0:T(8,128)(2,1)}), s16[32,264,128]{2,1,0:T(8,128)(2,1)S(1)}, u32[]{:S(2)}, u32[]{:S(2)}) %all-to-all-start) | async-done | bytes 2162720 | tf_op jit(solution)/shard_map/all_to_all | solution.py:599
  66.6 5.1 %collect.1 = (f32[1024,256]{1,0:T(8,128)S(1)}, bf16[8,160,256]{2,1,0:T(8,128)(2,1)}, f32[32,128]{1,0:T(8,128)}) custom-call(s16[32,264,128]{2,1,0:T(8,128)(2,1)S(1)} %all-to-all-done.got_ref, bf16[2,64,512]{2,1,0:T(8,128)(2,1)S(1)} %rise.1.rise_ref, bf16[32,256]{1,0:T(8,128)(2,1)S(1)} %reshape.83.ascend_ref), custom_call_target="tpu_custom_call" | custom-call | flops 2147483648 | bytes 4194304 | tf_op jit(solution)/shard_map/collect/pallas_call | solution.py:305
  71.7 4.4 %all-to-all-start.1 = ((bf16[8,160,256]{2,1,0:T(8,128)(2,1)}), bf16[8,160,256]{2,1,0:T(8,128)(2,1)}, u32[]{:S(2)}, u32[]{:S(2)}) async-start(bf16[8,160,256]{2,1,0:T(8,128)(2,1)} %get-tuple-element.32), calls=%async_computation.1 | async-start | bytes 1310720 | tf_op jit(solution)/shard_map/all_to_all | solution.py:599
  76.1 0.0 copy-start.4
  76.1 5.9 %refine.1.first_ref = f32[1024,256]{1,0:T(8,128)S(1)} custom-call(s16[32,264,128]{2,1,0:T(8,128)(2,1)S(1)} %all-to-all-done.got_ref, f32[1024,256]{1,0:T(8,128)S(1)} %get-tuple-element.33.dual_ref, bf16[2,512,512]{2,1,0:T(8,128)(2,1)} %gram_ref.2), custom_call_target="tpu_custom_call" | custom-call | flops 2147483648 | bytes 4194304 | tf_op jit(solution)/shard_map/refine/pallas_call | solution.py:350
  82.0 0.0 copy-done.4
  82.1 6.3 %near_field.1.image_ref = f32[1024,256]{1,0:T(8,128)S(1)} custom-call(s32[2,8]{1,0:T(2,128)S(1)} %copy-done.4, bf16[2,8,512,512]{3,2,1,0:T(8,128)(2,1)} %block_ref.2, f32[1024,256]{1,0:T(8,128)S(1)} %refine.1.first_ref), custom_call_target="tpu_custom_call" | custom-call | flops 2147483648 | bytes 8388608 | tf_op jit(solution)/shard_map/near_field/pallas_call | solution.py:453
  88.4 0.0 copy-start.3
  88.4 2.3 %prepare.1 = (f32[1024,256]{1,0:T(8,128)S(1)}, bf16[1024,128]{1,0:T(8,128)(2,1)S(1)}) custom-call(f32[1024,256]{1,0:T(8,128)S(1)} %near_field.1.image_ref, bf16[2,64,512]{2,1,0:T(8,128)(2,1)} %base_ref.2, bf16[2,512,512]{2,1,0:T(8,128)(2,1)} %gram_ref.2), custom_call_target="tpu_custom_call" | custom-call | flops 536870912 | bytes 4194304 | tf_op jit(solution)/shard_map/prepare/pallas_call | solution.py:489
  90.7 2.4 %all-to-all-done.1.coeff_ref = bf16[8,160,256]{2,1,0:T(8,128)(2,1)} async-done(((bf16[8,160,256]{2,1,0:T(8,128)(2,1)}), bf16[8,160,256]{2,1,0:T(8,128)(2,1)}, u32[]{:S(2)}, u32[]{:S(2)}) %all-to-all-start.1) | async-done | bytes 655392 | tf_op jit(solution)/shard_map/all_to_all | solution.py:599
  93.2 1.4 parent_of.1.refs_6_
  94.6 0.0 collective-permute-start
  94.6 1.8 collective-permute-start.1
  96.4 0.1 collective-permute-start.2
  96.5 0.0 copy-done.3
  96.5 2.2 %far_field.1.refs_2_ = f32[2,64,256]{2,1,0:T(8,128)S(1)} custom-call(s32[2,16]{1,0:T(2,128)S(1)} %copy-done.3, bf16[8,160,256]{2,1,0:T(8,128)(2,1)} %all-to-all-done.1.coeff_ref, bf16[2,16,64,64]{3,2,1,0:T(8,128)(2,1)} %block_ref.3), custom_call_target="tpu_custom_call" | custom-call | flops 67108864 | bytes 1048576 | tf_op jit(solution)/shard_map/far_field/pallas_call | solution.py:411
  98.7 0.0 collective-permute-done.refs_7_
  98.7 0.0 collective-permute-done.1.refs_8_
  98.7 1.0 collective-permute-done.2.refs_9_
  99.7 5.4 %reply.1 = bf16[4096,256]{1,0:T(8,128)(2,1)} custom-call(f32[1024,256]{1,0:T(8,128)S(1)} %get-tuple-element.36.refs_0_, bf16[1024,128]{1,0:T(8,128)(2,1)S(1)} %get-tuple-element.37.refs_1_, f32[2,64,256]{2,1,0:T(8,128)S(1)} %far_field.1.refs_2_, bf16[4,64,64]{2,1,0:T(8,128)(2,1)} %gather_fusion, bf16[2,64,64]{2,1,0:T(8,128)(2,1)} %refs_4_.1, ...), custom_call_target="tpu_custom_call" | custom-call | flops 2147483648 | bytes 4194304 | tf_op jit(solution)/shard_map/reply/pallas_call | solution.py:528
  105.1 0.0 copy-start.6
  105.1 0.0 copy-start
  105.2 3.6 %all-to-all-start.2 = ((bf16[32,128,256]{2,1,0:T(8,128)(2,1)}), bf16[32,128,256]{2,1,0:T(8,128)(2,1)}, u32[]{:S(2)}, u32[]{:S(2)}) async-start(bf16[32,128,256]{2,1,0:T(8,128)(2,1)} %bitcast.20), calls=%async_computation.2 | async-start | bytes 4194304 | tf_op jit(solution)/shard_map/all_to_all | solution.py:599
  108.8 0.0 copy-done.6
  108.8 1.0 copy.27
  109.8 0.0 copy-done
  109.8 0.2 multiply_reduce_fusion.3
  110.0 47.4 %all-to-all-done.2 = bf16[32,128,256]{2,1,0:T(8,128)(2,1)} async-done(((bf16[32,128,256]{2,1,0:T(8,128)(2,1)}), bf16[32,128,256]{2,1,0:T(8,128)(2,1)}, u32[]{:S(2)}, u32[]{:S(2)}) %all-to-all-start.2) | async-done | bytes 2097184 | tf_op jit(solution)/shard_map/all_to_all | solution.py:599
  157.4 7.1 %gather_back.1 = (f32[1024,256]{1,0:T(8,128)S(1)}, f32[6,256]{1,0:T(8,128)S(1)}) custom-call(bf16[4096,256]{1,0:T(8,128)(2,1)} %bitcast.8.ret_ref, f32[1024,8]{1,0:T(8,128)} %bitcast.21, f32[2,1024,256]{2,1,0:T(8,128)S(1)} %copy-done, f32[3,256]{1,0:T(4,128)S(1)} %pad_maximum_fusion.mutual_ref), custom_call_target="tpu_custom_call" | custom-call | flops 4294967296 | bytes 6291456 | tf_op jit(solution)/shard_map/gather_back/pallas_call | solution.py:575
  164.6 14.3 %all_to_all.20 = f32[32,6,256]{2,1,0:T(8,128)S(1)} all-to-all(f32[32,6,256]{2,1,0:T(8,128)S(1)} %broadcast_in_dim.2), channel_id=1, replica_groups=mesh['branch'=8,'group'=4] {'branch','group'}, dimensions={0} | all-to-all | bytes 393216 | tf_op jit(solution)/shard_map/all_to_all | solution.py:599
  179.0 0.2 multiply_reduce_fusion
  179.2 0.6 pad_maximum_fusion.1
  179.8 1.1 subtract_divide_fusion
  (10 shorter events, 0.2 us)
Async XLA Ops:
  9.1 7.4 %copy-start.5 = (bf16[64,256]{1,0:T(8,128)(2,1)S(1)}, bf16[64,256]{1,0:T(8,128)(2,1)}, u32[]{:S(2)}) copy-start(bf16[64,256]{1,0:T(8,128)(2,1)} %param.25) | copy-start | bytes 98308
  9.1 7.5 %copy-start.7 = (bf16[2,64,64]{2,1,0:T(8,128)(2,1)S(1)}, bf16[2,64,64]{2,1,0:T(8,128)(2,1)}, u32[]{:S(2)}) copy-start(bf16[2,64,64]{2,1,0:T(8,128)(2,1)} %param.23) | copy-start | bytes 49156
  9.1 8.8 %copy-start.1 = (bf16[2,512,512]{2,1,0:T(8,128)(2,1)S(1)}, bf16[2,512,512]{2,1,0:T(8,128)(2,1)}, u32[]{:S(2)}) copy-start(bf16[2,512,512]{2,1,0:T(8,128)(2,1)} %gram_ref.2) | copy-start | bytes 3145732
  9.1 8.8 %copy-start.2 = (bf16[2,64,512]{2,1,0:T(8,128)(2,1)S(1)}, bf16[2,64,512]{2,1,0:T(8,128)(2,1)}, u32[]{:S(2)}) copy-start(bf16[2,64,512]{2,1,0:T(8,128)(2,1)} %base_ref.2) | copy-start | bytes 393220
  9.1 57.5 %all-to-all-start = ((s16[32,264,128]{2,1,0:T(8,128)(2,1)}), s16[32,264,128]{2,1,0:T(8,128)(2,1)S(1)}, u32[]{:S(2)}, u32[]{:S(2)}) async-start(s16[32,264,128]{2,1,0:T(8,128)(2,1)} %get-tuple-element.24), calls=%async_computation | async-start | bytes 4325376 | tf_op jit(solution)/shard_map/all_to_all | solution.py:599
  71.7 21.5 %all-to-all-start.1 = ((bf16[8,160,256]{2,1,0:T(8,128)(2,1)}), bf16[8,160,256]{2,1,0:T(8,128)(2,1)}, u32[]{:S(2)}, u32[]{:S(2)}) async-start(bf16[8,160,256]{2,1,0:T(8,128)(2,1)} %get-tuple-element.32), calls=%async_computation.1 | async-start | bytes 1310720 | tf_op jit(solution)/shard_map/all_to_all | solution.py:599
  76.1 6.0 %copy-start.4 = (s32[2,8]{1,0:T(2,128)S(1)}, s32[2,8]{1,0:T(2,128)}, u32[]{:S(2)}) copy-start(s32[2,8]{1,0:T(2,128)} %list_ref.2) | copy-start | bytes 196
  88.4 8.1 %copy-start.3 = (s32[2,16]{1,0:T(2,128)S(1)}, s32[2,16]{1,0:T(2,128)}, u32[]{:S(2)}) copy-start(s32[2,16]{1,0:T(2,128)} %list_ref.3) | copy-start | bytes 388
  94.6 4.1 %collective-permute-start = (bf16[64,256]{1,0:T(8,128)(2,1)S(1)}, bf16[64,256]{1,0:T(8,128)(2,1)S(1)}, u32[]{:S(2)}, u32[]{:S(2)}) collective-permute-start(bf16[64,256]{1,0:T(8,128)(2,1)S(1)} %parent_of.1.refs_6_), channel_id=1, source_target_pairs={{0,1},{1,0},{2,3},{3,2},{4,5},{5,4},{6,7},{7,6},{8,9},{9,8},{10,11... | collective-permute-start | bytes 98312 | tf_op jit(solution)/shard_map/ppermute | solution.py:605
  94.6 4.1 %collective-permute-start.1 = (bf16[64,256]{1,0:T(8,128)(2,1)S(1)}, bf16[64,256]{1,0:T(8,128)(2,1)S(1)}, u32[]{:S(2)}, u32[]{:S(2)}) collective-permute-start(bf16[64,256]{1,0:T(8,128)(2,1)S(1)} %parent_of.1.refs_6_), channel_id=1, source_target_pairs={{0,2},{1,3},{2,0},{3,1},{4,6},{5,7},{6,4},{7,5},{8,10},{9,11},{10,... | collective-permute-start | bytes 98312 | tf_op jit(solution)/shard_map/ppermute | solution.py:605
  96.4 3.4 %collective-permute-start.2 = (bf16[64,256]{1,0:T(8,128)(2,1)S(1)}, bf16[64,256]{1,0:T(8,128)(2,1)S(1)}, u32[]{:S(2)}, u32[]{:S(2)}) collective-permute-start(bf16[64,256]{1,0:T(8,128)(2,1)S(1)} %parent_of.1.refs_6_), channel_id=1, source_target_pairs={{0,3},{1,2},{2,1},{3,0},{4,7},{5,6},{6,5},{7,4},{8,11},{9,10},{10,... | collective-permute-start | bytes 98312 | tf_op jit(solution)/shard_map/ppermute | solution.py:605
  105.1 3.6 %copy-start.6 = (f32[8,1024]{1,0:T(8,128)S(1)}, f32[8,1024]{1,0:T(8,128)}, u32[]{:S(2)}) copy-start(f32[8,1024]{1,0:T(8,128)} %get-tuple-element.41) | copy-start | bytes 98308
  105.1 4.6 %copy-start = (f32[2,1024,256]{2,1,0:T(8,128)S(1)}, f32[2,1024,256]{2,1,0:T(8,128)}, u32[]{:S(2)}) copy-start(f32[2,1024,256]{2,1,0:T(8,128)} %basis_ref.1) | copy-start | bytes 6291460
  105.2 52.3 %all-to-all-start.2 = ((bf16[32,128,256]{2,1,0:T(8,128)(2,1)}), bf16[32,128,256]{2,1,0:T(8,128)(2,1)}, u32[]{:S(2)}, u32[]{:S(2)}) async-start(bf16[32,128,256]{2,1,0:T(8,128)(2,1)} %bitcast.20), calls=%async_computation.2 | async-start | bytes 4194304 | tf_op jit(solution)/shard_map/all_to_all | solution.py:599

commit v4 on v3

--- a/solution.py
+++ b/solution.py
@@ -662,9 +662,15 @@
     returned = exchange(replies.reshape(devices, slots, columns)).reshape(total, columns)
     pairs = [(i, j) for i in range(krylov) for j in range(i, krylov)]
     mutual = jnp.stack([jnp.sum(basis[i] * basis[j], axis=0) for i, j in pairs])
-    primal, sums = gather_back(near_by(returned), kept(place.T), basis, mutual, spread)
-    sums = jnp.sum(to_all(sums, AXES, devices), axis=0)
-    mutual = sums[krylov + 1 :]
+    mutual = sum(swaps(mutual, "group"))
+    share = -(-len(pairs) // groups)
+    mutual = jnp.pad(mutual, ((0, share * groups - len(pairs)), (0, 0)))
+    own = lax.dynamic_slice_in_dim(mutual, share * lax.axis_index("group"), share, 0)
+    primal, sums = gather_back(near_by(returned), kept(place.T), basis, own, spread)
+    everyone = to_all(sums, AXES, devices)
+    sums = jnp.sum(everyone[:, : krylov + 1], axis=0)
+    mutual = jnp.sum(everyone.reshape(branches, groups, -1, columns)[:, :, krylov + 1 :], axis=0)
+    mutual = mutual.reshape(share * groups, columns)
 
     total_rows = rows_dev * devices
     projection = sums[:krylov] / total_rows

time: 182 us -> 179 us (0.984)
  blocking collectives: 14.3 us -> 12 us
  waiting for transfers between devices: 99.1 us -> 97.1 us
  starting transfers between devices: 17.2 us -> 19.1 us
    all_to_all x3, waiting for transfers between devices: 98 us -> 93.2 us  [exchange(): return lax.all_to_all(values, axes, split_axis=0, concat_axis=0, tiled=True)]
    ppermute x3 -> x6, waiting for transfers between devices: 1.03 us -> 3.92 us  [swaps(): lax.ppermute(values, axis, [(i, i ^ k) for i in range(size)])]
    all_to_all x1, blocking collectives: 14.3 us -> 12 us  [exchange(): return lax.all_to_all(values, axes, split_axis=0, concat_axis=0, tiled=True)]
    ppermute x3 -> x6, starting transfers between devices: 1.89 us -> 3.81 us  [swaps(): lax.ppermute(values, axis, [(i, i ^ k) for i in range(size)])]
  transfers between devices with their start and end apart: 6 -> 9, of which waited for: 4 -> 5; matrix products, arithmetic and copies ran while one was open for 1% -> 2% of each run, Pallas kernels for 10% -> 10%
where the time goes in v4:
time: 179 us
  waiting for transfers between devices  97.1 us (54%)
  Pallas kernels  44.7 us (25%)
  starting transfers between devices  19.1 us (11%)
  blocking collectives  12 us (7%)
  local copies, waits for them, and re-layouts  2.49 us (1%)
  other arithmetic  2.32 us (1%)
    all_to_all x3, waiting for transfers between devices, exchange(): return lax.all_to_all(values, axes, split_axis=0, concat_axis=0, tiled=True)  93.2 us
    all_to_all x3, starting transfers between devices, exchange(): return lax.all_to_all(values, axes, split_axis=0, concat_axis=0, tiled=True)  15.3 us
    all_to_all x1, blocking collectives, exchange(): return lax.all_to_all(values, axes, split_axis=0, concat_axis=0, tiled=True)  12 us
    pallas_call x1, Pallas kernels, spread_out(): pl.pallas_call(functools.partial(spread_kernel, slots), grid=(devices //...  8.44 us
    pallas_call x1, Pallas kernels, gather_back(): pl.pallas_call(functools.partial(gather_kernel, spread), grid=(rows_dev /...  7.14 us
    pallas_call x1, Pallas kernels, near_field(): pl.pallas_call(near_kernel, grid_spec=pltpu.PrefetchScalarGridSpec(num_sc...  6.3 us
    pallas_call x1, Pallas kernels, refine(): pl.pallas_call(functools.partial(refine_kernel, slots), in_specs=[direct,...  5.94 us
    pallas_call x1, Pallas kernels, reply(): pl.pallas_call(functools.partial(reply_kernel, slots), grid=(total // REP...  5.41 us
  transfers between devices with their start and end apart: 9, of which 5 were waited for; matrix products, arithmetic and copies ran while one was open for 2% of the time, Pallas kernels for 10%

profile of v4, /device:TPU:0, one launch (start us, length us, event | category | flops | bytes accessed | tf_op | source)
XLA Modules:
  0.0 178.6 jit_solution(16858874037082589195)
XLA Ops:
  0.6 8.4 %spread_out.1 = (s16[32,264,128]{2,1,0:T(8,128)(2,1)}, f32[8,1024]{1,0:T(8,128)}) custom-call(s32[2,1024]{1,0:T(2,128)} %bitcast.35, s32[2,1024]{1,0:T(2,128)} %bitcast.36, f32[2,1024]{1,0:T(2,128)} %bitcast.37, f32[2,1024,256]{2,1,0:T(8,128)} %basis_ref.1), custom_call_target="tpu_custom_call" | custom-call | flops 4294967296 | bytes 4194304 | tf_op jit(solution)/shard_map/spread_out/pallas_call | solution.py:181
  9.1 0.0 copy-start.5
  9.1 0.0 copy-start.7
  9.1 0.0 copy-start.1
  9.1 0.0 copy-start.2
  9.1 7.3 %all-to-all-start = ((s16[32,264,128]{2,1,0:T(8,128)(2,1)}), s16[32,264,128]{2,1,0:T(8,128)(2,1)S(1)}, u32[]{:S(2)}, u32[]{:S(2)}) async-start(s16[32,264,128]{2,1,0:T(8,128)(2,1)} %get-tuple-element.24), calls=%async_computation | async-start | bytes 4325376 | tf_op jit(solution)/shard_map/all_to_all | solution.py:599
  16.5 0.0 copy-done.5
  16.5 0.1 reshape.104
  16.6 0.0 copy-done.7
  16.6 0.1 reshape.103.ascend_ref
  16.8 1.2 gather_fusion
  17.9 0.0 copy-done.1
  18.0 0.0 copy-done.2
  18.0 0.4 rise.1.rise_ref
  18.4 48.2 %all-to-all-done.got_ref = s16[32,264,128]{2,1,0:T(8,128)(2,1)S(1)} async-done(((s16[32,264,128]{2,1,0:T(8,128)(2,1)}), s16[32,264,128]{2,1,0:T(8,128)(2,1)S(1)}, u32[]{:S(2)}, u32[]{:S(2)}) %all-to-all-start) | async-done | bytes 2162720 | tf_op jit(solution)/shard_map/all_to_all | solution.py:599
  66.6 5.1 %collect.1 = (f32[1024,256]{1,0:T(8,128)S(1)}, bf16[8,160,256]{2,1,0:T(8,128)(2,1)}, f32[32,128]{1,0:T(8,128)}) custom-call(s16[32,264,128]{2,1,0:T(8,128)(2,1)S(1)} %all-to-all-done.got_ref, bf16[2,64,512]{2,1,0:T(8,128)(2,1)S(1)} %rise.1.rise_ref, bf16[32,256]{1,0:T(8,128)(2,1)S(1)} %reshape.103.ascend_ref), custom_call_target="tpu_custom_call" | custom-call | flops 2147483648 | bytes 4194304 | tf_op jit(solution)/shard_map/collect/pallas_call | solution.py:305
  71.7 4.4 %all-to-all-start.1 = ((bf16[8,160,256]{2,1,0:T(8,128)(2,1)}), bf16[8,160,256]{2,1,0:T(8,128)(2,1)}, u32[]{:S(2)}, u32[]{:S(2)}) async-start(bf16[8,160,256]{2,1,0:T(8,128)(2,1)} %get-tuple-element.32), calls=%async_computation.1 | async-start | bytes 1310720 | tf_op jit(solution)/shard_map/all_to_all | solution.py:599
  76.1 0.0 copy-start.4
  76.1 5.9 %refine.1.first_ref = f32[1024,256]{1,0:T(8,128)S(1)} custom-call(s16[32,264,128]{2,1,0:T(8,128)(2,1)S(1)} %all-to-all-done.got_ref, f32[1024,256]{1,0:T(8,128)S(1)} %get-tuple-element.33.dual_ref, bf16[2,512,512]{2,1,0:T(8,128)(2,1)} %gram_ref.2), custom_call_target="tpu_custom_call" | custom-call | flops 2147483648 | bytes 4194304 | tf_op jit(solution)/shard_map/refine/pallas_call | solution.py:350
  82.0 0.0 copy-done.4
  82.1 6.3 %near_field.1.image_ref = f32[1024,256]{1,0:T(8,128)S(1)} custom-call(s32[2,8]{1,0:T(2,128)S(1)} %copy-done.4, bf16[2,8,512,512]{3,2,1,0:T(8,128)(2,1)} %block_ref.2, f32[1024,256]{1,0:T(8,128)S(1)} %refine.1.first_ref), custom_call_target="tpu_custom_call" | custom-call | flops 2147483648 | bytes 8388608 | tf_op jit(solution)/shard_map/near_field/pallas_call | solution.py:453
  88.4 0.0 copy-start.3
  88.4 2.3 %prepare.1 = (f32[1024,256]{1,0:T(8,128)S(1)}, bf16[1024,128]{1,0:T(8,128)(2,1)S(1)}) custom-call(f32[1024,256]{1,0:T(8,128)S(1)} %near_field.1.image_ref, bf16[2,64,512]{2,1,0:T(8,128)(2,1)} %base_ref.2, bf16[2,512,512]{2,1,0:T(8,128)(2,1)} %gram_ref.2), custom_call_target="tpu_custom_call" | custom-call | flops 536870912 | bytes 4194304 | tf_op jit(solution)/shard_map/prepare/pallas_call | solution.py:489
  90.7 2.4 %all-to-all-done.1.coeff_ref = bf16[8,160,256]{2,1,0:T(8,128)(2,1)} async-done(((bf16[8,160,256]{2,1,0:T(8,128)(2,1)}), bf16[8,160,256]{2,1,0:T(8,128)(2,1)}, u32[]{:S(2)}, u32[]{:S(2)}) %all-to-all-start.1) | async-done | bytes 655392 | tf_op jit(solution)/shard_map/all_to_all | solution.py:599
  93.2 1.4 parent_of.1.refs_6_
  94.6 0.0 collective-permute-start
  94.6 1.8 collective-permute-start.1
  96.4 0.1 collective-permute-start.2
  96.5 0.0 copy-done.3
  96.5 2.2 %far_field.1.refs_2_ = f32[2,64,256]{2,1,0:T(8,128)S(1)} custom-call(s32[2,16]{1,0:T(2,128)S(1)} %copy-done.3, bf16[8,160,256]{2,1,0:T(8,128)(2,1)} %all-to-all-done.1.coeff_ref, bf16[2,16,64,64]{3,2,1,0:T(8,128)(2,1)} %block_ref.3), custom_call_target="tpu_custom_call" | custom-call | flops 67108864 | bytes 1048576 | tf_op jit(solution)/shard_map/far_field/pallas_call | solution.py:411
  98.7 0.0 collective-permute-done.refs_7_
  98.7 0.0 collective-permute-done.1.refs_8_
  98.7 1.0 collective-permute-done.2.refs_9_
  99.7 5.4 %reply.1 = bf16[4096,256]{1,0:T(8,128)(2,1)} custom-call(f32[1024,256]{1,0:T(8,128)S(1)} %get-tuple-element.36.refs_0_, bf16[1024,128]{1,0:T(8,128)(2,1)S(1)} %get-tuple-element.37.refs_1_, f32[2,64,256]{2,1,0:T(8,128)S(1)} %far_field.1.refs_2_, bf16[4,64,64]{2,1,0:T(8,128)(2,1)} %gather_fusion, bf16[2,64,64]{2,1,0:T(8,128)(2,1)} %refs_4_.1, ...), custom_call_target="tpu_custom_call" | custom-call | flops 2147483648 | bytes 4194304 | tf_op jit(solution)/shard_map/reply/pallas_call | solution.py:528
  105.1 0.0 copy-start
  105.1 3.6 %all-to-all-start.2 = ((bf16[32,128,256]{2,1,0:T(8,128)(2,1)}), bf16[32,128,256]{2,1,0:T(8,128)(2,1)}, u32[]{:S(2)}, u32[]{:S(2)}) async-start(bf16[32,128,256]{2,1,0:T(8,128)(2,1)} %bitcast.21), calls=%async_computation.2 | async-start | bytes 4194304 | tf_op jit(solution)/shard_map/all_to_all | solution.py:599
  108.8 0.0 copy-done
  108.8 0.0 copy-start.6
  108.8 0.2 multiply_reduce_fusion.3
  109.0 0.1 collective-permute-start.3
  109.1 1.7 collective-permute-start.4
  110.8 0.2 collective-permute-start.5
  111.0 0.0 copy-done.6
  111.0 1.0 copy.27
  112.0 0.0 collective-permute-done.3
  112.0 2.9 %collective-permute-done.4 = f32[3,256]{1,0:T(4,128)S(1)} collective-permute-done((f32[3,256]{1,0:T(4,128)S(1)}, f32[3,256]{1,0:T(4,128)S(1)}, u32[]{:S(2)}, u32[]{:S(2)}) %collective-permute-start.4) | collective-permute-done | bytes 3104 | tf_op jit(solution)/shard_map/ppermute | solution.py:605
  114.9 0.0 collective-permute-done.5
  114.9 42.5 %all-to-all-done.2 = bf16[32,128,256]{2,1,0:T(8,128)(2,1)} async-done(((bf16[32,128,256]{2,1,0:T(8,128)(2,1)}), bf16[32,128,256]{2,1,0:T(8,128)(2,1)}, u32[]{:S(2)}, u32[]{:S(2)}) %all-to-all-start.2) | async-done | bytes 2097184 | tf_op jit(solution)/shard_map/all_to_all | solution.py:599
  157.4 7.1 %gather_back.1 = (f32[1024,256]{1,0:T(8,128)S(1)}, f32[4,256]{1,0:T(4,128)S(1)}) custom-call(bf16[4096,256]{1,0:T(8,128)(2,1)} %bitcast.8.ret_ref, f32[1024,8]{1,0:T(8,128)} %bitcast.23, f32[2,1024,256]{2,1,0:T(8,128)S(1)} %copy-done, f32[1,256]{1,0:T(1,128)S(1)} %pad_dynamic-slice_fusion.mutual_ref), custom_call_target="tpu_custom_call" | custom-call | flops 4294967296 | bytes 6291456 | tf_op jit(solution)/shard_map/gather_back/pallas_call | solution.py:575
  164.6 12.0 %all_to_all.20 = f32[32,4,256]{2,1,0:T(4,128)S(1)} all-to-all(f32[32,4,256]{2,1,0:T(4,128)S(1)} %broadcast_in_dim.2), channel_id=1, replica_groups=mesh['branch'=8,'group'=4] {'branch','group'}, dimensions={0} | all-to-all | bytes 262144 | tf_op jit(solution)/shard_map/all_to_all | solution.py:599
  176.6 0.1 slice_reduce_fusion.1
  176.7 0.2 multiply_reduce_fusion
  176.9 0.6 pad_maximum_fusion.1
  177.5 1.1 subtract_divide_fusion
  (12 shorter events, 0.2 us)
Async XLA Ops:
  9.1 7.4 %copy-start.5 = (bf16[64,256]{1,0:T(8,128)(2,1)S(1)}, bf16[64,256]{1,0:T(8,128)(2,1)}, u32[]{:S(2)}) copy-start(bf16[64,256]{1,0:T(8,128)(2,1)} %param.25) | copy-start | bytes 98308
  9.1 7.5 %copy-start.7 = (bf16[2,64,64]{2,1,0:T(8,128)(2,1)S(1)}, bf16[2,64,64]{2,1,0:T(8,128)(2,1)}, u32[]{:S(2)}) copy-start(bf16[2,64,64]{2,1,0:T(8,128)(2,1)} %param.23) | copy-start | bytes 49156
  9.1 8.8 %copy-start.1 = (bf16[2,512,512]{2,1,0:T(8,128)(2,1)S(1)}, bf16[2,512,512]{2,1,0:T(8,128)(2,1)}, u32[]{:S(2)}) copy-start(bf16[2,512,512]{2,1,0:T(8,128)(2,1)} %gram_ref.2) | copy-start | bytes 3145732
  9.1 8.8 %copy-start.2 = (bf16[2,64,512]{2,1,0:T(8,128)(2,1)S(1)}, bf16[2,64,512]{2,1,0:T(8,128)(2,1)}, u32[]{:S(2)}) copy-start(bf16[2,64,512]{2,1,0:T(8,128)(2,1)} %base_ref.2) | copy-start | bytes 393220
  9.1 57.5 %all-to-all-start = ((s16[32,264,128]{2,1,0:T(8,128)(2,1)}), s16[32,264,128]{2,1,0:T(8,128)(2,1)S(1)}, u32[]{:S(2)}, u32[]{:S(2)}) async-start(s16[32,264,128]{2,1,0:T(8,128)(2,1)} %get-tuple-element.24), calls=%async_computation | async-start | bytes 4325376 | tf_op jit(solution)/shard_map/all_to_all | solution.py:599
  71.7 21.5 %all-to-all-start.1 = ((bf16[8,160,256]{2,1,0:T(8,128)(2,1)}), bf16[8,160,256]{2,1,0:T(8,128)(2,1)}, u32[]{:S(2)}, u32[]{:S(2)}) async-start(bf16[8,160,256]{2,1,0:T(8,128)(2,1)} %get-tuple-element.32), calls=%async_computation.1 | async-start | bytes 1310720 | tf_op jit(solution)/shard_map/all_to_all | solution.py:599
  76.1 6.0 %copy-start.4 = (s32[2,8]{1,0:T(2,128)S(1)}, s32[2,8]{1,0:T(2,128)}, u32[]{:S(2)}) copy-start(s32[2,8]{1,0:T(2,128)} %list_ref.2) | copy-start | bytes 196
  88.4 8.1 %copy-start.3 = (s32[2,16]{1,0:T(2,128)S(1)}, s32[2,16]{1,0:T(2,128)}, u32[]{:S(2)}) copy-start(s32[2,16]{1,0:T(2,128)} %list_ref.3) | copy-start | bytes 388
  94.6 4.1 %collective-permute-start = (bf16[64,256]{1,0:T(8,128)(2,1)S(1)}, bf16[64,256]{1,0:T(8,128)(2,1)S(1)}, u32[]{:S(2)}, u32[]{:S(2)}) collective-permute-start(bf16[64,256]{1,0:T(8,128)(2,1)S(1)} %parent_of.1.refs_6_), channel_id=1, source_target_pairs={{0,1},{1,0},{2,3},{3,2},{4,5},{5,4},{6,7},{7,6},{8,9},{9,8},{10,11... | collective-permute-start | bytes 98312 | tf_op jit(solution)/shard_map/ppermute | solution.py:605
  94.6 4.1 %collective-permute-start.1 = (bf16[64,256]{1,0:T(8,128)(2,1)S(1)}, bf16[64,256]{1,0:T(8,128)(2,1)S(1)}, u32[]{:S(2)}, u32[]{:S(2)}) collective-permute-start(bf16[64,256]{1,0:T(8,128)(2,1)S(1)} %parent_of.1.refs_6_), channel_id=1, source_target_pairs={{0,2},{1,3},{2,0},{3,1},{4,6},{5,7},{6,4},{7,5},{8,10},{9,11},{10,... | collective-permute-start | bytes 98312 | tf_op jit(solution)/shard_map/ppermute | solution.py:605
  96.4 3.4 %collective-permute-start.2 = (bf16[64,256]{1,0:T(8,128)(2,1)S(1)}, bf16[64,256]{1,0:T(8,128)(2,1)S(1)}, u32[]{:S(2)}, u32[]{:S(2)}) collective-permute-start(bf16[64,256]{1,0:T(8,128)(2,1)S(1)} %parent_of.1.refs_6_), channel_id=1, source_target_pairs={{0,3},{1,2},{2,1},{3,0},{4,7},{5,6},{6,5},{7,4},{8,11},{9,10},{10,... | collective-permute-start | bytes 98312 | tf_op jit(solution)/shard_map/ppermute | solution.py:605
  105.1 3.6 %copy-start = (f32[2,1024,256]{2,1,0:T(8,128)S(1)}, f32[2,1024,256]{2,1,0:T(8,128)}, u32[]{:S(2)}) copy-start(f32[2,1024,256]{2,1,0:T(8,128)} %basis_ref.1) | copy-start | bytes 6291460
  105.1 52.3 %all-to-all-start.2 = ((bf16[32,128,256]{2,1,0:T(8,128)(2,1)}), bf16[32,128,256]{2,1,0:T(8,128)(2,1)}, u32[]{:S(2)}, u32[]{:S(2)}) async-start(bf16[32,128,256]{2,1,0:T(8,128)(2,1)} %bitcast.21), calls=%async_computation.2 | async-start | bytes 4194304 | tf_op jit(solution)/shard_map/all_to_all | solution.py:599
  108.8 2.2 %copy-start.6 = (f32[8,1024]{1,0:T(8,128)S(1)}, f32[8,1024]{1,0:T(8,128)}, u32[]{:S(2)}) copy-start(f32[8,1024]{1,0:T(8,128)} %get-tuple-element.41) | copy-start | bytes 98308
  109.0 2.9 %collective-permute-start.3 = (f32[3,256]{1,0:T(4,128)S(1)}, f32[3,256]{1,0:T(4,128)S(1)}, u32[]{:S(2)}, u32[]{:S(2)}) collective-permute-start(f32[3,256]{1,0:T(4,128)S(1)} %pad_maximum_fusion), channel_id=1, source_target_pairs={{0,1},{1,0},{2,3},{3,2},{4,5},{5,4},{6,7},{7,6},{8,9},{9,8},{10,11... | collective-permute-start | bytes 9224 | tf_op jit(solution)/shard_map/ppermute | solution.py:605
  109.1 5.7 %collective-permute-start.4 = (f32[3,256]{1,0:T(4,128)S(1)}, f32[3,256]{1,0:T(4,128)S(1)}, u32[]{:S(2)}, u32[]{:S(2)}) collective-permute-start(f32[3,256]{1,0:T(4,128)S(1)} %pad_maximum_fusion), channel_id=1, source_target_pairs={{0,2},{1,3},{2,0},{3,1},{4,6},{5,7},{6,4},{7,5},{8,10},{9,11},{10,... | collective-permute-start | bytes 9224 | tf_op jit(solution)/shard_map/ppermute | solution.py:605
  110.8 4.0 %collective-permute-start.5 = (f32[3,256]{1,0:T(4,128)S(1)}, f32[3,256]{1,0:T(4,128)S(1)}, u32[]{:S(2)}, u32[]{:S(2)}) collective-permute-start(f32[3,256]{1,0:T(4,128)S(1)} %pad_maximum_fusion), channel_id=1, source_target_pairs={{0,3},{1,2},{2,1},{3,0},{4,7},{5,6},{6,5},{7,4},{8,11},{9,10},{10,... | collective-permute-start | bytes 9224 | tf_op jit(solution)/shard_map/ppermute | solution.py:605

commit v5 on v4

--- a/solution.py
+++ b/solution.py
@@ -15,7 +15,8 @@
 LOG2 = 0.6931471805599453
 SPREAD_BLOCK = 1024
 COLLECT_BLOCK = 512
-REPLY_BLOCK = 1024
+REPLY_BLOCK = 512
+GATHER_BLOCK = 256
 LANES = 128
 
 
@@ -497,96 +498,116 @@
 
 def reply_kernel(slots, *refs):
     dual_ref, lift_ref, far_ref, top_ref, descend_ref, rows_ref = refs[:6]
-    parents, (out_ref, field_ref, low_ref, pick_ref) = refs[6:-4], refs[-4:]
-    step = pl.program_id(0)
-
-    @pl.when(step == 0)
-    def _():
-        leaves, rank = far_ref.shape[:2]
-        field = dot(top_ref[0], parents[0][...])
-        for k in range(1, len(parents)):
-            field = field + dot(top_ref[k], parents[k][...])
-        field = field.astype(LOW)
-        for l in range(leaves):
-            descent = far_ref[l] + dot(descend_ref[l], field)
-            field_ref[l * rank : (l + 1) * rank, :] = descent.astype(LOW)
-        low_ref[...] = (dual_ref[...] + dot(lift_ref[...], field_ref[...])).astype(LOW)
-
+    parents, rest = refs[6:-7], refs[-7:]
+    out_hbm, field_ref, low_ref, pick_a, pick_b, ready_ref, sems = rest
+    picks = (pick_a, pick_b)
     owners = REPLY_BLOCK // slots
+    blocks = ready_ref.shape[0] // REPLY_BLOCK
     ids = lax.broadcasted_iota(jnp.int32, (slots, low_ref.shape[0]), 1).astype(F32)
-    for j in range(owners):
-        row = column(rows_ref[pl.ds(step * owners + j, 1), :][:, :slots])
-        pick_ref[j * slots : (j + 1) * slots, :] = jnp.where(ids == row, 1.0, 0.0).astype(LOW)
-    out_ref[...] = dot(pick_ref[...], low_ref[...]).astype(LOW)
+
+    def build(block):
+        for j in range(owners):
+            source = block * owners + j
+            row = column(rows_ref[source : source + 1, :][:, :slots])
+            pick = jnp.where(ids == row, 1.0, 0.0).astype(LOW)
+            picks[block % 2][j * slots : (j + 1) * slots, :] = pick
+
+    build(0)
+    leaves, rank = far_ref.shape[:2]
+    field = dot(top_ref[0], parents[0][...])
+    for k in range(1, len(parents)):
+        field = field + dot(top_ref[k], parents[k][...])
+    field = field.astype(LOW)
+    for l in range(leaves):
+        descent = far_ref[l] + dot(descend_ref[l], field)
+        field_ref[l * rank : (l + 1) * rank, :] = descent.astype(LOW)
+    low_ref[...] = (dual_ref[...] + dot(lift_ref[...], field_ref[...])).astype(LOW)
+    copies = []
+    for block in range(blocks):
+        if block + 1 < blocks:
+            build(block + 1)
+        at = pl.ds(block * REPLY_BLOCK, REPLY_BLOCK)
+        ready_ref[at, :] = dot(picks[block % 2][...], low_ref[...]).astype(LOW)
+        copies.append(pltpu.make_async_copy(ready_ref.at[at], out_hbm.at[at], sems.at[block]))
+        copies[-1].start()
+    for copy in copies:
+        copy.wait()
 
 
 def reply(dual, lift, far, top, parents, descend, rows, slots):
     rows_dev, width = dual.shape
     total = rows.shape[0] * slots
-    args = (far, top, descend, rows, *parents)
+    args = (dual, lift, far, top, descend, rows, *parents)
     direct = pl.BlockSpec(memory_space=pltpu.VMEM)
     return pl.pallas_call(
         functools.partial(reply_kernel, slots),
-        grid=(total // REPLY_BLOCK,),
-        in_specs=[direct, direct] + [whole(a.shape) for a in args[:4]] + [direct] * len(parents),
-        out_specs=pl.BlockSpec((REPLY_BLOCK, width), lambda i: (i, 0)),
+        in_specs=[direct] * len(args),
+        out_specs=pl.BlockSpec(memory_space=pltpu.HBM),
         out_shape=in_hbm((total, width), LOW),
         scratch_shapes=[
             pltpu.VMEM((lift.shape[1], width), LOW),
             pltpu.VMEM((rows_dev, width), LOW),
             pltpu.VMEM((REPLY_BLOCK, rows_dev), LOW),
+            pltpu.VMEM((REPLY_BLOCK, rows_dev), LOW),
+            pltpu.VMEM((total, width), LOW),
+            pltpu.SemaphoreType.DMA((total // REPLY_BLOCK,)),
         ],
-        compiler_params=params(("arbitrary",), 16),
+        compiler_params=params(mib=16),
         cost_estimate=cost(2 * total * rows_dev * width, 4 << 20),
         name="reply",
-    )(dual, lift, *args)
-
-
-def gather_kernel(spread, ret_ref, place_ref, basis_ref, mutual_ref, image_ref, sums_ref):
-    step = pl.program_id(0)
-    rows = place_ref.shape[0]
-    total = ret_ref.shape[0]
-    ids = lax.broadcasted_iota(jnp.int32, (rows, total), 1).astype(F32)
-    image = jnp.zeros(image_ref.shape, F32)
-    for s in range(spread):
-        pick = jnp.where(ids == place_ref[:, s : s + 1], 1.0, 0.0).astype(LOW)
-        image = image + place_ref[:, spread + s : spread + s + 1] * dot(pick, ret_ref[...])
-    image_ref[...] = image
+    )(*args)
+
+
+def gather_kernel(spread, ret_ref, place_ref, basis_ref, mutual_ref, image_ref, sums_ref, pick_a, pick_b):
+    picks = (pick_a, pick_b)
+    total, width = ret_ref.shape
     krylov = basis_ref.shape[0]
-    parts = [jnp.sum(basis_ref[k] * image, axis=0, keepdims=True) for k in range(krylov)]
-    parts.append(jnp.sum(image * image, axis=0, keepdims=True))
-    added = jnp.concatenate(parts, axis=0)
-
-    @pl.when(step == 0)
-    def _():
-        sums_ref[: krylov + 1, :] = added
-        sums_ref[krylov + 1 :, :] = mutual_ref[...]
-
-    @pl.when(step > 0)
-    def _():
-        sums_ref[: krylov + 1, :] += added
+    blocks = image_ref.shape[0] // GATHER_BLOCK
+    ids = lax.broadcasted_iota(jnp.int32, (GATHER_BLOCK, total), 1).astype(F32)
+
+    def build(block):
+        at = slice(block * GATHER_BLOCK, (block + 1) * GATHER_BLOCK)
+        for s in range(spread):
+            pick = jnp.where(ids == place_ref[at, s : s + 1], 1.0, 0.0).astype(LOW)
+            picks[block % 2][s * GATHER_BLOCK : (s + 1) * GATHER_BLOCK, :] = pick
+
+    build(0)
+    sums = [jnp.zeros((1, width), F32) for _ in range(krylov + 1)]
+    for block in range(blocks):
+        if block + 1 < blocks:
+            build(block + 1)
+        at = slice(block * GATHER_BLOCK, (block + 1) * GATHER_BLOCK)
+        picked = dot(picks[block % 2][...], ret_ref[...])
+        image = jnp.zeros((GATHER_BLOCK, width), F32)
+        for s in range(spread):
+            weight = place_ref[at, spread + s : spread + s + 1]
+            image = image + weight * picked[s * GATHER_BLOCK : (s + 1) * GATHER_BLOCK, :]
+        image_ref[at, :] = image
+        for k in range(krylov):
+            sums[k] = sums[k] + jnp.sum(basis_ref[k, at, :] * image, axis=0, keepdims=True)
+        sums[krylov] = sums[krylov] + jnp.sum(image * image, axis=0, keepdims=True)
+    sums_ref[: krylov + 1, :] = jnp.concatenate(sums, axis=0)
+    sums_ref[krylov + 1 :, :] = mutual_ref[...]
 
 
 def gather_back(ret, place_col, basis, mutual, spread):
-    lines = basis.shape[0] + 1 + mutual.shape[0]
     total, width = ret.shape
     krylov, rows_dev = basis.shape[:2]
-    rows = 256
+    lines = krylov + 1 + mutual.shape[0]
+    direct = pl.BlockSpec(memory_space=pltpu.VMEM)
     return pl.pallas_call(
         functools.partial(gather_kernel, spread),
-        grid=(rows_dev // rows,),
-        in_specs=[
-            pl.BlockSpec(memory_space=pltpu.VMEM),
-            pl.BlockSpec((rows, place_col.shape[1]), lambda i: (i, 0)),
-            pl.BlockSpec((krylov, rows, width), lambda i: (0, i, 0)),
-            whole(mutual.shape),
-        ],
-        out_specs=(pl.BlockSpec((rows, width), lambda i: (i, 0)), whole((lines, width))),
+        in_specs=[direct] * 4,
+        out_specs=[direct] * 2,
         out_shape=(
             jax.ShapeDtypeStruct((rows_dev, width), F32),
             jax.ShapeDtypeStruct((lines, width), F32),
         ),
-        compiler_params=params(("arbitrary",)),
+        scratch_shapes=[
+            pltpu.VMEM((spread * GATHER_BLOCK, total), LOW),
+            pltpu.VMEM((spread * GATHER_BLOCK, total), LOW),
+        ],
+        compiler_params=params(),
         cost_estimate=cost(2 * spread * total * rows_dev * width, 6 << 20),
         name="gather_back",
     )(ret, place_col, basis, mutual)

time: 179 us -> 178 us (level)
  no operation moved by 1% of the time
where the time goes in v5:
time: 178 us; the launch traced here: 177 us
  waiting for transfers between devices  96.9 us (54%)
  Pallas kernels  43.3 us (24%)
  starting transfers between devices  19.4 us (11%)
  blocking collectives  12 us (7%)
  local copies, waits for them, and re-layouts  2.49 us (1%)
  other arithmetic  2.32 us (1%)
    all_to_all x3, waiting for transfers between devices, exchange(): return lax.all_to_all(values, axes, split_axis=0, concat_axis=0, tiled=True)  93.2 us
    all_to_all x3, starting transfers between devices, exchange(): return lax.all_to_all(values, axes, split_axis=0, concat_axis=0, tiled=True)  15.6 us
    all_to_all x1, blocking collectives, exchange(): return lax.all_to_all(values, axes, split_axis=0, concat_axis=0, tiled=True)  12 us
    pallas_call x1, Pallas kernels, spread_out(): pl.pallas_call(functools.partial(spread_kernel, slots), grid=(devices //...  8.44 us
    pallas_call x1, Pallas kernels, gather_back(): pl.pallas_call(functools.partial(gather_kernel, spread), in_specs=[direct...  6.45 us
    pallas_call x1, Pallas kernels, near_field(): pl.pallas_call(near_kernel, grid_spec=pltpu.PrefetchScalarGridSpec(num_sc...  6.3 us
    pallas_call x1, Pallas kernels, refine(): pl.pallas_call(functools.partial(refine_kernel, slots), in_specs=[direct,...  5.94 us
    pallas_call x1, Pallas kernels, collect(): pl.pallas_call(functools.partial(collect_kernel, slots), in_specs=[direct...  5.11 us
  transfers between devices with their start and end apart: 9, of which 5 were waited for; matrix products, arithmetic and copies ran while one was open for 2% of the time, Pallas kernels for 10%

profile of v5, /device:TPU:0, one launch (start us, length us, event | category | flops | bytes accessed | tf_op | source)
XLA Modules:
  0.0 177.2 jit_solution(9482533204298154008)
XLA Ops:
  0.6 8.4 %spread_out.1 = (s16[32,264,128]{2,1,0:T(8,128)(2,1)}, f32[8,1024]{1,0:T(8,128)}) custom-call(s32[2,1024]{1,0:T(2,128)} %bitcast.35, s32[2,1024]{1,0:T(2,128)} %bitcast.36, f32[2,1024]{1,0:T(2,128)} %bitcast.37, f32[2,1024,256]{2,1,0:T(8,128)} %basis_ref.1), custom_call_target="tpu_custom_call" | custom-call | flops 4294967296 | bytes 4194304 | tf_op jit(solution)/shard_map/spread_out/pallas_call | solution.py:182
  9.1 0.0 copy-start.5
  9.1 0.0 copy-start.7
  9.1 0.0 copy-start.1
  9.1 0.0 copy-start.2
  9.1 7.3 %all-to-all-start = ((s16[32,264,128]{2,1,0:T(8,128)(2,1)}), s16[32,264,128]{2,1,0:T(8,128)(2,1)S(1)}, u32[]{:S(2)}, u32[]{:S(2)}) async-start(s16[32,264,128]{2,1,0:T(8,128)(2,1)} %get-tuple-element.24), calls=%async_computation | async-start | bytes 4325376 | tf_op jit(solution)/shard_map/all_to_all | solution.py:620
  16.5 0.0 copy-done.5
  16.5 0.1 reshape.104
  16.6 0.0 copy-done.7
  16.6 0.1 reshape.103.ascend_ref
  16.8 1.2 gather_fusion
  17.9 0.0 copy-done.1
  18.0 0.0 copy-done.2
  18.0 0.4 rise.1.rise_ref
  18.4 48.2 %all-to-all-done.got_ref = s16[32,264,128]{2,1,0:T(8,128)(2,1)S(1)} async-done(((s16[32,264,128]{2,1,0:T(8,128)(2,1)}), s16[32,264,128]{2,1,0:T(8,128)(2,1)S(1)}, u32[]{:S(2)}, u32[]{:S(2)}) %all-to-all-start) | async-done | bytes 2162720 | tf_op jit(solution)/shard_map/all_to_all | solution.py:620
  66.6 5.1 %collect.1 = (f32[1024,256]{1,0:T(8,128)S(1)}, bf16[8,160,256]{2,1,0:T(8,128)(2,1)}, f32[32,128]{1,0:T(8,128)}) custom-call(s16[32,264,128]{2,1,0:T(8,128)(2,1)S(1)} %all-to-all-done.got_ref, bf16[2,64,512]{2,1,0:T(8,128)(2,1)S(1)} %rise.1.rise_ref, bf16[32,256]{1,0:T(8,128)(2,1)S(1)} %reshape.103.ascend_ref), custom_call_target="tpu_custom_call" | custom-call | flops 2147483648 | bytes 4194304 | tf_op jit(solution)/shard_map/collect/pallas_call | solution.py:306
  71.7 4.4 %all-to-all-start.1 = ((bf16[8,160,256]{2,1,0:T(8,128)(2,1)}), bf16[8,160,256]{2,1,0:T(8,128)(2,1)}, u32[]{:S(2)}, u32[]{:S(2)}) async-start(bf16[8,160,256]{2,1,0:T(8,128)(2,1)} %get-tuple-element.32), calls=%async_computation.1 | async-start | bytes 1310720 | tf_op jit(solution)/shard_map/all_to_all | solution.py:620
  76.1 0.0 copy-start.4
  76.1 5.9 %refine.1.first_ref = f32[1024,256]{1,0:T(8,128)S(1)} custom-call(s16[32,264,128]{2,1,0:T(8,128)(2,1)S(1)} %all-to-all-done.got_ref, f32[1024,256]{1,0:T(8,128)S(1)} %get-tuple-element.33.dual_ref, bf16[2,512,512]{2,1,0:T(8,128)(2,1)} %gram_ref.2), custom_call_target="tpu_custom_call" | custom-call | flops 2147483648 | bytes 4194304 | tf_op jit(solution)/shard_map/refine/pallas_call | solution.py:351
  82.0 0.0 copy-done.4
  82.1 6.3 %near_field.1.image_ref = f32[1024,256]{1,0:T(8,128)S(1)} custom-call(s32[2,8]{1,0:T(2,128)S(1)} %copy-done.4, bf16[2,8,512,512]{3,2,1,0:T(8,128)(2,1)} %block_ref.2, f32[1024,256]{1,0:T(8,128)S(1)} %refine.1.first_ref), custom_call_target="tpu_custom_call" | custom-call | flops 2147483648 | bytes 8388608 | tf_op jit(solution)/shard_map/near_field/pallas_call | solution.py:454
  88.4 0.0 copy-start.3
  88.4 2.3 %prepare.1 = (f32[1024,256]{1,0:T(8,128)S(1)}, bf16[1024,128]{1,0:T(8,128)(2,1)S(1)}) custom-call(f32[1024,256]{1,0:T(8,128)S(1)} %near_field.1.image_ref, bf16[2,64,512]{2,1,0:T(8,128)(2,1)} %base_ref.2, bf16[2,512,512]{2,1,0:T(8,128)(2,1)} %gram_ref.2), custom_call_target="tpu_custom_call" | custom-call | flops 536870912 | bytes 4194304 | tf_op jit(solution)/shard_map/prepare/pallas_call | solution.py:490
  90.7 2.4 %all-to-all-done.1.coeff_ref = bf16[8,160,256]{2,1,0:T(8,128)(2,1)} async-done(((bf16[8,160,256]{2,1,0:T(8,128)(2,1)}), bf16[8,160,256]{2,1,0:T(8,128)(2,1)}, u32[]{:S(2)}, u32[]{:S(2)}) %all-to-all-start.1) | async-done | bytes 655392 | tf_op jit(solution)/shard_map/all_to_all | solution.py:620
  93.2 1.4 parent_of.1.refs_6_
  94.6 0.0 collective-permute-start
  94.6 1.8 collective-permute-start.1
  96.4 0.1 collective-permute-start.2
  96.5 0.0 copy-done.3
  96.5 2.2 %far_field.1.refs_2_ = f32[2,64,256]{2,1,0:T(8,128)S(1)} custom-call(s32[2,16]{1,0:T(2,128)S(1)} %copy-done.3, bf16[8,160,256]{2,1,0:T(8,128)(2,1)} %all-to-all-done.1.coeff_ref, bf16[2,16,64,64]{3,2,1,0:T(8,128)(2,1)} %block_ref.3), custom_call_target="tpu_custom_call" | custom-call | flops 67108864 | bytes 1048576 | tf_op jit(solution)/shard_map/far_field/pallas_call | solution.py:412
  98.7 0.0 collective-permute-done.refs_7_
  98.7 0.0 collective-permute-done.1.refs_8_
  98.7 1.0 collective-permute-done.2.refs_9_
  99.7 4.7 %reply.1 = bf16[4096,256]{1,0:T(8,128)(2,1)} custom-call(f32[1024,256]{1,0:T(8,128)S(1)} %get-tuple-element.36.refs_0_, bf16[1024,128]{1,0:T(8,128)(2,1)S(1)} %get-tuple-element.37.refs_1_, f32[2,64,256]{2,1,0:T(8,128)S(1)} %far_field.1.refs_2_, bf16[4,64,64]{2,1,0:T(8,128)(2,1)} %gather_fusion, bf16[2,64,64]{2,1,0:T(8,128)(2,1)} %refs_4_.1, ...), custom_call_target="tpu_custom_call" | custom-call | flops 2147483648 | bytes 4194304 | tf_op jit(solution)/shard_map/reply/pallas_call | solution.py:542
  104.4 0.0 copy-start
  104.4 3.8 %all-to-all-start.2 = ((bf16[32,128,256]{2,1,0:T(8,128)(2,1)}), bf16[32,128,256]{2,1,0:T(8,128)(2,1)}, u32[]{:S(2)}, u32[]{:S(2)}) async-start(bf16[32,128,256]{2,1,0:T(8,128)(2,1)} %bitcast.21), calls=%async_computation.2 | async-start | bytes 4194304 | tf_op jit(solution)/shard_map/all_to_all | solution.py:620
  108.3 0.0 copy-done
  108.3 0.0 copy-start.6
  108.3 0.2 multiply_reduce_fusion.3
  108.6 0.1 collective-permute-start.3
  108.6 1.5 collective-permute-start.4
  110.1 0.4 collective-permute-start.5
  110.5 0.0 copy-done.6
  110.5 1.0 copy.27
  111.5 0.0 collective-permute-done.3
  111.5 2.7 %collective-permute-done.4 = f32[3,256]{1,0:T(4,128)S(1)} collective-permute-done((f32[3,256]{1,0:T(4,128)S(1)}, f32[3,256]{1,0:T(4,128)S(1)}, u32[]{:S(2)}, u32[]{:S(2)}) %collective-permute-start.4) | collective-permute-done | bytes 3104 | tf_op jit(solution)/shard_map/ppermute | solution.py:626
  114.2 0.0 collective-permute-done.5
  114.2 42.5 %all-to-all-done.2 = bf16[32,128,256]{2,1,0:T(8,128)(2,1)} async-done(((bf16[32,128,256]{2,1,0:T(8,128)(2,1)}), bf16[32,128,256]{2,1,0:T(8,128)(2,1)}, u32[]{:S(2)}, u32[]{:S(2)}) %all-to-all-start.2) | async-done | bytes 2097184 | tf_op jit(solution)/shard_map/all_to_all | solution.py:620
  156.7 6.5 %gather_back.1 = (f32[1024,256]{1,0:T(8,128)S(1)}, f32[4,256]{1,0:T(4,128)S(1)}) custom-call(bf16[4096,256]{1,0:T(8,128)(2,1)} %bitcast.8.ret_ref, f32[1024,8]{1,0:T(8,128)} %bitcast.23, f32[2,1024,256]{2,1,0:T(8,128)S(1)} %copy-done, f32[1,256]{1,0:T(1,128)S(1)} %pad_dynamic-slice_fusion.mutual_ref), custom_call_target="tpu_custom_call" | custom-call | flops 4294967296 | bytes 6291456 | tf_op jit(solution)/shard_map/gather_back/pallas_call | solution.py:598
  163.2 12.0 %all_to_all.20 = f32[32,4,256]{2,1,0:T(4,128)S(1)} all-to-all(f32[32,4,256]{2,1,0:T(4,128)S(1)} %broadcast_in_dim.2), channel_id=1, replica_groups=mesh['branch'=8,'group'=4] {'branch','group'}, dimensions={0} | all-to-all | bytes 262144 | tf_op jit(solution)/shard_map/all_to_all | solution.py:620
  175.2 0.1 slice_reduce_fusion.1
  175.3 0.2 multiply_reduce_fusion
  175.5 0.6 pad_maximum_fusion.1
  176.1 1.1 subtract_divide_fusion
  (12 shorter events, 0.2 us)
Async XLA Ops:
  9.1 7.4 %copy-start.5 = (bf16[64,256]{1,0:T(8,128)(2,1)S(1)}, bf16[64,256]{1,0:T(8,128)(2,1)}, u32[]{:S(2)}) copy-start(bf16[64,256]{1,0:T(8,128)(2,1)} %param.25) | copy-start | bytes 98308
  9.1 7.5 %copy-start.7 = (bf16[2,64,64]{2,1,0:T(8,128)(2,1)S(1)}, bf16[2,64,64]{2,1,0:T(8,128)(2,1)}, u32[]{:S(2)}) copy-start(bf16[2,64,64]{2,1,0:T(8,128)(2,1)} %param.23) | copy-start | bytes 49156
  9.1 8.8 %copy-start.1 = (bf16[2,512,512]{2,1,0:T(8,128)(2,1)S(1)}, bf16[2,512,512]{2,1,0:T(8,128)(2,1)}, u32[]{:S(2)}) copy-start(bf16[2,512,512]{2,1,0:T(8,128)(2,1)} %gram_ref.2) | copy-start | bytes 3145732
  9.1 8.8 %copy-start.2 = (bf16[2,64,512]{2,1,0:T(8,128)(2,1)S(1)}, bf16[2,64,512]{2,1,0:T(8,128)(2,1)}, u32[]{:S(2)}) copy-start(bf16[2,64,512]{2,1,0:T(8,128)(2,1)} %base_ref.2) | copy-start | bytes 393220
  9.1 57.5 %all-to-all-start = ((s16[32,264,128]{2,1,0:T(8,128)(2,1)}), s16[32,264,128]{2,1,0:T(8,128)(2,1)S(1)}, u32[]{:S(2)}, u32[]{:S(2)}) async-start(s16[32,264,128]{2,1,0:T(8,128)(2,1)} %get-tuple-element.24), calls=%async_computation | async-start | bytes 4325376 | tf_op jit(solution)/shard_map/all_to_all | solution.py:620
  71.7 21.5 %all-to-all-start.1 = ((bf16[8,160,256]{2,1,0:T(8,128)(2,1)}), bf16[8,160,256]{2,1,0:T(8,128)(2,1)}, u32[]{:S(2)}, u32[]{:S(2)}) async-start(bf16[8,160,256]{2,1,0:T(8,128)(2,1)} %get-tuple-element.32), calls=%async_computation.1 | async-start | bytes 1310720 | tf_op jit(solution)/shard_map/all_to_all | solution.py:620
  76.1 6.0 %copy-start.4 = (s32[2,8]{1,0:T(2,128)S(1)}, s32[2,8]{1,0:T(2,128)}, u32[]{:S(2)}) copy-start(s32[2,8]{1,0:T(2,128)} %list_ref.2) | copy-start | bytes 196
  88.4 8.1 %copy-start.3 = (s32[2,16]{1,0:T(2,128)S(1)}, s32[2,16]{1,0:T(2,128)}, u32[]{:S(2)}) copy-start(s32[2,16]{1,0:T(2,128)} %list_ref.3) | copy-start | bytes 388
  94.6 4.1 %collective-permute-start = (bf16[64,256]{1,0:T(8,128)(2,1)S(1)}, bf16[64,256]{1,0:T(8,128)(2,1)S(1)}, u32[]{:S(2)}, u32[]{:S(2)}) collective-permute-start(bf16[64,256]{1,0:T(8,128)(2,1)S(1)} %parent_of.1.refs_6_), channel_id=1, source_target_pairs={{0,1},{1,0},{2,3},{3,2},{4,5},{5,4},{6,7},{7,6},{8,9},{9,8},{10,11... | collective-permute-start | bytes 98312 | tf_op jit(solution)/shard_map/ppermute | solution.py:626
  94.6 4.1 %collective-permute-start.1 = (bf16[64,256]{1,0:T(8,128)(2,1)S(1)}, bf16[64,256]{1,0:T(8,128)(2,1)S(1)}, u32[]{:S(2)}, u32[]{:S(2)}) collective-permute-start(bf16[64,256]{1,0:T(8,128)(2,1)S(1)} %parent_of.1.refs_6_), channel_id=1, source_target_pairs={{0,2},{1,3},{2,0},{3,1},{4,6},{5,7},{6,4},{7,5},{8,10},{9,11},{10,... | collective-permute-start | bytes 98312 | tf_op jit(solution)/shard_map/ppermute | solution.py:626
  96.4 3.4 %collective-permute-start.2 = (bf16[64,256]{1,0:T(8,128)(2,1)S(1)}, bf16[64,256]{1,0:T(8,128)(2,1)S(1)}, u32[]{:S(2)}, u32[]{:S(2)}) collective-permute-start(bf16[64,256]{1,0:T(8,128)(2,1)S(1)} %parent_of.1.refs_6_), channel_id=1, source_target_pairs={{0,3},{1,2},{2,1},{3,0},{4,7},{5,6},{6,5},{7,4},{8,11},{9,10},{10,... | collective-permute-start | bytes 98312 | tf_op jit(solution)/shard_map/ppermute | solution.py:626
  104.4 3.9 %copy-start = (f32[2,1024,256]{2,1,0:T(8,128)S(1)}, f32[2,1024,256]{2,1,0:T(8,128)}, u32[]{:S(2)}) copy-start(f32[2,1024,256]{2,1,0:T(8,128)} %basis_ref.1) | copy-start | bytes 6291460
  104.4 52.3 %all-to-all-start.2 = ((bf16[32,128,256]{2,1,0:T(8,128)(2,1)}), bf16[32,128,256]{2,1,0:T(8,128)(2,1)}, u32[]{:S(2)}, u32[]{:S(2)}) async-start(bf16[32,128,256]{2,1,0:T(8,128)(2,1)} %bitcast.21), calls=%async_computation.2 | async-start | bytes 4194304 | tf_op jit(solution)/shard_map/all_to_all | solution.py:620
  108.3 2.2 %copy-start.6 = (f32[8,1024]{1,0:T(8,128)S(1)}, f32[8,1024]{1,0:T(8,128)}, u32[]{:S(2)}) copy-start(f32[8,1024]{1,0:T(8,128)} %get-tuple-element.41) | copy-start | bytes 98308
  108.6 2.9 %collective-permute-start.3 = (f32[3,256]{1,0:T(4,128)S(1)}, f32[3,256]{1,0:T(4,128)S(1)}, u32[]{:S(2)}, u32[]{:S(2)}) collective-permute-start(f32[3,256]{1,0:T(4,128)S(1)} %pad_maximum_fusion), channel_id=1, source_target_pairs={{0,1},{1,0},{2,3},{3,2},{4,5},{5,4},{6,7},{7,6},{8,9},{9,8},{10,11... | collective-permute-start | bytes 9224 | tf_op jit(solution)/shard_map/ppermute | solution.py:626
  108.6 5.5 %collective-permute-start.4 = (f32[3,256]{1,0:T(4,128)S(1)}, f32[3,256]{1,0:T(4,128)S(1)}, u32[]{:S(2)}, u32[]{:S(2)}) collective-permute-start(f32[3,256]{1,0:T(4,128)S(1)} %pad_maximum_fusion), channel_id=1, source_target_pairs={{0,2},{1,3},{2,0},{3,1},{4,6},{5,7},{6,4},{7,5},{8,10},{9,11},{10,... | collective-permute-start | bytes 9224 | tf_op jit(solution)/shard_map/ppermute | solution.py:626
  110.1 4.0 %collective-permute-start.5 = (f32[3,256]{1,0:T(4,128)S(1)}, f32[3,256]{1,0:T(4,128)S(1)}, u32[]{:S(2)}, u32[]{:S(2)}) collective-permute-start(f32[3,256]{1,0:T(4,128)S(1)} %pad_maximum_fusion), channel_id=1, source_target_pairs={{0,3},{1,2},{2,1},{3,0},{4,7},{5,6},{6,5},{7,4},{8,11},{9,10},{10,... | collective-permute-start | bytes 9224 | tf_op jit(solution)/shard_map/ppermute | solution.py:626

commit v6 on v5

--- a/solution.py
+++ b/solution.py
@@ -613,6 +613,58 @@
     )(ret, place_col, basis, mutual)
 
 
+def finish_kernel(groups, total_rows, sums_ref, image_ref, basis_ref, next_hbm, column_ref, ready_ref, sems):
+    krylov, rows_dev, width = basis_ref.shape
+    devices, lines = sums_ref.shape[:2]
+    share = lines - krylov - 1
+    whole_sum = jnp.sum(sums_ref[...], axis=0)
+    projection = [whole_sum[k : k + 1, :] * (1.0 / total_rows) for k in range(krylov)]
+    square = whole_sum[krylov : krylov + 1, :] * (1.0 / total_rows)
+    for part in projection:
+        square = square - 2.0 * part * part
+    pairs = [(i, j) for i in range(krylov) for j in range(i, krylov)]
+    for at, (i, j) in enumerate(pairs):
+        line = krylov + 1 + at % share
+        mutual = jnp.zeros((1, width), F32)
+        for d in range(at // share, devices, groups):
+            mutual = mutual + sums_ref[d, line : line + 1, :]
+        times = (1.0 if i == j else 2.0) / total_rows
+        square = square + times * projection[i] * projection[j] * mutual
+    scale = jnp.sqrt(jnp.maximum(square, 0.0) + 1e-06)
+    column_ref[...] = jnp.concatenate(projection + [scale], axis=0)
+    inverse = 1.0 / scale
+    size = rows_dev // sems.shape[0]
+    copies = []
+    for block in range(sems.shape[0]):
+        at = pl.ds(block * size, size)
+        remainder = image_ref[at, :]
+        for k in range(krylov):
+            remainder = remainder - projection[k] * basis_ref[k, at, :]
+        ready_ref[at, :] = remainder * inverse
+        copies.append(pltpu.make_async_copy(ready_ref.at[at], next_hbm.at[at], sems.at[block]))
+        copies[-1].start()
+    for copy in copies:
+        copy.wait()
+
+
+def finish(sums, image, basis, groups, total_rows):
+    krylov, rows_dev, width = basis.shape
+    direct = pl.BlockSpec(memory_space=pltpu.VMEM)
+    return pl.pallas_call(
+        functools.partial(finish_kernel, groups, total_rows),
+        in_specs=[direct] * 3,
+        out_specs=(pl.BlockSpec(memory_space=pltpu.HBM), direct),
+        out_shape=(
+            in_hbm((rows_dev, width), F32),
+            jax.ShapeDtypeStruct((krylov + 1, width), F32),
+        ),
+        scratch_shapes=[pltpu.VMEM((rows_dev, width), F32), pltpu.SemaphoreType.DMA((4,))],
+        compiler_params=params(mib=8),
+        cost_estimate=cost(8 * rows_dev * width, 4 << 20),
+        name="finish",
+    )(sums, image, basis)
+
+
 AXES = ("branch", "group")
 
 
@@ -689,19 +741,7 @@
     own = lax.dynamic_slice_in_dim(mutual, share * lax.axis_index("group"), share, 0)
     primal, sums = gather_back(near_by(returned), kept(place.T), basis, own, spread)
     everyone = to_all(sums, AXES, devices)
-    sums = jnp.sum(everyone[:, : krylov + 1], axis=0)
-    mutual = jnp.sum(everyone.reshape(branches, groups, -1, columns)[:, :, krylov + 1 :], axis=0)
-    mutual = mutual.reshape(share * groups, columns)
-
-    total_rows = rows_dev * devices
-    projection = sums[:krylov] / total_rows
-    remainder = primal - jnp.sum(projection[:, None, :] * basis, axis=0)
-    square = sums[krylov] / total_rows - 2.0 * jnp.sum(projection * projection, axis=0)
-    for at, (i, j) in enumerate(pairs):
-        times = 1.0 if i == j else 2.0
-        square = square + times * projection[i] * projection[j] * mutual[at] / total_rows
-    norm_scale = jnp.sqrt(jnp.maximum(square, 0.0) + 1e-06)
-    return (remainder / norm_scale, jnp.concatenate([projection, norm_scale[None]], axis=0))
+    return finish(everyone, primal, basis, groups, rows_dev * devices)
 
 
 def solution(mesh):

time: 178 us -> 178 us (level)
  other arithmetic: 2.32 us -> 0.28 us
  Pallas kernels: 43.3 us -> 45.1 us
where the time goes in v6:
time: 178 us; the launch traced here: 177 us
  waiting for transfers between devices  96.8 us (54%)
  Pallas kernels  45.1 us (25%)
  starting transfers between devices  19.4 us (11%)
  blocking collectives  12 us (7%)
  local copies, waits for them, and re-layouts  2.5 us (1%)
    all_to_all x3, waiting for transfers between devices, exchange(): return lax.all_to_all(values, axes, split_axis=0, concat_axis=0, tiled=True)  93.2 us
    all_to_all x3, starting transfers between devices, exchange(): return lax.all_to_all(values, axes, split_axis=0, concat_axis=0, tiled=True)  15.6 us
    all_to_all x1, blocking collectives, exchange(): return lax.all_to_all(values, axes, split_axis=0, concat_axis=0, tiled=True)  12 us
    pallas_call x1, Pallas kernels, spread_out(): pl.pallas_call(functools.partial(spread_kernel, slots), grid=(devices //...  8.48 us
    pallas_call x1, Pallas kernels, gather_back(): pl.pallas_call(functools.partial(gather_kernel, spread), in_specs=[direct...  6.45 us
    pallas_call x1, Pallas kernels, near_field(): pl.pallas_call(near_kernel, grid_spec=pltpu.PrefetchScalarGridSpec(num_sc...  6.3 us
    pallas_call x1, Pallas kernels, refine(): pl.pallas_call(functools.partial(refine_kernel, slots), in_specs=[direct,...  5.94 us
    pallas_call x1, Pallas kernels, collect(): pl.pallas_call(functools.partial(collect_kernel, slots), in_specs=[direct...  5.11 us
  transfers between devices with their start and end apart: 9, of which 5 were waited for; matrix products, arithmetic and copies ran while one was open for 2% of the time, Pallas kernels for 10%

profile of v6, /device:TPU:0, one launch (start us, length us, event | category | flops | bytes accessed | tf_op | source)
XLA Modules:
  0.0 177.1 jit_solution(12152355232666278955)
XLA Ops:
  0.6 8.5 %spread_out.1 = (s16[32,264,128]{2,1,0:T(8,128)(2,1)}, f32[8,1024]{1,0:T(8,128)}) custom-call(s32[2,1024]{1,0:T(2,128)} %bitcast.29, s32[2,1024]{1,0:T(2,128)} %bitcast.30, f32[2,1024]{1,0:T(2,128)} %bitcast.31, f32[2,1024,256]{2,1,0:T(8,128)} %basis_ref.3), custom_call_target="tpu_custom_call" | custom-call | flops 4294967296 | bytes 4194304 | tf_op jit(solution)/shard_map/spread_out/pallas_call | solution.py:182
  9.1 0.0 copy-start.5
  9.1 0.0 copy-start.7
  9.1 0.0 copy-start.1
  9.1 0.0 copy-start.2
  9.2 7.3 %all-to-all-start = ((s16[32,264,128]{2,1,0:T(8,128)(2,1)}), s16[32,264,128]{2,1,0:T(8,128)(2,1)S(1)}, u32[]{:S(2)}, u32[]{:S(2)}) async-start(s16[32,264,128]{2,1,0:T(8,128)(2,1)} %get-tuple-element.24), calls=%async_computation | async-start | bytes 4325376 | tf_op jit(solution)/shard_map/all_to_all | solution.py:672
  16.5 0.0 copy-done.5
  16.5 0.1 reshape.74
  16.6 0.0 copy-done.7
  16.7 0.1 reshape.73.ascend_ref
  16.8 1.2 gather_fusion
  18.0 0.0 copy-done.1
  18.0 0.0 copy-done.2
  18.0 0.4 rise.1.rise_ref
  18.4 48.2 %all-to-all-done.got_ref = s16[32,264,128]{2,1,0:T(8,128)(2,1)S(1)} async-done(((s16[32,264,128]{2,1,0:T(8,128)(2,1)}), s16[32,264,128]{2,1,0:T(8,128)(2,1)S(1)}, u32[]{:S(2)}, u32[]{:S(2)}) %all-to-all-start) | async-done | bytes 2162720 | tf_op jit(solution)/shard_map/all_to_all | solution.py:672
  66.6 5.1 %collect.1 = (f32[1024,256]{1,0:T(8,128)S(1)}, bf16[8,160,256]{2,1,0:T(8,128)(2,1)}, f32[32,128]{1,0:T(8,128)}) custom-call(s16[32,264,128]{2,1,0:T(8,128)(2,1)S(1)} %all-to-all-done.got_ref, bf16[2,64,512]{2,1,0:T(8,128)(2,1)S(1)} %rise.1.rise_ref, bf16[32,256]{1,0:T(8,128)(2,1)S(1)} %reshape.73.ascend_ref), custom_call_target="tpu_custom_call" | custom-call | flops 2147483648 | bytes 4194304 | tf_op jit(solution)/shard_map/collect/pallas_call | solution.py:306
  71.7 4.4 %all-to-all-start.1 = ((bf16[8,160,256]{2,1,0:T(8,128)(2,1)}), bf16[8,160,256]{2,1,0:T(8,128)(2,1)}, u32[]{:S(2)}, u32[]{:S(2)}) async-start(bf16[8,160,256]{2,1,0:T(8,128)(2,1)} %get-tuple-element.32), calls=%async_computation.1 | async-start | bytes 1310720 | tf_op jit(solution)/shard_map/all_to_all | solution.py:672
  76.1 0.0 copy-start.4
  76.1 5.9 %refine.1.first_ref = f32[1024,256]{1,0:T(8,128)S(1)} custom-call(s16[32,264,128]{2,1,0:T(8,128)(2,1)S(1)} %all-to-all-done.got_ref, f32[1024,256]{1,0:T(8,128)S(1)} %get-tuple-element.33.dual_ref, bf16[2,512,512]{2,1,0:T(8,128)(2,1)} %gram_ref.2), custom_call_target="tpu_custom_call" | custom-call | flops 2147483648 | bytes 4194304 | tf_op jit(solution)/shard_map/refine/pallas_call | solution.py:351
  82.1 0.0 copy-done.4
  82.1 6.3 %near_field.1.image_ref = f32[1024,256]{1,0:T(8,128)S(1)} custom-call(s32[2,8]{1,0:T(2,128)S(1)} %copy-done.4, bf16[2,8,512,512]{3,2,1,0:T(8,128)(2,1)} %block_ref.2, f32[1024,256]{1,0:T(8,128)S(1)} %refine.1.first_ref), custom_call_target="tpu_custom_call" | custom-call | flops 2147483648 | bytes 8388608 | tf_op jit(solution)/shard_map/near_field/pallas_call | solution.py:454
  88.4 0.0 copy-start.3
  88.4 2.3 %prepare.1 = (f32[1024,256]{1,0:T(8,128)S(1)}, bf16[1024,128]{1,0:T(8,128)(2,1)S(1)}) custom-call(f32[1024,256]{1,0:T(8,128)S(1)} %near_field.1.image_ref, bf16[2,64,512]{2,1,0:T(8,128)(2,1)} %base_ref.2, bf16[2,512,512]{2,1,0:T(8,128)(2,1)} %gram_ref.2), custom_call_target="tpu_custom_call" | custom-call | flops 536870912 | bytes 4194304 | tf_op jit(solution)/shard_map/prepare/pallas_call | solution.py:490
  90.8 2.4 %all-to-all-done.1.coeff_ref = bf16[8,160,256]{2,1,0:T(8,128)(2,1)} async-done(((bf16[8,160,256]{2,1,0:T(8,128)(2,1)}), bf16[8,160,256]{2,1,0:T(8,128)(2,1)}, u32[]{:S(2)}, u32[]{:S(2)}) %all-to-all-start.1) | async-done | bytes 655392 | tf_op jit(solution)/shard_map/all_to_all | solution.py:672
  93.2 1.4 parent_of.1.refs_6_
  94.6 0.0 collective-permute-start
  94.7 1.8 collective-permute-start.1
  96.4 0.1 collective-permute-start.2
  96.5 0.0 copy-done.3
  96.5 2.2 %far_field.1.refs_2_ = f32[2,64,256]{2,1,0:T(8,128)S(1)} custom-call(s32[2,16]{1,0:T(2,128)S(1)} %copy-done.3, bf16[8,160,256]{2,1,0:T(8,128)(2,1)} %all-to-all-done.1.coeff_ref, bf16[2,16,64,64]{3,2,1,0:T(8,128)(2,1)} %block_ref.3), custom_call_target="tpu_custom_call" | custom-call | flops 67108864 | bytes 1048576 | tf_op jit(solution)/shard_map/far_field/pallas_call | solution.py:412
  98.7 0.0 collective-permute-done.refs_7_
  98.7 0.0 collective-permute-done.1.refs_8_
  98.8 1.0 collective-permute-done.2.refs_9_
  99.8 4.7 %reply.1 = bf16[4096,256]{1,0:T(8,128)(2,1)} custom-call(f32[1024,256]{1,0:T(8,128)S(1)} %get-tuple-element.36.refs_0_, bf16[1024,128]{1,0:T(8,128)(2,1)S(1)} %get-tuple-element.37.refs_1_, f32[2,64,256]{2,1,0:T(8,128)S(1)} %far_field.1.refs_2_, bf16[4,64,64]{2,1,0:T(8,128)(2,1)} %gather_fusion, bf16[2,64,64]{2,1,0:T(8,128)(2,1)} %refs_4_.1, ...), custom_call_target="tpu_custom_call" | custom-call | flops 2147483648 | bytes 4194304 | tf_op jit(solution)/shard_map/reply/pallas_call | solution.py:542
  104.5 0.0 copy-start
  104.5 3.8 %all-to-all-start.2 = ((bf16[32,128,256]{2,1,0:T(8,128)(2,1)}), bf16[32,128,256]{2,1,0:T(8,128)(2,1)}, u32[]{:S(2)}, u32[]{:S(2)}) async-start(bf16[32,128,256]{2,1,0:T(8,128)(2,1)} %bitcast.18), calls=%async_computation.2 | async-start | bytes 4194304 | tf_op jit(solution)/shard_map/all_to_all | solution.py:672
  108.3 0.0 copy-done
  108.4 0.0 copy-start.6
  108.4 0.2 multiply_reduce_fusion.2
  108.6 0.1 collective-permute-start.3
  108.7 1.5 collective-permute-start.4
  110.2 0.4 collective-permute-start.5
  110.6 0.0 copy-done.6
  110.6 1.0 copy.21
  111.6 0.0 collective-permute-done.3
  111.6 2.7 %collective-permute-done.4 = f32[3,256]{1,0:T(4,128)S(1)} collective-permute-done((f32[3,256]{1,0:T(4,128)S(1)}, f32[3,256]{1,0:T(4,128)S(1)}, u32[]{:S(2)}, u32[]{:S(2)}) %collective-permute-start.4) | collective-permute-done | bytes 3104 | tf_op jit(solution)/shard_map/ppermute | solution.py:678
  114.2 0.0 collective-permute-done.5
  114.3 42.5 %all-to-all-done.2 = bf16[32,128,256]{2,1,0:T(8,128)(2,1)} async-done(((bf16[32,128,256]{2,1,0:T(8,128)(2,1)}), bf16[32,128,256]{2,1,0:T(8,128)(2,1)}, u32[]{:S(2)}, u32[]{:S(2)}) %all-to-all-start.2) | async-done | bytes 2097184 | tf_op jit(solution)/shard_map/all_to_all | solution.py:672
  156.8 6.5 %gather_back.1 = (f32[1024,256]{1,0:T(8,128)S(1)}, f32[4,256]{1,0:T(4,128)S(1)}) custom-call(bf16[4096,256]{1,0:T(8,128)(2,1)} %bitcast.8.ret_ref, f32[1024,8]{1,0:T(8,128)} %bitcast.19, f32[2,1024,256]{2,1,0:T(8,128)S(1)} %copy-done, f32[1,256]{1,0:T(1,128)S(1)} %pad_dynamic-slice_fusion.mutual_ref), custom_call_target="tpu_custom_call" | custom-call | flops 4294967296 | bytes 6291456 | tf_op jit(solution)/shard_map/gather_back/pallas_call | solution.py:598
  163.3 12.0 %all_to_all.20.sums_ref = f32[32,4,256]{2,1,0:T(4,128)S(1)} all-to-all(f32[32,4,256]{2,1,0:T(4,128)S(1)} %broadcast_in_dim.2), channel_id=1, replica_groups=mesh['branch'=8,'group'=4] {'branch','group'}, dimensions={0} | all-to-all | bytes 262144 | tf_op jit(solution)/shard_map/all_to_all | solution.py:672
  175.2 1.7 finish.1
  (8 shorter events, 0.1 us)
Async XLA Ops:
  9.1 7.4 %copy-start.5 = (bf16[64,256]{1,0:T(8,128)(2,1)S(1)}, bf16[64,256]{1,0:T(8,128)(2,1)}, u32[]{:S(2)}) copy-start(bf16[64,256]{1,0:T(8,128)(2,1)} %param.25) | copy-start | bytes 98308
  9.1 7.5 %copy-start.7 = (bf16[2,64,64]{2,1,0:T(8,128)(2,1)S(1)}, bf16[2,64,64]{2,1,0:T(8,128)(2,1)}, u32[]{:S(2)}) copy-start(bf16[2,64,64]{2,1,0:T(8,128)(2,1)} %param.23) | copy-start | bytes 49156
  9.1 8.9 %copy-start.1 = (bf16[2,512,512]{2,1,0:T(8,128)(2,1)S(1)}, bf16[2,512,512]{2,1,0:T(8,128)(2,1)}, u32[]{:S(2)}) copy-start(bf16[2,512,512]{2,1,0:T(8,128)(2,1)} %gram_ref.2) | copy-start | bytes 3145732
  9.1 8.8 %copy-start.2 = (bf16[2,64,512]{2,1,0:T(8,128)(2,1)S(1)}, bf16[2,64,512]{2,1,0:T(8,128)(2,1)}, u32[]{:S(2)}) copy-start(bf16[2,64,512]{2,1,0:T(8,128)(2,1)} %base_ref.2) | copy-start | bytes 393220
  9.2 57.5 %all-to-all-start = ((s16[32,264,128]{2,1,0:T(8,128)(2,1)}), s16[32,264,128]{2,1,0:T(8,128)(2,1)S(1)}, u32[]{:S(2)}, u32[]{:S(2)}) async-start(s16[32,264,128]{2,1,0:T(8,128)(2,1)} %get-tuple-element.24), calls=%async_computation | async-start | bytes 4325376 | tf_op jit(solution)/shard_map/all_to_all | solution.py:672
  71.7 21.5 %all-to-all-start.1 = ((bf16[8,160,256]{2,1,0:T(8,128)(2,1)}), bf16[8,160,256]{2,1,0:T(8,128)(2,1)}, u32[]{:S(2)}, u32[]{:S(2)}) async-start(bf16[8,160,256]{2,1,0:T(8,128)(2,1)} %get-tuple-element.32), calls=%async_computation.1 | async-start | bytes 1310720 | tf_op jit(solution)/shard_map/all_to_all | solution.py:672
  76.1 6.0 %copy-start.4 = (s32[2,8]{1,0:T(2,128)S(1)}, s32[2,8]{1,0:T(2,128)}, u32[]{:S(2)}) copy-start(s32[2,8]{1,0:T(2,128)} %list_ref.2) | copy-start | bytes 196
  88.4 8.1 %copy-start.3 = (s32[2,16]{1,0:T(2,128)S(1)}, s32[2,16]{1,0:T(2,128)}, u32[]{:S(2)}) copy-start(s32[2,16]{1,0:T(2,128)} %list_ref.3) | copy-start | bytes 388
  94.6 4.1 %collective-permute-start = (bf16[64,256]{1,0:T(8,128)(2,1)S(1)}, bf16[64,256]{1,0:T(8,128)(2,1)S(1)}, u32[]{:S(2)}, u32[]{:S(2)}) collective-permute-start(bf16[64,256]{1,0:T(8,128)(2,1)S(1)} %parent_of.1.refs_6_), channel_id=1, source_target_pairs={{0,1},{1,0},{2,3},{3,2},{4,5},{5,4},{6,7},{7,6},{8,9},{9,8},{10,11... | collective-permute-start | bytes 98312 | tf_op jit(solution)/shard_map/ppermute | solution.py:678
  94.7 4.1 %collective-permute-start.1 = (bf16[64,256]{1,0:T(8,128)(2,1)S(1)}, bf16[64,256]{1,0:T(8,128)(2,1)S(1)}, u32[]{:S(2)}, u32[]{:S(2)}) collective-permute-start(bf16[64,256]{1,0:T(8,128)(2,1)S(1)} %parent_of.1.refs_6_), channel_id=1, source_target_pairs={{0,2},{1,3},{2,0},{3,1},{4,6},{5,7},{6,4},{7,5},{8,10},{9,11},{10,... | collective-permute-start | bytes 98312 | tf_op jit(solution)/shard_map/ppermute | solution.py:678
  96.4 3.4 %collective-permute-start.2 = (bf16[64,256]{1,0:T(8,128)(2,1)S(1)}, bf16[64,256]{1,0:T(8,128)(2,1)S(1)}, u32[]{:S(2)}, u32[]{:S(2)}) collective-permute-start(bf16[64,256]{1,0:T(8,128)(2,1)S(1)} %parent_of.1.refs_6_), channel_id=1, source_target_pairs={{0,3},{1,2},{2,1},{3,0},{4,7},{5,6},{6,5},{7,4},{8,11},{9,10},{10,... | collective-permute-start | bytes 98312 | tf_op jit(solution)/shard_map/ppermute | solution.py:678
  104.5 3.9 %copy-start = (f32[2,1024,256]{2,1,0:T(8,128)S(1)}, f32[2,1024,256]{2,1,0:T(8,128)}, u32[]{:S(2)}) copy-start(f32[2,1024,256]{2,1,0:T(8,128)} %basis_ref.3) | copy-start | bytes 6291460
  104.5 52.3 %all-to-all-start.2 = ((bf16[32,128,256]{2,1,0:T(8,128)(2,1)}), bf16[32,128,256]{2,1,0:T(8,128)(2,1)}, u32[]{:S(2)}, u32[]{:S(2)}) async-start(bf16[32,128,256]{2,1,0:T(8,128)(2,1)} %bitcast.18), calls=%async_computation.2 | async-start | bytes 4194304 | tf_op jit(solution)/shard_map/all_to_all | solution.py:672
  108.4 2.2 %copy-start.6 = (f32[8,1024]{1,0:T(8,128)S(1)}, f32[8,1024]{1,0:T(8,128)}, u32[]{:S(2)}) copy-start(f32[8,1024]{1,0:T(8,128)} %get-tuple-element.41) | copy-start | bytes 98308
  108.6 2.9 %collective-permute-start.3 = (f32[3,256]{1,0:T(4,128)S(1)}, f32[3,256]{1,0:T(4,128)S(1)}, u32[]{:S(2)}, u32[]{:S(2)}) collective-permute-start(f32[3,256]{1,0:T(4,128)S(1)} %pad_maximum_fusion), channel_id=1, source_target_pairs={{0,1},{1,0},{2,3},{3,2},{4,5},{5,4},{6,7},{7,6},{8,9},{9,8},{10,11... | collective-permute-start | bytes 9224 | tf_op jit(solution)/shard_map/ppermute | solution.py:678
  108.7 5.5 %collective-permute-start.4 = (f32[3,256]{1,0:T(4,128)S(1)}, f32[3,256]{1,0:T(4,128)S(1)}, u32[]{:S(2)}, u32[]{:S(2)}) collective-permute-start(f32[3,256]{1,0:T(4,128)S(1)} %pad_maximum_fusion), channel_id=1, source_target_pairs={{0,2},{1,3},{2,0},{3,1},{4,6},{5,7},{6,4},{7,5},{8,10},{9,11},{10,... | collective-permute-start | bytes 9224 | tf_op jit(solution)/shard_map/ppermute | solution.py:678
  110.2 4.0 %collective-permute-start.5 = (f32[3,256]{1,0:T(4,128)S(1)}, f32[3,256]{1,0:T(4,128)S(1)}, u32[]{:S(2)}, u32[]{:S(2)}) collective-permute-start(f32[3,256]{1,0:T(4,128)S(1)} %pad_maximum_fusion), channel_id=1, source_target_pairs={{0,3},{1,2},{2,1},{3,0},{4,7},{5,6},{6,5},{7,4},{8,11},{9,10},{10,... | collective-permute-start | bytes 9224 | tf_op jit(solution)/shard_map/ppermute | solution.py:678

commit v7 on v6

--- a/solution.py
+++ b/solution.py
@@ -13,7 +13,7 @@
 TOP = 32767.0
 REST = 65534.0
 LOG2 = 0.6931471805599453
-SPREAD_BLOCK = 1024
+SPREAD_BLOCK = 2048
 COLLECT_BLOCK = 512
 REPLY_BLOCK = 512
 GATHER_BLOCK = 256

time: 178 us -> 178 us (level)
  no operation moved by 1% of the time
where the time goes in v7:
time: 178 us; the launch traced here: 177 us
  waiting for transfers between devices  96.9 us (54%)
  Pallas kernels  44.9 us (25%)
  starting transfers between devices  19.4 us (11%)
  blocking collectives  12 us (7%)
  local copies, waits for them, and re-layouts  2.5 us (1%)
    all_to_all x3, waiting for transfers between devices, exchange(): return lax.all_to_all(values, axes, split_axis=0, concat_axis=0, tiled=True)  93.2 us
    all_to_all x3, starting transfers between devices, exchange(): return lax.all_to_all(values, axes, split_axis=0, concat_axis=0, tiled=True)  15.6 us
    all_to_all x1, blocking collectives, exchange(): return lax.all_to_all(values, axes, split_axis=0, concat_axis=0, tiled=True)  12 us
    pallas_call x1, Pallas kernels, spread_out(): pl.pallas_call(functools.partial(spread_kernel, slots), grid=(devices //...  8.32 us
    pallas_call x1, Pallas kernels, gather_back(): pl.pallas_call(functools.partial(gather_kernel, spread), in_specs=[direct...  6.46 us
    pallas_call x1, Pallas kernels, near_field(): pl.pallas_call(near_kernel, grid_spec=pltpu.PrefetchScalarGridSpec(num_sc...  6.3 us
    pallas_call x1, Pallas kernels, refine(): pl.pallas_call(functools.partial(refine_kernel, slots), in_specs=[direct,...  5.94 us
    pallas_call x1, Pallas kernels, collect(): pl.pallas_call(functools.partial(collect_kernel, slots), in_specs=[direct...  5.11 us
  transfers between devices with their start and end apart: 9, of which 5 were waited for; matrix products, arithmetic and copies ran while one was open for 2% of the time, Pallas kernels for 10%

profile of v7, /device:TPU:0, one launch (start us, length us, event | category | flops | bytes accessed | tf_op | source)
XLA Modules:
  0.0 177.0 jit_solution(1648217650616785142)
XLA Ops:
  0.6 8.3 %spread_out.1 = (s16[32,264,128]{2,1,0:T(8,128)(2,1)}, f32[8,1024]{1,0:T(8,128)}) custom-call(s32[2,1024]{1,0:T(2,128)} %bitcast.29, s32[2,1024]{1,0:T(2,128)} %bitcast.30, f32[2,1024]{1,0:T(2,128)} %bitcast.31, f32[2,1024,256]{2,1,0:T(8,128)} %basis_ref.3), custom_call_target="tpu_custom_call" | custom-call | flops 4294967296 | bytes 4194304 | tf_op jit(solution)/shard_map/spread_out/pallas_call | solution.py:182
  9.0 0.0 copy-start.5
  9.0 0.0 copy-start.7
  9.0 0.0 copy-start.1
  9.0 0.0 copy-start.2
  9.0 7.3 %all-to-all-start = ((s16[32,264,128]{2,1,0:T(8,128)(2,1)}), s16[32,264,128]{2,1,0:T(8,128)(2,1)S(1)}, u32[]{:S(2)}, u32[]{:S(2)}) async-start(s16[32,264,128]{2,1,0:T(8,128)(2,1)} %get-tuple-element.24), calls=%async_computation | async-start | bytes 4325376 | tf_op jit(solution)/shard_map/all_to_all | solution.py:672
  16.4 0.0 copy-done.5
  16.4 0.1 reshape.74
  16.5 0.0 copy-done.7
  16.5 0.1 reshape.73.ascend_ref
  16.7 1.2 gather_fusion
  17.8 0.0 copy-done.1
  17.8 0.0 copy-done.2
  17.8 0.4 rise.1.rise_ref
  18.3 48.2 %all-to-all-done.got_ref = s16[32,264,128]{2,1,0:T(8,128)(2,1)S(1)} async-done(((s16[32,264,128]{2,1,0:T(8,128)(2,1)}), s16[32,264,128]{2,1,0:T(8,128)(2,1)S(1)}, u32[]{:S(2)}, u32[]{:S(2)}) %all-to-all-start) | async-done | bytes 2162720 | tf_op jit(solution)/shard_map/all_to_all | solution.py:672
  66.5 5.1 %collect.1 = (f32[1024,256]{1,0:T(8,128)S(1)}, bf16[8,160,256]{2,1,0:T(8,128)(2,1)}, f32[32,128]{1,0:T(8,128)}) custom-call(s16[32,264,128]{2,1,0:T(8,128)(2,1)S(1)} %all-to-all-done.got_ref, bf16[2,64,512]{2,1,0:T(8,128)(2,1)S(1)} %rise.1.rise_ref, bf16[32,256]{1,0:T(8,128)(2,1)S(1)} %reshape.73.ascend_ref), custom_call_target="tpu_custom_call" | custom-call | flops 2147483648 | bytes 4194304 | tf_op jit(solution)/shard_map/collect/pallas_call | solution.py:306
  71.6 4.4 %all-to-all-start.1 = ((bf16[8,160,256]{2,1,0:T(8,128)(2,1)}), bf16[8,160,256]{2,1,0:T(8,128)(2,1)}, u32[]{:S(2)}, u32[]{:S(2)}) async-start(bf16[8,160,256]{2,1,0:T(8,128)(2,1)} %get-tuple-element.32), calls=%async_computation.1 | async-start | bytes 1310720 | tf_op jit(solution)/shard_map/all_to_all | solution.py:672
  76.0 0.0 copy-start.4
  76.0 5.9 %refine.1.first_ref = f32[1024,256]{1,0:T(8,128)S(1)} custom-call(s16[32,264,128]{2,1,0:T(8,128)(2,1)S(1)} %all-to-all-done.got_ref, f32[1024,256]{1,0:T(8,128)S(1)} %get-tuple-element.33.dual_ref, bf16[2,512,512]{2,1,0:T(8,128)(2,1)} %gram_ref.2), custom_call_target="tpu_custom_call" | custom-call | flops 2147483648 | bytes 4194304 | tf_op jit(solution)/shard_map/refine/pallas_call | solution.py:351
  81.9 0.0 copy-done.4
  81.9 6.3 %near_field.1.image_ref = f32[1024,256]{1,0:T(8,128)S(1)} custom-call(s32[2,8]{1,0:T(2,128)S(1)} %copy-done.4, bf16[2,8,512,512]{3,2,1,0:T(8,128)(2,1)} %block_ref.2, f32[1024,256]{1,0:T(8,128)S(1)} %refine.1.first_ref), custom_call_target="tpu_custom_call" | custom-call | flops 2147483648 | bytes 8388608 | tf_op jit(solution)/shard_map/near_field/pallas_call | solution.py:454
  88.3 0.0 copy-start.3
  88.3 2.3 %prepare.1 = (f32[1024,256]{1,0:T(8,128)S(1)}, bf16[1024,128]{1,0:T(8,128)(2,1)S(1)}) custom-call(f32[1024,256]{1,0:T(8,128)S(1)} %near_field.1.image_ref, bf16[2,64,512]{2,1,0:T(8,128)(2,1)} %base_ref.2, bf16[2,512,512]{2,1,0:T(8,128)(2,1)} %gram_ref.2), custom_call_target="tpu_custom_call" | custom-call | flops 536870912 | bytes 4194304 | tf_op jit(solution)/shard_map/prepare/pallas_call | solution.py:490
  90.6 2.4 %all-to-all-done.1.coeff_ref = bf16[8,160,256]{2,1,0:T(8,128)(2,1)} async-done(((bf16[8,160,256]{2,1,0:T(8,128)(2,1)}), bf16[8,160,256]{2,1,0:T(8,128)(2,1)}, u32[]{:S(2)}, u32[]{:S(2)}) %all-to-all-start.1) | async-done | bytes 655392 | tf_op jit(solution)/shard_map/all_to_all | solution.py:672
  93.1 1.4 parent_of.1.refs_6_
  94.5 0.0 collective-permute-start
  94.5 1.8 collective-permute-start.1
  96.3 0.1 collective-permute-start.2
  96.4 0.0 copy-done.3
  96.4 2.2 %far_field.1.refs_2_ = f32[2,64,256]{2,1,0:T(8,128)S(1)} custom-call(s32[2,16]{1,0:T(2,128)S(1)} %copy-done.3, bf16[8,160,256]{2,1,0:T(8,128)(2,1)} %all-to-all-done.1.coeff_ref, bf16[2,16,64,64]{3,2,1,0:T(8,128)(2,1)} %block_ref.3), custom_call_target="tpu_custom_call" | custom-call | flops 67108864 | bytes 1048576 | tf_op jit(solution)/shard_map/far_field/pallas_call | solution.py:412
  98.6 0.0 collective-permute-done.refs_7_
  98.6 0.0 collective-permute-done.1.refs_8_
  98.6 1.0 collective-permute-done.2.refs_9_
  99.6 4.7 %reply.1 = bf16[4096,256]{1,0:T(8,128)(2,1)} custom-call(f32[1024,256]{1,0:T(8,128)S(1)} %get-tuple-element.36.refs_0_, bf16[1024,128]{1,0:T(8,128)(2,1)S(1)} %get-tuple-element.37.refs_1_, f32[2,64,256]{2,1,0:T(8,128)S(1)} %far_field.1.refs_2_, bf16[4,64,64]{2,1,0:T(8,128)(2,1)} %gather_fusion, bf16[2,64,64]{2,1,0:T(8,128)(2,1)} %refs_4_.1, ...), custom_call_target="tpu_custom_call" | custom-call | flops 2147483648 | bytes 4194304 | tf_op jit(solution)/shard_map/reply/pallas_call | solution.py:542
  104.3 0.0 copy-start
  104.3 3.8 %all-to-all-start.2 = ((bf16[32,128,256]{2,1,0:T(8,128)(2,1)}), bf16[32,128,256]{2,1,0:T(8,128)(2,1)}, u32[]{:S(2)}, u32[]{:S(2)}) async-start(bf16[32,128,256]{2,1,0:T(8,128)(2,1)} %bitcast.18), calls=%async_computation.2 | async-start | bytes 4194304 | tf_op jit(solution)/shard_map/all_to_all | solution.py:672
  108.2 0.0 copy-done
  108.2 0.0 copy-start.6
  108.2 0.2 multiply_reduce_fusion.2
  108.5 0.1 collective-permute-start.3
  108.6 1.5 collective-permute-start.4
  110.0 0.4 collective-permute-start.5
  110.4 0.0 copy-done.6
  110.4 1.0 copy.21
  111.4 0.0 collective-permute-done.3
  111.4 2.7 %collective-permute-done.4 = f32[3,256]{1,0:T(4,128)S(1)} collective-permute-done((f32[3,256]{1,0:T(4,128)S(1)}, f32[3,256]{1,0:T(4,128)S(1)}, u32[]{:S(2)}, u32[]{:S(2)}) %collective-permute-start.4) | collective-permute-done | bytes 3104 | tf_op jit(solution)/shard_map/ppermute | solution.py:678
  114.1 0.0 collective-permute-done.5
  114.1 42.5 %all-to-all-done.2 = bf16[32,128,256]{2,1,0:T(8,128)(2,1)} async-done(((bf16[32,128,256]{2,1,0:T(8,128)(2,1)}), bf16[32,128,256]{2,1,0:T(8,128)(2,1)}, u32[]{:S(2)}, u32[]{:S(2)}) %all-to-all-start.2) | async-done | bytes 2097184 | tf_op jit(solution)/shard_map/all_to_all | solution.py:672
  156.6 6.5 %gather_back.1 = (f32[1024,256]{1,0:T(8,128)S(1)}, f32[4,256]{1,0:T(4,128)S(1)}) custom-call(bf16[4096,256]{1,0:T(8,128)(2,1)} %bitcast.8.ret_ref, f32[1024,8]{1,0:T(8,128)} %bitcast.19, f32[2,1024,256]{2,1,0:T(8,128)S(1)} %copy-done, f32[1,256]{1,0:T(1,128)S(1)} %pad_dynamic-slice_fusion.mutual_ref), custom_call_target="tpu_custom_call" | custom-call | flops 4294967296 | bytes 6291456 | tf_op jit(solution)/shard_map/gather_back/pallas_call | solution.py:598
  163.1 12.0 %all_to_all.20.sums_ref = f32[32,4,256]{2,1,0:T(4,128)S(1)} all-to-all(f32[32,4,256]{2,1,0:T(4,128)S(1)} %broadcast_in_dim.2), channel_id=1, replica_groups=mesh['branch'=8,'group'=4] {'branch','group'}, dimensions={0} | all-to-all | bytes 262144 | tf_op jit(solution)/shard_map/all_to_all | solution.py:672
  175.1 1.7 finish.1
  (8 shorter events, 0.1 us)
Async XLA Ops:
  9.0 7.4 %copy-start.5 = (bf16[64,256]{1,0:T(8,128)(2,1)S(1)}, bf16[64,256]{1,0:T(8,128)(2,1)}, u32[]{:S(2)}) copy-start(bf16[64,256]{1,0:T(8,128)(2,1)} %param.25) | copy-start | bytes 98308
  9.0 7.5 %copy-start.7 = (bf16[2,64,64]{2,1,0:T(8,128)(2,1)S(1)}, bf16[2,64,64]{2,1,0:T(8,128)(2,1)}, u32[]{:S(2)}) copy-start(bf16[2,64,64]{2,1,0:T(8,128)(2,1)} %param.23) | copy-start | bytes 49156
  9.0 8.9 %copy-start.1 = (bf16[2,512,512]{2,1,0:T(8,128)(2,1)S(1)}, bf16[2,512,512]{2,1,0:T(8,128)(2,1)}, u32[]{:S(2)}) copy-start(bf16[2,512,512]{2,1,0:T(8,128)(2,1)} %gram_ref.2) | copy-start | bytes 3145732
  9.0 8.9 %copy-start.2 = (bf16[2,64,512]{2,1,0:T(8,128)(2,1)S(1)}, bf16[2,64,512]{2,1,0:T(8,128)(2,1)}, u32[]{:S(2)}) copy-start(bf16[2,64,512]{2,1,0:T(8,128)(2,1)} %base_ref.2) | copy-start | bytes 393220
  9.0 57.5 %all-to-all-start = ((s16[32,264,128]{2,1,0:T(8,128)(2,1)}), s16[32,264,128]{2,1,0:T(8,128)(2,1)S(1)}, u32[]{:S(2)}, u32[]{:S(2)}) async-start(s16[32,264,128]{2,1,0:T(8,128)(2,1)} %get-tuple-element.24), calls=%async_computation | async-start | bytes 4325376 | tf_op jit(solution)/shard_map/all_to_all | solution.py:672
  71.6 21.5 %all-to-all-start.1 = ((bf16[8,160,256]{2,1,0:T(8,128)(2,1)}), bf16[8,160,256]{2,1,0:T(8,128)(2,1)}, u32[]{:S(2)}, u32[]{:S(2)}) async-start(bf16[8,160,256]{2,1,0:T(8,128)(2,1)} %get-tuple-element.32), calls=%async_computation.1 | async-start | bytes 1310720 | tf_op jit(solution)/shard_map/all_to_all | solution.py:672
  76.0 6.0 %copy-start.4 = (s32[2,8]{1,0:T(2,128)S(1)}, s32[2,8]{1,0:T(2,128)}, u32[]{:S(2)}) copy-start(s32[2,8]{1,0:T(2,128)} %list_ref.2) | copy-start | bytes 196
  88.3 8.1 %copy-start.3 = (s32[2,16]{1,0:T(2,128)S(1)}, s32[2,16]{1,0:T(2,128)}, u32[]{:S(2)}) copy-start(s32[2,16]{1,0:T(2,128)} %list_ref.3) | copy-start | bytes 388
  94.5 4.1 %collective-permute-start = (bf16[64,256]{1,0:T(8,128)(2,1)S(1)}, bf16[64,256]{1,0:T(8,128)(2,1)S(1)}, u32[]{:S(2)}, u32[]{:S(2)}) collective-permute-start(bf16[64,256]{1,0:T(8,128)(2,1)S(1)} %parent_of.1.refs_6_), channel_id=1, source_target_pairs={{0,1},{1,0},{2,3},{3,2},{4,5},{5,4},{6,7},{7,6},{8,9},{9,8},{10,11... | collective-permute-start | bytes 98312 | tf_op jit(solution)/shard_map/ppermute | solution.py:678
  94.5 4.1 %collective-permute-start.1 = (bf16[64,256]{1,0:T(8,128)(2,1)S(1)}, bf16[64,256]{1,0:T(8,128)(2,1)S(1)}, u32[]{:S(2)}, u32[]{:S(2)}) collective-permute-start(bf16[64,256]{1,0:T(8,128)(2,1)S(1)} %parent_of.1.refs_6_), channel_id=1, source_target_pairs={{0,2},{1,3},{2,0},{3,1},{4,6},{5,7},{6,4},{7,5},{8,10},{9,11},{10,... | collective-permute-start | bytes 98312 | tf_op jit(solution)/shard_map/ppermute | solution.py:678
  96.3 3.4 %collective-permute-start.2 = (bf16[64,256]{1,0:T(8,128)(2,1)S(1)}, bf16[64,256]{1,0:T(8,128)(2,1)S(1)}, u32[]{:S(2)}, u32[]{:S(2)}) collective-permute-start(bf16[64,256]{1,0:T(8,128)(2,1)S(1)} %parent_of.1.refs_6_), channel_id=1, source_target_pairs={{0,3},{1,2},{2,1},{3,0},{4,7},{5,6},{6,5},{7,4},{8,11},{9,10},{10,... | collective-permute-start | bytes 98312 | tf_op jit(solution)/shard_map/ppermute | solution.py:678
  104.3 3.9 %copy-start = (f32[2,1024,256]{2,1,0:T(8,128)S(1)}, f32[2,1024,256]{2,1,0:T(8,128)}, u32[]{:S(2)}) copy-start(f32[2,1024,256]{2,1,0:T(8,128)} %basis_ref.3) | copy-start | bytes 6291460
  104.3 52.3 %all-to-all-start.2 = ((bf16[32,128,256]{2,1,0:T(8,128)(2,1)}), bf16[32,128,256]{2,1,0:T(8,128)(2,1)}, u32[]{:S(2)}, u32[]{:S(2)}) async-start(bf16[32,128,256]{2,1,0:T(8,128)(2,1)} %bitcast.18), calls=%async_computation.2 | async-start | bytes 4194304 | tf_op jit(solution)/shard_map/all_to_all | solution.py:672
  108.2 2.2 %copy-start.6 = (f32[8,1024]{1,0:T(8,128)S(1)}, f32[8,1024]{1,0:T(8,128)}, u32[]{:S(2)}) copy-start(f32[8,1024]{1,0:T(8,128)} %get-tuple-element.41) | copy-start | bytes 98308
  108.5 2.9 %collective-permute-start.3 = (f32[3,256]{1,0:T(4,128)S(1)}, f32[3,256]{1,0:T(4,128)S(1)}, u32[]{:S(2)}, u32[]{:S(2)}) collective-permute-start(f32[3,256]{1,0:T(4,128)S(1)} %pad_maximum_fusion), channel_id=1, source_target_pairs={{0,1},{1,0},{2,3},{3,2},{4,5},{5,4},{6,7},{7,6},{8,9},{9,8},{10,11... | collective-permute-start | bytes 9224 | tf_op jit(solution)/shard_map/ppermute | solution.py:678
  108.6 5.5 %collective-permute-start.4 = (f32[3,256]{1,0:T(4,128)S(1)}, f32[3,256]{1,0:T(4,128)S(1)}, u32[]{:S(2)}, u32[]{:S(2)}) collective-permute-start(f32[3,256]{1,0:T(4,128)S(1)} %pad_maximum_fusion), channel_id=1, source_target_pairs={{0,2},{1,3},{2,0},{3,1},{4,6},{5,7},{6,4},{7,5},{8,10},{9,11},{10,... | collective-permute-start | bytes 9224 | tf_op jit(solution)/shard_map/ppermute | solution.py:678
  110.0 4.0 %collective-permute-start.5 = (f32[3,256]{1,0:T(4,128)S(1)}, f32[3,256]{1,0:T(4,128)S(1)}, u32[]{:S(2)}, u32[]{:S(2)}) collective-permute-start(f32[3,256]{1,0:T(4,128)S(1)} %pad_maximum_fusion), channel_id=1, source_target_pairs={{0,3},{1,2},{2,1},{3,0},{4,7},{5,6},{6,5},{7,4},{8,11},{9,10},{10,... | collective-permute-start | bytes 9224 | tf_op jit(solution)/shard_map/ppermute | solution.py:678
